TPU v7x, 768 devices: a whole 4x8x12 slice. The times are simulated.
768 devices in a mesh: tile: 96 (over z, y), mode: 8 (over x, core).
Axes of the slice: x: 4, y: 8, z: 12, core: 2. Of those that a mesh axis runs over, the one named last changes fastest.
Arguments:
- intensity: float32 [192, 256, 256], P('tile'), may hold values from 0.05 to 4
- positions: int32 [192, 2], replicated, may hold values from 0 to 24575, as said below
- object_field: float32 [2, 320, 24576], P(None, None, 'tile'), may hold values from -4 to 4
- probe_modes: float32 [8, 2, 256, 256], P('mode'), may hold values from -1.5 to 1.5
- kernel_taps: float32 [2, 129], replicated, may hold values from -0.375 to 0.375
Outputs:
- new_object: float32 [2, 320, 24576], P(None, None, 'tile')
Inputs may be any that keep to these rules, and one draw needn't show every extreme that they name: `positions`: pattern g belongs to scan block b = g // 2; its centre column lies in tile b - 1, b or b + 1, tile t holding columns t * 256 to (t + 1) * 256 - 1. From one block at most 1 patterns lie in each neighbouring tile; in every draw some block has 1 in its right neighbour and some block 1 in its left neighbour, and some tile keeps all 2 of its own block and gets 1 from each neighbouring block. Within its tile, the centre column of an even-numbered pattern of a block lies in the last 64 columns, that of an odd-numbered one in the first 64 columns. Rows lie in 0 to 64.
All inputs are finite; a program needn't handle non-finite values.
Results may differ from a plain program's by a relative error of at most 0.0023.
Values sent between devices are 32-bit elements; how exact they have to be, the bound alone decides.
No kernel may reach another device: no remote copies, remote signals or barrier semaphores. Data moves between devices by JAX's collectives and lax.ppermute only.
A program may use at most 32 MiB of HBM per device.

v0:
```python
import jax
import jax.numpy as jnp
from jax import lax
from jax.sharding import PartitionSpec as P

P_SIZE = 256
BAND = 64
CAP = 1
SCAN = 2
TW = 256
HALF = 128


def with_halo(block, sides, width):
    for axis, dim in sides:
        count = lax.axis_size(axis)
        forward = [(i, i + 1) for i in range(count - 1)]
        backward = [(target, source) for source, target in forward]
        low = lax.ppermute(
            lax.slice_in_dim(block, block.shape[dim] - width, None, axis=dim), axis, forward
        )
        high = lax.ppermute(lax.slice_in_dim(block, 0, width, axis=dim), axis, backward)
        block = jnp.concatenate([low, block, high], axis=dim)
    return block


def band_matrix(taps_row):
    leading = jnp.zeros((P_SIZE - 1 - BAND,), jnp.float32)
    trailing = jnp.zeros((P_SIZE - BAND,), jnp.float32)
    vector = jnp.concatenate([leading, taps_row, trailing])
    tiled = jnp.tile(vector, P_SIZE)[: P_SIZE * (2 * P_SIZE - 1)].reshape(P_SIZE, 2 * P_SIZE - 1)
    return tiled[:, P_SIZE - 1 :]


def product(form, left_op, right_op):
    return jnp.einsum(form, left_op, right_op, preferred_element_type=jnp.float32)


def forward_pass(wave_re, wave_im, band_re, band_im):
    mid_re = (
        product("ab,wbc->wac", band_re, wave_re) - product("ab,wbc->wac", band_im, wave_im)
    ).astype(jnp.bfloat16)
    mid_im = (
        product("ab,wbc->wac", band_re, wave_im) + product("ab,wbc->wac", band_im, wave_re)
    ).astype(jnp.bfloat16)
    far_re = product("wab,cb->wac", mid_re, band_re) - product("wab,cb->wac", mid_im, band_im)
    far_im = product("wab,cb->wac", mid_re, band_im) + product("wab,cb->wac", mid_im, band_re)
    return (far_re, far_im)


def backward_pass(near_re, near_im, band_re, band_im):
    mid_re = (
        product("ba,wbc->wac", band_re, near_re) + product("ba,wbc->wac", band_im, near_im)
    ).astype(jnp.bfloat16)
    mid_im = (
        product("ba,wbc->wac", band_re, near_im) - product("ba,wbc->wac", band_im, near_re)
    ).astype(jnp.bfloat16)
    back_re = product("wab,bc->wac", mid_re, band_re) + product("wab,bc->wac", mid_im, band_im)
    back_im = product("wab,bc->wac", mid_im, band_re) - product("wab,bc->wac", mid_re, band_im)
    return (back_re, back_im)


def route_lists(positions, block_index, tiles):
    first_row = jnp.clip(block_index, 0, tiles - 1) * SCAN
    columns = lax.dynamic_slice_in_dim(positions[:, 1], first_row, SCAN, 0)
    offset = columns // TW - block_index
    inside = (block_index >= 0) & (block_index < tiles)
    counter = jnp.arange(SCAN, dtype=jnp.int32)
    slot_number = jnp.arange(CAP, dtype=jnp.int32)
    outcome = []
    for target in (-1, 1):
        going = (offset == target) & inside
        ranking = jnp.cumsum(going.astype(jnp.int32)) - 1
        matches = going[None, :] & (ranking[None, :] == slot_number[:, None])
        chosen = first_row + jnp.sum(jnp.where(matches, counter[None, :], 0), axis=1)
        outcome.append((chosen, jnp.any(matches, axis=1)))
    staying = (offset == 0) & inside
    return (outcome[0], outcome[1], staying, first_row)


def fold_rims(wide):
    width = wide.shape[2] - 2 * P_SIZE
    middle = wide[:, :, P_SIZE : P_SIZE + width]
    middle = middle.at[:, :, :HALF].add(wide[:, :, :HALF])
    middle = middle.at[:, :, width - HALF :].add(wide[:, :, wide.shape[2] - HALF :])
    return middle


def local(intensity, positions, object_field, probe_modes, kernel_taps):
    tiles = lax.axis_size("tile")
    here = lax.axis_index("tile")
    to_left, to_right, staying, first_row = route_lists(positions, here, tiles)

    def pick(entry):
        chosen, usable_rows = entry
        taken = jnp.take(intensity, chosen - first_row, axis=0)
        return jnp.where(usable_rows[:, None, None], taken, 0.0)

    outgoing = jnp.concatenate([pick(to_left), pick(to_right)], axis=0)
    arrived = with_halo(outgoing, (("tile", 0),), CAP)
    from_lower = route_lists(positions, here - 1, tiles)[1]
    from_upper = route_lists(positions, here + 1, tiles)[0]
    measured = jnp.concatenate(
        [arrived[:CAP], jnp.where(staying[:, None, None], intensity, 0.0), arrived[3 * CAP :]],
        axis=0,
    )
    slot_ids = jnp.concatenate(
        [from_lower[0], first_row + jnp.arange(SCAN, dtype=jnp.int32), from_upper[0]]
    )
    usable = jnp.concatenate([from_lower[1], staying, from_upper[1]]).astype(jnp.float32)
    placed = jnp.take(positions, slot_ids, axis=0)
    top_rows = placed[:, 0]
    left_cols = placed[:, 1] - here * TW
    extended = with_halo(object_field, (("tile", 2),), HALF)
    anchor = jnp.zeros((), jnp.int32)

    def window_at(top_row, left_col):
        return lax.dynamic_slice(extended, (anchor, top_row, left_col), (2, P_SIZE, P_SIZE))

    patches = jax.vmap(window_at)(top_rows, left_cols)
    probe_re = probe_modes[0, 0]
    probe_im = probe_modes[0, 1]
    exit_re = probe_re * patches[:, 0] - probe_im * patches[:, 1]
    exit_im = probe_re * patches[:, 1] + probe_im * patches[:, 0]
    band_re = band_matrix(kernel_taps[0]).astype(jnp.bfloat16)
    band_im = band_matrix(kernel_taps[1]).astype(jnp.bfloat16)
    far_re, far_im = forward_pass(
        exit_re.astype(jnp.bfloat16), exit_im.astype(jnp.bfloat16), band_re, band_im
    )
    power = far_re * far_re + far_im * far_im
    total_power = lax.psum(power, "mode")
    ratio = jnp.sqrt(measured) / jnp.sqrt(total_power + 1.0)
    near_re = (far_re * ratio).astype(jnp.bfloat16)
    near_im = (far_im * ratio).astype(jnp.bfloat16)
    back_re, back_im = backward_pass(near_re, near_im, band_re, band_im)
    diff_re = back_re - exit_re
    diff_im = back_im - exit_im
    weight = usable[:, None, None]
    pieces = jnp.stack(
        [
            (probe_re * diff_re + probe_im * diff_im) * weight,
            (probe_re * diff_im - probe_im * diff_re) * weight,
            (probe_re * probe_re + probe_im * probe_im) * weight,
        ],
        axis=1,
    )

    def deposit(index, total):
        top_row = top_rows[index]
        left_col = left_cols[index]
        current = lax.dynamic_slice(total, (anchor, top_row, left_col), (3, P_SIZE, P_SIZE))
        return lax.dynamic_update_slice(total, current + pieces[index], (anchor, top_row, left_col))

    start_total = jnp.zeros((3, extended.shape[1], extended.shape[2]), jnp.float32)
    accumulated = lax.fori_loop(0, pieces.shape[0], deposit, start_total)
    wide = with_halo(accumulated, (("tile", 2),), HALF)
    summed = lax.psum(fold_rims(wide), "mode")
    return object_field + summed[:2] / (summed[2] + 0.5)


def solution(mesh):
    return jax.shard_map(
        local,
        mesh=mesh,
        in_specs=(
            P("tile", None, None),
            P(),
            P(None, None, "tile"),
            P("mode", None, None, None),
            P(),
        ),
        out_specs=P(None, None, "tile"),
        check_vma=False,
    )
```

profile of v0, /device:TPU:1, one launch (start us, length us, event | category | flops | bytes accessed | tf_op | source)
XLA Modules:
  0.0 330.6 jit_solution(2896551848627885678)
XLA Ops:
  6.5 2.0 fusion.43
  8.6 4.0 %collective-permute-start = (f32[2,320,128]{2,1,0:T(8,128)}, f32[2,320,128]{2,1,0:T(8,128)S(1)}, u32[]{:S(2)}, u32[]{:S(2)}) collective-permute-start(f32[2,320,128]{2,1,0:T(8,128)} %get-tuple-element.200), channel_id=1, source_target_pairs={{0,8},{8,16},{16,24},{24,32},{32,40},{40,48},{48,56},{56,64},{64,7... | collective-permute-start | bytes 983048 | tf_op jit(solution)/shard_map/ppermute | solution.py:19
  21.4 3.2 select_select_fusion.1
  24.6 4.8 %collective-permute-start.2 = (f32[1,256,256]{2,1,0:T(8,128)}, f32[1,256,256]{2,1,0:T(8,128)}, u32[]{:S(2)}, u32[]{:S(2)}) collective-permute-start(f32[1,256,256]{2,1,0:T(8,128)} %get-tuple-element.202), channel_id=1, source_target_pairs={{0,8},{8,16},{16,24},{24,32},{32,40},{40,48},{48,56},{56,64},{64,7... | collective-permute-start | bytes 786440 | tf_op jit(solution)/shard_map/ppermute | solution.py:19
  37.6 11.5 %while.18 = (s32[]{:T(128)}, f32[2,320,512]{2,1,0:T(8,128)S(1)}, s32[4,3]{1,0:T(4,128)S(1)}, f32[4,2,256,256]{3,2,0,1:T(8,128)}, s32[]{:T(128)}) while((s32[]{:T(128)}, f32[2,320,512]{2,1,0:T(8,128)S(1)}, s32[4,3]{1,0:T(4,128)S(1)}, f32[4,2,256,256]{3,2,0,1:T(8,128)}, s32[]{:T(128)}) %tuple.87), condition=%wide.while_cond.3, body=%wide.while_body.3.sunk | while | flops 2 | bytes 1050217 | solution.py:118
  38.2 2.2 bitcast_dynamic-update-slice_fusion.2
  41.1 2.2 bitcast_dynamic-update-slice_fusion.2
  43.9 2.2 bitcast_dynamic-update-slice_fusion.2
  46.8 2.2 bitcast_dynamic-update-slice_fusion.2
  49.0 1.8 fusion.12
  53.3 1.3 convolution_subtract_fusion.2
  54.7 1.8 multiply_add_fusion
  56.5 1.8 multiply_add_fusion.1
  58.3 1.3 add_convert_fusion
  59.6 2.1 broadcast_multiply_fusion
  61.7 83.0 %all-reduce.3.cloned.1.call-done = f32[4,256,256]{2,1,0:T(8,128)} async-done(((f32[4,256,256]{2,1,0:T(8,128)}), f32[4,256,256]{2,1,0:T(8,128)}) %all-reduce.3.cloned.1.call-update) | async-done | bytes 1048592 | tf_op jit(solution)/shard_map/psum | solution.py:131
  144.7 2.3 multiply_convert_fusion
  151.8 2.1 pad_maximum_fusion
  154.1 62.1 %while.17 = (s32[]{:T(128)}, f32[3,320,512]{2,1,0:T(8,128)S(1)}, s32[4]{0:T(128)S(1)}, s32[4]{0:T(128)S(1)}, f32[4,3,256,256]{3,2,0,1:T(8,128)}, /*index=5*/s32[]{:T(128)}, s32[]{:T(128)}, s32[]{:T(128)}, s32[]{:T(128)}) while((s32[]{:T(128)}, f32[3,320,512]{2,1,0:T(8,128)S(1)}, s32[4]{0:T(128)S(1)}, s32[4]{0:T(128)S(1)}, ...), condition=%wide.region_14.16_spmd, body=%wide.region_13.15_spmd.sunk | while | flops 196616 | bytes 3932361 | solution.py:155
  159.2 1.4 bitcast_add_fusion.2
  160.6 11.0 %dynamic_update_slice.8 = f32[3,320,512]{2,1,0:T(8,128)S(1)} dynamic-update-slice(f32[3,320,512]{2,1,0:T(8,128)S(1)} %get-tuple-element.311, f32[3,256,256]{2,1,0:T(8,128)S(1)} %bitcast_add_fusion.2, s32[]{:T(128)} %constant.173.clone.1..sunk, s32[]{:T(128)S(6)} %select_n.274, s32[]{:T(128)S(6)} %select_n.275) | dynamic-update-slice | bytes 1572868 | tf_op jit(solution)/shard_map/while/body/eval_jaxpr/dynamic_update_slice | solution.py:152
  176.8 1.4 bitcast_add_fusion.2
  178.2 11.0 %dynamic_update_slice.8 = f32[3,320,512]{2,1,0:T(8,128)S(1)} dynamic-update-slice(f32[3,320,512]{2,1,0:T(8,128)S(1)} %get-tuple-element.311, f32[3,256,256]{2,1,0:T(8,128)S(1)} %bitcast_add_fusion.2, s32[]{:T(128)} %constant.173.clone.1..sunk, s32[]{:T(128)S(6)} %select_n.274, s32[]{:T(128)S(6)} %select_n.275) | dynamic-update-slice | bytes 1572868 | tf_op jit(solution)/shard_map/while/body/eval_jaxpr/dynamic_update_slice | solution.py:152
  194.3 1.4 bitcast_add_fusion.2
  195.8 6.9 %dynamic_update_slice.8 = f32[3,320,512]{2,1,0:T(8,128)S(1)} dynamic-update-slice(f32[3,320,512]{2,1,0:T(8,128)S(1)} %get-tuple-element.311, f32[3,256,256]{2,1,0:T(8,128)S(1)} %bitcast_add_fusion.2, s32[]{:T(128)} %constant.173.clone.1..sunk, s32[]{:T(128)S(6)} %select_n.274, s32[]{:T(128)S(6)} %select_n.275) | dynamic-update-slice | bytes 1572868 | tf_op jit(solution)/shard_map/while/body/eval_jaxpr/dynamic_update_slice | solution.py:152
  207.7 1.4 bitcast_add_fusion.2
  209.2 7.1 %dynamic_update_slice.8 = f32[3,320,512]{2,1,0:T(8,128)S(1)} dynamic-update-slice(f32[3,320,512]{2,1,0:T(8,128)S(1)} %get-tuple-element.311, f32[3,256,256]{2,1,0:T(8,128)S(1)} %bitcast_add_fusion.2, s32[]{:T(128)} %constant.173.clone.1..sunk, s32[]{:T(128)S(6)} %select_n.274, s32[]{:T(128)S(6)} %select_n.275) | dynamic-update-slice | bytes 1572868 | tf_op jit(solution)/shard_map/while/body/eval_jaxpr/dynamic_update_slice | solution.py:152
  216.3 11.0 %collective-permute-start.4 = (f32[3,320,128]{2,1,0:T(8,128)S(1)}, f32[3,320,128]{2,1,0:T(8,128)S(1)}, u32[]{:S(2)}, u32[]{:S(2)}) collective-permute-start(f32[3,320,128]{2,1,0:T(8,128)S(1)} %get-tuple-element.199), channel_id=1, source_target_pairs={{0,8},{8,16},{16,24},{24,32},{32,40},{40,48},{48,56},{56,64},{64,7... | collective-permute-start | bytes 1474568 | tf_op jit(solution)/shard_map/ppermute | solution.py:19
  228.8 6.4 %collective-permute-done.4 = f32[3,320,128]{2,1,0:T(8,128)S(1)} collective-permute-done((f32[3,320,128]{2,1,0:T(8,128)S(1)}, f32[3,320,128]{2,1,0:T(8,128)S(1)}, u32[]{:S(2)}, u32[]{:S(2)}) %collective-permute-start.4) | collective-permute-done | bytes 491552 | tf_op jit(solution)/shard_map/ppermute | solution.py:19
  235.3 3.8 %collective-permute-done.5 = f32[3,320,128]{2,1,0:T(8,128)S(1)} collective-permute-done((f32[3,320,128]{2,1,0:T(8,128)S(1)}, f32[3,320,128]{2,1,0:T(8,128)S(1)}, u32[]{:S(2)}, u32[]{:S(2)}) %collective-permute-start.5) | collective-permute-done | bytes 491552 | tf_op jit(solution)/shard_map/ppermute | solution.py:22
  240.2 80.4 %all-reduce.5.cloned.1.call-done = f32[3,320,256]{2,1,0:T(8,128)} async-done(((f32[3,320,256]{2,1,0:T(8,128)}), f32[3,320,256]{2,1,0:T(8,128)}) %all-reduce.5.cloned.1.call-update) | async-done | bytes 983056 | tf_op jit(solution)/shard_map/psum | solution.py:157
  321.5 2.2 fusion.13
  (111 shorter events, 30.2 us)
Async XLA Ops:
  6.5 24.2 %copy-start.11 = (s32[192,2]{0,1:T(2,128)S(1)}, s32[192,2]{0,1:T(2,128)}, u32[]{:S(2)}) copy-start(s32[192,2]{0,1:T(2,128)} %param.14) | copy-start | bytes 4612
  6.5 26.5 %copy-start.10 = (f32[1,2,256,256]{3,2,1,0:T(8,128)S(1)}, f32[1,2,256,256]{3,2,1,0:T(8,128)}, u32[]{:S(2)}) copy-start(f32[1,2,256,256]{3,2,1,0:T(8,128)} %param.16) | copy-start | bytes 1572868
  6.5 26.6 %copy-start.12 = (f32[2,129]{1,0:T(2,128)S(1)}, f32[2,129]{1,0:T(2,128)}, u32[]{:S(2)}) copy-start(f32[2,129]{1,0:T(2,128)} %param.17) | copy-start | bytes 3100
  6.5 138.2 %all-reduce.3.cloned.1.call-start = ((), (), s32[]{:S(2)}) async-start(), calls=%async_computation | async-start | bytes 2097152 | tf_op jit(solution)/shard_map/psum | solution.py:131
  8.6 27.9 %collective-permute-start = (f32[2,320,128]{2,1,0:T(8,128)}, f32[2,320,128]{2,1,0:T(8,128)S(1)}, u32[]{:S(2)}, u32[]{:S(2)}) collective-permute-start(f32[2,320,128]{2,1,0:T(8,128)} %get-tuple-element.200), channel_id=1, source_target_pairs={{0,8},{8,16},{16,24},{24,32},{32,40},{40,48},{48,56},{56,64},{64,7... | collective-permute-start | bytes 983048 | tf_op jit(solution)/shard_map/ppermute | solution.py:19
  12.6 23.9 %collective-permute-start.1 = (f32[2,320,128]{2,1,0:T(8,128)}, f32[2,320,128]{2,1,0:T(8,128)}, u32[]{:S(2)}, u32[]{:S(2)}) collective-permute-start(f32[2,320,128]{2,1,0:T(8,128)} %get-tuple-element.201), channel_id=1, source_target_pairs={{8,0},{16,8},{24,16},{32,24},{40,32},{48,40},{56,48},{64,56},{72,6... | collective-permute-start | bytes 983048 | tf_op jit(solution)/shard_map/ppermute | solution.py:22
  24.6 10.9 %copy-start.9 = (f32[2,256,256]{2,1,0:T(8,128)S(1)}, f32[2,256,256]{2,1,0:T(8,128)}, u32[]{:S(2)}) copy-start(f32[2,256,256]{2,1,0:T(8,128)} %param.13) | copy-start | bytes 1572868
  24.6 37.1 %collective-permute-start.2 = (f32[1,256,256]{2,1,0:T(8,128)}, f32[1,256,256]{2,1,0:T(8,128)}, u32[]{:S(2)}, u32[]{:S(2)}) collective-permute-start(f32[1,256,256]{2,1,0:T(8,128)} %get-tuple-element.202), channel_id=1, source_target_pairs={{0,8},{8,16},{16,24},{24,32},{32,40},{40,48},{48,56},{56,64},{64,7... | collective-permute-start | bytes 786440 | tf_op jit(solution)/shard_map/ppermute | solution.py:19
  29.5 32.2 %collective-permute-start.3 = (f32[1,256,256]{2,1,0:T(8,128)}, f32[1,256,256]{2,1,0:T(8,128)}, u32[]{:S(2)}, u32[]{:S(2)}) collective-permute-start(f32[1,256,256]{2,1,0:T(8,128)} %get-tuple-element.203), channel_id=1, source_target_pairs={{8,0},{16,8},{24,16},{32,24},{40,32},{48,40},{56,48},{64,56},{72,6... | collective-permute-start | bytes 786440 | tf_op jit(solution)/shard_map/ppermute | solution.py:22
  33.1 15.9 %copy-start.5 = (f32[256,256]{1,0:T(8,128)}, f32[256,256]{1,0:T(8,128)S(1)}, u32[]{:S(2)}) copy-start(f32[256,256]{1,0:T(8,128)S(1)} %get-tuple-element.204) | copy-start | bytes 786436
  33.1 15.9 %copy-start.7 = (f32[256,256]{1,0:T(8,128)}, f32[256,256]{1,0:T(8,128)S(1)}, u32[]{:S(2)}) copy-start(f32[256,256]{1,0:T(8,128)S(1)} %get-tuple-element.205) | copy-start | bytes 786436
  33.1 3.3 %copy-start.3 = (f32[2,320,256]{2,1,0:T(8,128)S(1)}, f32[2,320,256]{2,1,0:T(8,128)}, u32[]{:S(2)}) copy-start(f32[2,320,256]{2,1,0:T(8,128)} %param.15) | copy-start | bytes 1966084
  34.5 18.4 %copy-start = (bf16[256,511]{1,0:T(8,128)(2,1)}, bf16[256,511]{1,0:T(8,128)(2,1)S(1)}, u32[]{:S(2)}) copy-start(bf16[256,511]{1,0:T(8,128)(2,1)S(1)} %reshape.748) | copy-start | bytes 784900
  56.5 264.1 %all-reduce.5.cloned.1.call-start = ((), (), s32[]{:S(2)}) async-start(), calls=%async_computation.1 | async-start | bytes 1966080 | tf_op jit(solution)/shard_map/psum | solution.py:157
  147.0 1.0 copy-start.1
  149.6 1.0 copy-start.6
  149.6 1.0 copy-start.8
  150.6 1.2 copy-start.4
  216.3 18.8 %collective-permute-start.4 = (f32[3,320,128]{2,1,0:T(8,128)S(1)}, f32[3,320,128]{2,1,0:T(8,128)S(1)}, u32[]{:S(2)}, u32[]{:S(2)}) collective-permute-start(f32[3,320,128]{2,1,0:T(8,128)S(1)} %get-tuple-element.199), channel_id=1, source_target_pairs={{0,8},{8,16},{16,24},{24,32},{32,40},{40,48},{48,56},{56,64},{64,7... | collective-permute-start | bytes 1474568 | tf_op jit(solution)/shard_map/ppermute | solution.py:19
  227.4 11.6 %collective-permute-start.5 = (f32[3,320,128]{2,1,0:T(8,128)S(1)}, f32[3,320,128]{2,1,0:T(8,128)S(1)}, u32[]{:S(2)}, u32[]{:S(2)}) collective-permute-start(f32[3,320,128]{2,1,0:T(8,128)S(1)} %get-tuple-element.198), channel_id=1, source_target_pairs={{8,0},{16,8},{24,16},{32,24},{40,32},{48,40},{56,48},{64,56},{72,6... | collective-permute-start | bytes 1474568 | tf_op jit(solution)/shard_map/ppermute | solution.py:22
  239.1 1.0 copy-start.2
Sparse Core Ops, SparseCore 0:
  56.6 88.0 all-reduce.2
  240.3 80.2 all-reduce.4
where the time goes:
time: 333 us; the launch traced here: 331 us
  waiting for transfers between devices  174 us (52%)
  local copies, waits for them, and re-layouts  59.5 us (18%)
  other arithmetic  30.1 us (9%)
  starting transfers between devices  23.8 us (7%)
  between operations  18.8 us (6%)
  loops' own time  15.7 us (5%)
  matrix products  9.17 us (3%)
    psum x1, waiting for transfers between devices, local(): total_power = lax.psum(power, 'mode')  83 us
    psum x1, waiting for transfers between devices, local(): summed = lax.psum(fold_rims(wide), 'mode')  80.4 us
    dynamic_update_slice x4, local copies, waits for them, and re-layouts, deposit(): lax.dynamic_update_slice(total, current + pieces[index], (anchor, top_row...  36.1 us
    ppermute x3, starting transfers between devices, with_halo(): lax.ppermute(lax.slice_in_dim(block, block.shape[dim] - width, None, axis...  19.9 us
    another operation x1, loops' own time, local(): accumulated = lax.fori_loop(0, pieces.shape[0], deposit, start_total)  15.7 us
    gather x12, local copies, waits for them, and re-layouts  11.4 us
    dot_general x16, matrix products, product(): jnp.einsum(form, left_op, right_op, preferred_element_type=jnp.float32)  9.17 us
  transfers between devices with their start and end apart: 8, of which 4 were waited for; matrix products, arithmetic and copies ran while one was open for 11% of the time, Pallas kernels for 0%

commit v1 on v0

v1 whole, which is shorter than its diff:
```python
import functools

import jax
import jax.numpy as jnp
from jax import lax
from jax.experimental import pallas as pl
from jax.experimental.pallas import tpu as pltpu
from jax.sharding import PartitionSpec as P

P_SIZE = 256
BAND = 64
TW = 256
HALF = 128
OH = 320
MODES = 8
EXT = TW + HALF
TALL = P_SIZE + 8
GROUP = 2
F32 = jnp.float32
BF16 = jnp.bfloat16


def place_of(tiles):
    return lax.axis_index("tile"), lax.rem(lax.axis_index("mode"), 2)


def slot_of(pos_ref, tile, core, tiles, shift):
    block = tile + shift
    inside = (block >= 0) & (block < tiles)
    pattern = 2 * jnp.clip(block, 0, tiles - 1) + core
    return inside, pos_ref[0, pattern], pos_ref[1, pattern]


def aligned(top_row):
    extra = lax.rem(top_row, 8)
    return pl.multiple_of(top_row - extra, 8), extra


def lowered(window, extra, width):
    tall = jnp.concatenate([window, jnp.zeros((TALL - P_SIZE, P_SIZE), F32)], axis=0)
    return jnp.concatenate([pltpu.roll(tall, extra, 0), jnp.zeros((TALL, width - P_SIZE), F32)], axis=1)


def pack_kernel(obj, inten, inward, outward, sem):
    core = lax.rem(lax.axis_index("mode"), 2)
    edge = pl.ds(pl.multiple_of(core * HALF, HALF), HALF)
    moves = (
        (obj.at[0, :, edge], inward.at[0:OH]),
        (obj.at[1, :, edge], inward.at[OH : 2 * OH]),
        (inten.at[core, :, 0:HALF], inward.at[2 * OH : 2 * OH + P_SIZE]),
        (inten.at[core, :, HALF:P_SIZE], inward.at[2 * OH + P_SIZE : 2 * OH + 2 * P_SIZE]),
        (inten.at[core], outward),
    )
    copies = [pltpu.make_async_copy(src, dst, sem.at[i]) for i, (src, dst) in enumerate(moves)]
    for copy in copies:
        copy.start()
    for copy in copies:
        copy.wait()


def main_kernel(tiles, pos_ref, taps_ref, int_own, inward, outward, obj, *rest):
    probes_in = rest[:MODES]
    mid_out, rim_out, weight_out = rest[MODES : MODES + 3]
    (wave, total, meas, probe, far, low, midb, stack, stack_t, ratio, patch, acc, row_pad, sem) = rest[MODES + 3 :]
    tile, core = place_of(tiles)

    copies = []

    def bring(src, dst):
        copy = pltpu.make_async_copy(src, dst, sem.at[len(copies)])
        copy.start()
        copies.append(copy)

    rim = pl.ds(pl.multiple_of((1 - core) * TW, HALF), HALF)
    bring(obj, wave.at[:, :OH, pl.ds(pl.multiple_of(core * HALF, HALF), TW)])
    bring(inward.at[0:OH], wave.at[0, :OH, rim])
    bring(inward.at[OH : 2 * OH], wave.at[1, :OH, rim])
    bring(outward, meas.at[0])
    bring(int_own.at[core], meas.at[1])
    bring(inward.at[2 * OH : 2 * OH + P_SIZE], meas.at[2, :, 0:HALF])
    bring(inward.at[2 * OH + P_SIZE : 2 * OH + 2 * P_SIZE], meas.at[2, :, HALF:P_SIZE])
    for index in range(MODES):
        bring(probes_in[index].at[0], probe.at[index])

    row_pad[...] = jnp.zeros_like(row_pad)
    row_pad[0:2, 0 : 2 * BAND + 1] = taps_ref[...]

    def band(part):
        line = jnp.broadcast_to(row_pad[part : part + 1, :], (P_SIZE, 2 * P_SIZE))
        turned = pltpu.roll(line, 2 * P_SIZE - BAND, 1, stride=1, stride_axis=0)
        return turned[:, :P_SIZE]

    band_re = band(0)
    band_im = band(1)
    stack[:P_SIZE, :P_SIZE] = band_re.astype(BF16)
    stack[:P_SIZE, P_SIZE:] = (-band_im).astype(BF16)
    stack[P_SIZE:, :P_SIZE] = band_im.astype(BF16)
    stack[P_SIZE:, P_SIZE:] = band_re.astype(BF16)
    turned_re = band_re.T
    turned_im = band_im.T
    stack_t[:P_SIZE, :P_SIZE] = turned_re.astype(BF16)
    stack_t[:P_SIZE, P_SIZE:] = turned_im.astype(BF16)
    stack_t[P_SIZE:, :P_SIZE] = (-turned_im).astype(BF16)
    stack_t[P_SIZE:, P_SIZE:] = turned_re.astype(BF16)

    total[...] = jnp.zeros_like(total)
    for copy in copies:
        copy.wait()

    weight_out[...] = jnp.zeros_like(weight_out)

    @pl.loop(0, MODES)
    def _(mode):
        weight_out[...] += probe[mode, 0] * probe[mode, 0] + probe[mode, 1] * probe[mode, 1]

    def mix(first, second):
        mid = jnp.dot(first[...], low[...], preferred_element_type=F32)
        for unit in range(GROUP):
            own = slice(unit * P_SIZE, (unit + 1) * P_SIZE)
            midb[own, :P_SIZE] = mid[:P_SIZE, own].astype(BF16)
            midb[own, P_SIZE:] = mid[P_SIZE:, own].astype(BF16)
        return jnp.dot(midb[...], second[...], preferred_element_type=F32)

    @pl.loop(0, 3)
    def _(slot):
        shift = (slot - 1) * (1 - 2 * core)
        inside, top_row, column = slot_of(pos_ref, tile, core, tiles, shift)
        offset = column - tile * TW - (1 - core) * HALF
        here = inside & (column >= tile * TW) & (column < (tile + 1) * TW)

        @pl.when(here)
        def _():
            base, extra = aligned(top_row)
            for part in range(2):
                rows = wave[part, pl.ds(base, TALL), :]
                turned = pltpu.roll(rows, lax.rem(EXT - offset, EXT), 1)[:, :P_SIZE]
                patch[part] = pltpu.roll(turned, lax.rem(TALL - extra, TALL), 0)[:P_SIZE]
            for start in range(0, MODES, GROUP):
                for unit in range(GROUP):
                    own = slice(unit * P_SIZE, (unit + 1) * P_SIZE)
                    pr = probe[start + unit, 0]
                    pi = probe[start + unit, 1]
                    low[:P_SIZE, own] = (pr * patch[0] - pi * patch[1]).astype(BF16)
                    low[P_SIZE:, own] = (pr * patch[1] + pi * patch[0]).astype(BF16)
                out = mix(stack, stack_t)
                power = 0.0
                for unit in range(GROUP):
                    block = out[unit * P_SIZE : (unit + 1) * P_SIZE]
                    far[start + unit] = block
                    power += block[:, :P_SIZE] * block[:, :P_SIZE] + block[:, P_SIZE:] * block[:, P_SIZE:]
                ratio[...] = power if start == 0 else ratio[...] + power

            ratio[...] = jnp.sqrt(meas[slot]) / jnp.sqrt(ratio[...] + 1.0)
            acc[0] = -weight_out[...] * patch[0]
            acc[1] = -weight_out[...] * patch[1]

            for start in range(0, MODES, GROUP):
                for unit in range(GROUP):
                    own = slice(unit * P_SIZE, (unit + 1) * P_SIZE)
                    low[:P_SIZE, own] = (far[start + unit, :, :P_SIZE] * ratio[...]).astype(BF16)
                    low[P_SIZE:, own] = (far[start + unit, :, P_SIZE:] * ratio[...]).astype(BF16)
                out = mix(stack_t, stack)
                term_re = 0.0
                term_im = 0.0
                for unit in range(GROUP):
                    back_re = out[unit * P_SIZE : (unit + 1) * P_SIZE, :P_SIZE]
                    back_im = out[unit * P_SIZE : (unit + 1) * P_SIZE, P_SIZE:]
                    pr = probe[start + unit, 0]
                    pi = probe[start + unit, 1]
                    term_re += pr * back_re + pi * back_im
                    term_im += pr * back_im - pi * back_re
                acc[0] += term_re
                acc[1] += term_im

            for part in range(2):
                total[part, pl.ds(base, TALL), :] += pltpu.roll(lowered(acc[part], extra, EXT), offset, 1)

    mid_out[...] = total[:, :OH, pl.ds(pl.multiple_of(core * HALF, HALF), TW)]
    rim_out[...] = total[:, :OH, rim]


def denom_kernel(tiles, pos_ref, weight_in, scale, denom, weight, sem):
    tile, _ = place_of(tiles)
    copy = pltpu.make_async_copy(weight_in, weight, sem)
    copy.start()
    copy.wait()
    denom[...] = jnp.zeros_like(denom)
    for parity, shifts in ((0, (-2, -1, 0, 1)), (1, (-1, 0, 1, 2))):
        for shift in shifts:
            inside, top_row, column = slot_of(pos_ref, tile, parity, tiles, shift)
            start = column - HALF - tile * TW

            @pl.when(inside & (start > -P_SIZE) & (start < TW))
            def _():
                base, extra = aligned(top_row)
                wide = lowered(weight[...], extra, 2 * P_SIZE)
                turned = pltpu.roll(wide, jnp.where(start < 0, start + 2 * P_SIZE, start), 1)
                denom[pl.ds(base, TALL), :] += turned[:, :TW]

    scale[...] = 1.0 / (denom[:OH] + 0.5)


ANY = pl.BlockSpec(memory_space=pl.ANY)
VMEM = pl.BlockSpec(memory_space=pltpu.VMEM)
SMEM = pl.BlockSpec(memory_space=pltpu.SMEM)


def local(intensity, positions, object_field, probe_modes, kernel_taps):
    tiles = lax.axis_size("tile")
    modes = lax.axis_size("mode")
    core = lax.rem(lax.axis_index("mode"), 2)
    spots = positions.T

    def along_x(array, steps):
        return lax.ppermute(array, "mode", [(i, (i + 2 * steps) % modes) for i in range(modes)])

    def swap(array):
        return lax.ppermute(array, "mode", [(i, i ^ 1) for i in range(modes)])

    def between_tiles(array, cross):
        pairs = []
        for tile in range(tiles):
            for mode in range(modes):
                target = tile + 1 if mode % 2 == 0 else tile - 1
                if 0 <= target < tiles:
                    pairs.append((tile * modes + mode, target * modes + (mode ^ 1 if cross else mode)))
        return lax.ppermute(array, ("tile", "mode"), pairs)

    def from_tile(array, step):
        pairs = []
        for tile in range(tiles):
            for mode in range(modes):
                source = tile + step if mode % 2 == 0 else tile - step
                if 0 <= source < tiles:
                    pairs.append((source * modes + mode, tile * modes + mode))
        return lax.ppermute(array, ("tile", "mode"), pairs)

    ring = [along_x(probe_modes, step) for step in (1, -1, 2)]
    inward, outward = pl.pallas_call(
        pack_kernel,
        out_shape=(
            jax.ShapeDtypeStruct((2 * OH + 2 * P_SIZE, HALF), F32),
            jax.ShapeDtypeStruct((P_SIZE, P_SIZE), F32),
        ),
        in_specs=[ANY, ANY],
        out_specs=(ANY, ANY),
        scratch_shapes=[pltpu.SemaphoreType.DMA((5,))],
        name="pack",
    )(object_field, intensity)
    inward = from_tile(inward, 1)
    outward = from_tile(outward, -1)
    ring[0], ring[1], inward, outward = lax.optimization_barrier((ring[0], ring[1], inward, outward))
    own = [probe_modes] + ring
    probes = own + [swap(array) for array in own]

    middle, rim, weight = pl.pallas_call(
        functools.partial(main_kernel, tiles),
        out_shape=(
            jax.ShapeDtypeStruct((2, OH, TW), F32),
            jax.ShapeDtypeStruct((2, OH, HALF), F32),
            jax.ShapeDtypeStruct((P_SIZE, P_SIZE), F32),
        ),
        in_specs=[SMEM, VMEM] + [ANY] * (4 + MODES),
        out_specs=(VMEM, VMEM, VMEM),
        scratch_shapes=[
            pltpu.VMEM((2, OH + 8, EXT), F32),
            pltpu.VMEM((2, OH + 8, EXT), F32),
            pltpu.VMEM((3, P_SIZE, P_SIZE), F32),
            pltpu.VMEM((MODES, 2, P_SIZE, P_SIZE), F32),
            pltpu.VMEM((MODES, P_SIZE, 2 * P_SIZE), F32),
            pltpu.VMEM((2 * P_SIZE, GROUP * P_SIZE), BF16),
            pltpu.VMEM((GROUP * P_SIZE, 2 * P_SIZE), BF16),
            pltpu.VMEM((2 * P_SIZE, 2 * P_SIZE), BF16),
            pltpu.VMEM((2 * P_SIZE, 2 * P_SIZE), BF16),
            pltpu.VMEM((P_SIZE, P_SIZE), F32),
            pltpu.VMEM((2, P_SIZE, P_SIZE), F32),
            pltpu.VMEM((2, P_SIZE, P_SIZE), F32),
            pltpu.VMEM((8, 2 * P_SIZE), F32),
            pltpu.SemaphoreType.DMA((7 + MODES,)),
        ],
        compiler_params=pltpu.CompilerParams(vmem_limit_bytes=28 * 2**20),
        name="update_terms",
    )(spots, kernel_taps, intensity, inward, outward, object_field, *probes)

    rim_same = between_tiles(rim, False)
    rim_cross = between_tiles(rim, True)
    scale = pl.pallas_call(
        functools.partial(denom_kernel, tiles),
        out_shape=jax.ShapeDtypeStruct((OH, TW), F32),
        in_specs=[SMEM, ANY],
        out_specs=VMEM,
        scratch_shapes=[
            pltpu.VMEM((OH + 8, TW), F32),
            pltpu.VMEM((P_SIZE, P_SIZE), F32),
            pltpu.SemaphoreType.DMA,
        ],
        name="denominator",
    )(spots, weight)
    other = swap(middle)
    low = jnp.where(core == 0, rim_same, rim_cross)
    high = jnp.where(core == 0, rim_cross, rim_same)
    return object_field + (middle + other + jnp.concatenate([low, high], axis=2)) * scale


def solution(mesh):
    return jax.shard_map(
        local,
        mesh=mesh,
        in_specs=(
            P("tile", None, None),
            P(),
            P(None, None, "tile"),
            P("mode", None, None, None),
            P(),
        ),
        out_specs=P(None, None, "tile"),
        check_vma=False,
    )
```

time: 333 us -> 102 us (0.31)
  the two profiles are of different devices: /device:TPU:1 before, /device:TPU:513 now
where the time goes in v1:
time: 102 us
  starting transfers between devices  48.4 us (47%)
  Pallas kernels  38.7 us (38%)
  waiting for transfers between devices  11.5 us (11%)
  local copies, waits for them, and re-layouts  1.75 us (2%)
  other arithmetic  1.09 us (1%)
    pallas_call x1, Pallas kernels, local(): pl.pallas_call(pack_kernel, out_shape=(jax.ShapeDtypeStruct((2 * OH + 2 *...  27 us
    ppermute x5, starting transfers between devices, swap(): return lax.ppermute(array, 'mode', [(i, i ^ 1) for i in range(modes)])  17.7 us
    ppermute x3, starting transfers between devices, along_x(): lax.ppermute(array, 'mode', [(i, (i + 2 * steps) % modes) for i in range(...  11.2 us
    ppermute x2, starting transfers between devices, between_tiles(): return lax.ppermute(array, ('tile', 'mode'), pairs)  10.9 us
    ppermute x2, starting transfers between devices, from_tile(): return lax.ppermute(array, ('tile', 'mode'), pairs)  8.6 us
    pallas_call x1, Pallas kernels, local(): pl.pallas_call(functools.partial(main_kernel, tiles), out_shape=(jax.Shap...  8.25 us
    ppermute x2, waiting for transfers between devices, between_tiles(): return lax.ppermute(array, ('tile', 'mode'), pairs)  5.99 us
    ppermute x2, waiting for transfers between devices, from_tile(): return lax.ppermute(array, ('tile', 'mode'), pairs)  3.61 us
  transfers between devices with their start and end apart: 12, of which 3 were waited for; matrix products, arithmetic and copies ran while one was open for 0% of the time, Pallas kernels for 3%

profile of v1, /device:TPU:513, one launch (start us, length us, event | category | flops | bytes accessed | tf_op | source)
XLA Modules:
  0.0 101.7 jit_solution(529893464369020091)
XLA Ops:
  0.0 27.0 %pack.1 = (f32[1152,128]{1,0:T(8,128)}, f32[256,256]{1,0:T(8,128)}) custom-call(f32[2,320,256]{2,1,0:T(8,128)} %obj.3, f32[2,256,256]{2,1,0:T(8,128)} %int_own.1), custom_call_target="tpu_custom_call" | custom-call | tf_op jit(solution)/shard_map/pack/pallas_call | solution.py:239
  27.0 0.0 copy-start.5
  27.0 0.0 copy-start.4
  27.0 3.2 %collective-permute-start.2 = (f32[1152,128]{1,0:T(8,128)}, f32[1152,128]{1,0:T(8,128)S(1)}, u32[]{:S(2)}, u32[]{:S(2)}) collective-permute-start(f32[1152,128]{1,0:T(8,128)} %get-tuple-element.14), channel_id=1, source_target_pairs={{8,0},{10,2},{12,4},{14,6},{16,8},{1,9},{18,10},{3,11},{20,12},{5,... | collective-permute-start | bytes 1769480 | tf_op jit(solution)/shard_map/ppermute | solution.py:236
  30.2 4.7 %collective-permute-start.4 = (f32[1,2,256,256]{3,2,1,0:T(8,128)}, f32[1,2,256,256]{3,2,1,0:T(8,128)S(1)}, u32[]{:S(2)}, u32[]{:S(2)}) collective-permute-start(f32[1,2,256,256]{3,2,1,0:T(8,128)} %rest_0_.1), channel_id=1, source_target_pairs={{0,4},{1,5},{2,6},{3,7},{4,0},{5,1},{6,2},{7,3},{8,12},{9,13},{10,... | collective-permute-start | bytes 1572872 | tf_op jit(solution)/shard_map/ppermute | solution.py:215
  34.9 2.2 %collective-permute-start = (f32[1,2,256,256]{3,2,1,0:T(8,128)}, f32[1,2,256,256]{3,2,1,0:T(8,128)S(1)}, u32[]{:S(2)}, u32[]{:S(2)}) collective-permute-start(f32[1,2,256,256]{3,2,1,0:T(8,128)} %rest_0_.1), channel_id=1, source_target_pairs={{0,2},{1,3},{2,4},{3,5},{4,6},{5,7},{6,0},{7,1},{8,10},{9,11},{10,... | collective-permute-start | bytes 1572872 | tf_op jit(solution)/shard_map/ppermute | solution.py:215
  37.1 4.3 %collective-permute-start.1 = (f32[1,2,256,256]{3,2,1,0:T(8,128)}, f32[1,2,256,256]{3,2,1,0:T(8,128)S(1)}, u32[]{:S(2)}, u32[]{:S(2)}) collective-permute-start(f32[1,2,256,256]{3,2,1,0:T(8,128)} %rest_0_.1), channel_id=1, source_target_pairs={{0,6},{1,7},{2,0},{3,1},{4,2},{5,3},{6,4},{7,5},{8,14},{9,15},{10,... | collective-permute-start | bytes 1572872 | tf_op jit(solution)/shard_map/ppermute | solution.py:215
  41.4 5.4 %collective-permute-start.3 = (f32[256,256]{1,0:T(8,128)}, f32[256,256]{1,0:T(8,128)S(1)}, u32[]{:S(2)}, u32[]{:S(2)}) collective-permute-start(f32[256,256]{1,0:T(8,128)} %get-tuple-element.15), channel_id=1, source_target_pairs={{9,1},{11,3},{13,5},{15,7},{0,8},{17,9},{2,10},{19,11},{4,12},{21,... | collective-permute-start | bytes 786440 | tf_op jit(solution)/shard_map/ppermute | solution.py:236
  46.8 3.6 %collective-permute-done.3.outward = f32[256,256]{1,0:T(8,128)S(1)} collective-permute-done((f32[256,256]{1,0:T(8,128)}, f32[256,256]{1,0:T(8,128)S(1)}, u32[]{:S(2)}, u32[]{:S(2)}) %collective-permute-start.3) | collective-permute-done | bytes 262176 | tf_op jit(solution)/shard_map/ppermute | solution.py:236
  50.4 9.6 %collective-permute-start.5 = (f32[1,2,256,256]{3,2,1,0:T(8,128)}, f32[1,2,256,256]{3,2,1,0:T(8,128)S(1)}, u32[]{:S(2)}, u32[]{:S(2)}) collective-permute-start(f32[1,2,256,256]{3,2,1,0:T(8,128)} %rest_0_.1), channel_id=1, source_target_pairs={{0,1},{1,0},{2,3},{3,2},{4,5},{5,4},{6,7},{7,6},{8,9},{9,8},{10,11... | collective-permute-start | bytes 1572872 | tf_op jit(solution)/shard_map/ppermute | solution.py:218
  60.0 0.0 collective-permute-done.4.rest_3_
  60.0 1.9 %collective-permute-start.8 = (f32[1,2,256,256]{3,2,1,0:T(8,128)S(1)}, f32[1,2,256,256]{3,2,1,0:T(8,128)S(1)}, u32[]{:S(2)}, u32[]{:S(2)}) collective-permute-start(f32[1,2,256,256]{3,2,1,0:T(8,128)S(1)} %collective-permute-done.4.rest_3_), channel_id=1, source_target_pairs={{0,1},{1,0},{2,3},{3,2},{4,5},{5,4},{6,7},{7,6},{8,9},{9,8},{10,11... | collective-permute-start | bytes 1572872 | tf_op jit(solution)/shard_map/ppermute | solution.py:218
  61.9 0.0 collective-permute-done.rest_1_
  61.9 0.0 collective-permute-done.1.rest_2_
  61.9 0.0 collective-permute-done.2.inward
  61.9 2.4 %collective-permute-start.6 = (f32[1,2,256,256]{3,2,1,0:T(8,128)S(1)}, f32[1,2,256,256]{3,2,1,0:T(8,128)S(1)}, u32[]{:S(2)}, u32[]{:S(2)}) collective-permute-start(f32[1,2,256,256]{3,2,1,0:T(8,128)S(1)} %collective-permute-done.rest_1_), channel_id=1, source_target_pairs={{0,1},{1,0},{2,3},{3,2},{4,5},{5,4},{6,7},{7,6},{8,9},{9,8},{10,11... | collective-permute-start | bytes 1572872 | tf_op jit(solution)/shard_map/ppermute | solution.py:218
  64.4 1.9 %collective-permute-start.7 = (f32[1,2,256,256]{3,2,1,0:T(8,128)S(1)}, f32[1,2,256,256]{3,2,1,0:T(8,128)S(1)}, u32[]{:S(2)}, u32[]{:S(2)}) collective-permute-start(f32[1,2,256,256]{3,2,1,0:T(8,128)S(1)} %collective-permute-done.1.rest_2_), channel_id=1, source_target_pairs={{0,1},{1,0},{2,3},{3,2},{4,5},{5,4},{6,7},{7,6},{8,9},{9,8},{10,11... | collective-permute-start | bytes 1572872 | tf_op jit(solution)/shard_map/ppermute | solution.py:218
  66.3 0.0 collective-permute-done.5.rest_4_
  66.3 0.0 collective-permute-done.8.rest_7_
  66.3 0.0 collective-permute-done.6.rest_5_
  66.3 1.8 %collective-permute-done.7.rest_6_ = f32[1,2,256,256]{3,2,1,0:T(8,128)S(1)} collective-permute-done((f32[1,2,256,256]{3,2,1,0:T(8,128)S(1)}, f32[1,2,256,256]{3,2,1,0:T(8,128)S(1)}, u32[]{:S(2)}, u32[]{:S(2)}) %collective-permute-start.7) | collective-permute-done | bytes 524320 | tf_op jit(solution)/shard_map/ppermute | solution.py:218
  68.2 0.0 copy-start.2
  68.2 1.0 %copy-done.2 = f32[1,2,256,256]{3,2,1,0:T(8,128)S(1)} copy-done((f32[1,2,256,256]{3,2,1,0:T(8,128)S(1)}, f32[1,2,256,256]{3,2,1,0:T(8,128)}, u32[]{:S(2)}) %copy-start.2) | copy-done | bytes 524312
  69.2 8.3 %update_terms.1 = (f32[2,320,256]{2,1,0:T(8,128)S(1)}, f32[2,320,128]{2,1,0:T(8,128)S(1)}, f32[256,256]{1,0:T(8,128)S(1)}) custom-call(s32[2,192]{1,0:T(2,128)S(1)} %bitcast.2, f32[2,129]{1,0:T(2,128)S(1)} %copy-done.5, f32[2,256,256]{2,1,0:T(8,128)S(1)} %copy-done.1, f32[1152,128]{1,0:T(8,128)S(1)} %collective-permute-done.2.inward, ...), custom_call_target="tpu_custom_call" | custom-call | tf_op jit(solution)/shard_map/update_terms/pallas_call | solution.py:256
  77.5 0.7 copy-done.3
  78.2 1.9 %collective-permute-start.9 = (f32[2,320,256]{2,1,0:T(8,128)S(1)}, f32[2,320,256]{2,1,0:T(8,128)S(1)}, u32[]{:S(2)}, u32[]{:S(2)}) collective-permute-start(f32[2,320,256]{2,1,0:T(8,128)S(1)} %get-tuple-element.20), channel_id=1, source_target_pairs={{0,1},{1,0},{2,3},{3,2},{4,5},{5,4},{6,7},{7,6},{8,9},{9,8},{10,11... | collective-permute-start | bytes 1966088 | tf_op jit(solution)/shard_map/ppermute | solution.py:218
  80.1 8.7 %collective-permute-start.10 = (f32[2,320,128]{2,1,0:T(8,128)S(1)}, f32[2,320,128]{2,1,0:T(8,128)S(1)}, u32[]{:S(2)}, u32[]{:S(2)}) collective-permute-start(f32[2,320,128]{2,1,0:T(8,128)S(1)} %get-tuple-element.21), channel_id=1, source_target_pairs={{0,8},{2,10},{4,12},{6,14},{8,16},{9,1},{10,18},{11,3},{12,20},{13... | collective-permute-start | bytes 983048 | tf_op jit(solution)/shard_map/ppermute | solution.py:227
  88.8 2.2 %collective-permute-start.11 = (f32[2,320,128]{2,1,0:T(8,128)S(1)}, f32[2,320,128]{2,1,0:T(8,128)S(1)}, u32[]{:S(2)}, u32[]{:S(2)}) collective-permute-start(f32[2,320,128]{2,1,0:T(8,128)S(1)} %get-tuple-element.21), channel_id=1, source_target_pairs={{0,9},{2,11},{4,13},{6,15},{8,17},{9,0},{10,19},{11,2},{12,21},{13... | collective-permute-start | bytes 983048 | tf_op jit(solution)/shard_map/ppermute | solution.py:227
  91.0 3.5 %denominator.1 = f32[320,256]{1,0:T(8,128)} custom-call(s32[2,192]{1,0:T(2,128)} %bitcast.1, f32[256,256]{1,0:T(8,128)} %copy-done.3), custom_call_target="tpu_custom_call" | custom-call | tf_op jit(solution)/shard_map/denominator/pallas_call | solution.py:287
  94.5 0.0 copy-start.6
  94.6 6.0 %collective-permute-done.11 = f32[2,320,128]{2,1,0:T(8,128)S(1)} collective-permute-done((f32[2,320,128]{2,1,0:T(8,128)S(1)}, f32[2,320,128]{2,1,0:T(8,128)S(1)}, u32[]{:S(2)}, u32[]{:S(2)}) %collective-permute-start.11) | collective-permute-done | bytes 327712 | tf_op jit(solution)/shard_map/ppermute | solution.py:227
  100.6 1.0 %fusion.1 = f32[2,320,256]{2,1,0:T(8,128)} fusion(f32[2,320,256]{2,1,0:T(8,128)S(1)} %copy-done, f32[2,320,128]{2,1,0:T(8,128)S(1)} %get-tuple-element.24, f32[2,320,128]{2,1,0:T(8,128)S(1)} %get-tuple-element.23, f32[2,320,256]{2,1,0:T(8,128)S(1)} %get-tuple-element.20, f32[2,320,256]{2,1,0:T(8,128)S(1)} %collective-permute-done.9, f32[320,256]{1,0:T(8,128)S(1)} %copy-done.6), kind=kLoop, calls=%fused_computation.2 | loop fusion | flops 819200 | bytes 3604480 | tf_op jit(solution)/shard_map/add | solution.py:302
  (11 shorter events, 0.1 us)
Async XLA Ops:
  0.0 68.2 %copy-start.1 = (f32[2,256,256]{2,1,0:T(8,128)S(1)}, f32[2,256,256]{2,1,0:T(8,128)}, u32[]{:S(2)}) copy-start(f32[2,256,256]{2,1,0:T(8,128)} %int_own.1) | copy-start | bytes 1572868
  0.0 68.2 %copy-start = (f32[2,320,256]{2,1,0:T(8,128)S(1)}, f32[2,320,256]{2,1,0:T(8,128)}, u32[]{:S(2)}) copy-start(f32[2,320,256]{2,1,0:T(8,128)} %obj.3) | copy-start | bytes 1966084
  27.0 41.2 %copy-start.5 = (f32[2,129]{1,0:T(2,128)S(1)}, f32[2,129]{1,0:T(2,128)}, u32[]{:S(2)}) copy-start(f32[2,129]{1,0:T(2,128)} %taps_ref.1) | copy-start | bytes 3100
  27.0 41.2 %copy-start.4 = (s32[192,2]{0,1:T(2,128)S(1)}, s32[192,2]{0,1:T(2,128)}, u32[]{:S(2)}) copy-start(s32[192,2]{0,1:T(2,128)} %param.6) | copy-start | bytes 4612
  27.0 34.9 %collective-permute-start.2 = (f32[1152,128]{1,0:T(8,128)}, f32[1152,128]{1,0:T(8,128)S(1)}, u32[]{:S(2)}, u32[]{:S(2)}) collective-permute-start(f32[1152,128]{1,0:T(8,128)} %get-tuple-element.14), channel_id=1, source_target_pairs={{8,0},{10,2},{12,4},{14,6},{16,8},{1,9},{18,10},{3,11},{20,12},{5,... | collective-permute-start | bytes 1769480 | tf_op jit(solution)/shard_map/ppermute | solution.py:236
  30.2 29.8 %collective-permute-start.4 = (f32[1,2,256,256]{3,2,1,0:T(8,128)}, f32[1,2,256,256]{3,2,1,0:T(8,128)S(1)}, u32[]{:S(2)}, u32[]{:S(2)}) collective-permute-start(f32[1,2,256,256]{3,2,1,0:T(8,128)} %rest_0_.1), channel_id=1, source_target_pairs={{0,4},{1,5},{2,6},{3,7},{4,0},{5,1},{6,2},{7,3},{8,12},{9,13},{10,... | collective-permute-start | bytes 1572872 | tf_op jit(solution)/shard_map/ppermute | solution.py:215
  34.9 27.0 %collective-permute-start = (f32[1,2,256,256]{3,2,1,0:T(8,128)}, f32[1,2,256,256]{3,2,1,0:T(8,128)S(1)}, u32[]{:S(2)}, u32[]{:S(2)}) collective-permute-start(f32[1,2,256,256]{3,2,1,0:T(8,128)} %rest_0_.1), channel_id=1, source_target_pairs={{0,2},{1,3},{2,4},{3,5},{4,6},{5,7},{6,0},{7,1},{8,10},{9,11},{10,... | collective-permute-start | bytes 1572872 | tf_op jit(solution)/shard_map/ppermute | solution.py:215
  37.1 24.8 %collective-permute-start.1 = (f32[1,2,256,256]{3,2,1,0:T(8,128)}, f32[1,2,256,256]{3,2,1,0:T(8,128)S(1)}, u32[]{:S(2)}, u32[]{:S(2)}) collective-permute-start(f32[1,2,256,256]{3,2,1,0:T(8,128)} %rest_0_.1), channel_id=1, source_target_pairs={{0,6},{1,7},{2,0},{3,1},{4,2},{5,3},{6,4},{7,5},{8,14},{9,15},{10,... | collective-permute-start | bytes 1572872 | tf_op jit(solution)/shard_map/ppermute | solution.py:215
  41.4 9.0 %collective-permute-start.3 = (f32[256,256]{1,0:T(8,128)}, f32[256,256]{1,0:T(8,128)S(1)}, u32[]{:S(2)}, u32[]{:S(2)}) collective-permute-start(f32[256,256]{1,0:T(8,128)} %get-tuple-element.15), channel_id=1, source_target_pairs={{9,1},{11,3},{13,5},{15,7},{0,8},{17,9},{2,10},{19,11},{4,12},{21,... | collective-permute-start | bytes 786440 | tf_op jit(solution)/shard_map/ppermute | solution.py:236
  50.4 15.9 %collective-permute-start.5 = (f32[1,2,256,256]{3,2,1,0:T(8,128)}, f32[1,2,256,256]{3,2,1,0:T(8,128)S(1)}, u32[]{:S(2)}, u32[]{:S(2)}) collective-permute-start(f32[1,2,256,256]{3,2,1,0:T(8,128)} %rest_0_.1), channel_id=1, source_target_pairs={{0,1},{1,0},{2,3},{3,2},{4,5},{5,4},{6,7},{7,6},{8,9},{9,8},{10,11... | collective-permute-start | bytes 1572872 | tf_op jit(solution)/shard_map/ppermute | solution.py:218
  60.0 6.3 %collective-permute-start.8 = (f32[1,2,256,256]{3,2,1,0:T(8,128)S(1)}, f32[1,2,256,256]{3,2,1,0:T(8,128)S(1)}, u32[]{:S(2)}, u32[]{:S(2)}) collective-permute-start(f32[1,2,256,256]{3,2,1,0:T(8,128)S(1)} %collective-permute-done.4.rest_3_), channel_id=1, source_target_pairs={{0,1},{1,0},{2,3},{3,2},{4,5},{5,4},{6,7},{7,6},{8,9},{9,8},{10,11... | collective-permute-start | bytes 1572872 | tf_op jit(solution)/shard_map/ppermute | solution.py:218
  61.9 4.4 %collective-permute-start.6 = (f32[1,2,256,256]{3,2,1,0:T(8,128)S(1)}, f32[1,2,256,256]{3,2,1,0:T(8,128)S(1)}, u32[]{:S(2)}, u32[]{:S(2)}) collective-permute-start(f32[1,2,256,256]{3,2,1,0:T(8,128)S(1)} %collective-permute-done.rest_1_), channel_id=1, source_target_pairs={{0,1},{1,0},{2,3},{3,2},{4,5},{5,4},{6,7},{7,6},{8,9},{9,8},{10,11... | collective-permute-start | bytes 1572872 | tf_op jit(solution)/shard_map/ppermute | solution.py:218
  64.4 3.8 %collective-permute-start.7 = (f32[1,2,256,256]{3,2,1,0:T(8,128)S(1)}, f32[1,2,256,256]{3,2,1,0:T(8,128)S(1)}, u32[]{:S(2)}, u32[]{:S(2)}) collective-permute-start(f32[1,2,256,256]{3,2,1,0:T(8,128)S(1)} %collective-permute-done.1.rest_2_), channel_id=1, source_target_pairs={{0,1},{1,0},{2,3},{3,2},{4,5},{5,4},{6,7},{7,6},{8,9},{9,8},{10,11... | collective-permute-start | bytes 1572872 | tf_op jit(solution)/shard_map/ppermute | solution.py:218
  68.2 1.0 %copy-start.2 = (f32[1,2,256,256]{3,2,1,0:T(8,128)S(1)}, f32[1,2,256,256]{3,2,1,0:T(8,128)}, u32[]{:S(2)}) copy-start(f32[1,2,256,256]{3,2,1,0:T(8,128)} %rest_0_.1) | copy-start | bytes 1572868
  77.5 0.7 copy-start.3
  78.2 22.4 %collective-permute-start.9 = (f32[2,320,256]{2,1,0:T(8,128)S(1)}, f32[2,320,256]{2,1,0:T(8,128)S(1)}, u32[]{:S(2)}, u32[]{:S(2)}) collective-permute-start(f32[2,320,256]{2,1,0:T(8,128)S(1)} %get-tuple-element.20), channel_id=1, source_target_pairs={{0,1},{1,0},{2,3},{3,2},{4,5},{5,4},{6,7},{7,6},{8,9},{9,8},{10,11... | collective-permute-start | bytes 1966088 | tf_op jit(solution)/shard_map/ppermute | solution.py:218
  80.1 14.5 %collective-permute-start.10 = (f32[2,320,128]{2,1,0:T(8,128)S(1)}, f32[2,320,128]{2,1,0:T(8,128)S(1)}, u32[]{:S(2)}, u32[]{:S(2)}) collective-permute-start(f32[2,320,128]{2,1,0:T(8,128)S(1)} %get-tuple-element.21), channel_id=1, source_target_pairs={{0,8},{2,10},{4,12},{6,14},{8,16},{9,1},{10,18},{11,3},{12,20},{13... | collective-permute-start | bytes 983048 | tf_op jit(solution)/shard_map/ppermute | solution.py:227
  88.8 11.7 %collective-permute-start.11 = (f32[2,320,128]{2,1,0:T(8,128)S(1)}, f32[2,320,128]{2,1,0:T(8,128)S(1)}, u32[]{:S(2)}, u32[]{:S(2)}) collective-permute-start(f32[2,320,128]{2,1,0:T(8,128)S(1)} %get-tuple-element.21), channel_id=1, source_target_pairs={{0,9},{2,11},{4,13},{6,15},{8,17},{9,0},{10,19},{11,2},{12,21},{13... | collective-permute-start | bytes 983048 | tf_op jit(solution)/shard_map/ppermute | solution.py:227
  94.5 6.1 %copy-start.6 = (f32[320,256]{1,0:T(8,128)S(1)}, f32[320,256]{1,0:T(8,128)}, u32[]{:S(2)}) copy-start(f32[320,256]{1,0:T(8,128)} %denominator.1) | copy-start | bytes 983044

commit v2 on v1

--- a/solution.py
+++ b/solution.py
@@ -243,7 +243,7 @@
             jax.ShapeDtypeStruct((P_SIZE, P_SIZE), F32),
         ),
         in_specs=[ANY, ANY],
-        out_specs=(ANY, ANY),
+        out_specs=(VMEM, VMEM),
         scratch_shapes=[pltpu.SemaphoreType.DMA((5,))],
         name="pack",
     )(object_field, intensity)

time: 102 us -> 78.8 us (0.77)
  Pallas kernels: 38.7 us -> 20.6 us
  waiting for transfers between devices: 11.5 us -> 7.78 us
  starting transfers between devices: 48.4 us -> 46.7 us
    pallas_call x1, Pallas kernels: 27 us -> 2.26 us  [local(): pl.pallas_call(pack_kernel, out_shape=(jax.ShapeDtypeStruct((2 * OH + 2 *...]
    pallas_call x1, Pallas kernels: 8.25 us -> 14.4 us  [local(): pl.pallas_call(functools.partial(main_kernel, tiles), out_shape=(jax.Shap...]
    ppermute x2, waiting for transfers between devices: 5.99 us -> 2.3 us  [between_tiles(): return lax.ppermute(array, ('tile', 'mode'), pairs)]
    ppermute x2, starting transfers between devices: 10.9 us -> 9.14 us  [between_tiles(): return lax.ppermute(array, ('tile', 'mode'), pairs)]
  transfers between devices with their start and end apart: 12 -> 12, of which waited for: 3 -> 3; matrix products, arithmetic and copies ran while one was open for 0% -> 0% of each run, Pallas kernels for 3% -> 5%
where the time goes in v2:
time: 78.8 us; the launch traced here: 78.3 us
  starting transfers between devices  46.7 us (59%)
  Pallas kernels  20.6 us (26%)
  waiting for transfers between devices  7.78 us (10%)
  local copies, waits for them, and re-layouts  1.75 us (2%)
  other arithmetic  1.09 us (1%)
    ppermute x5, starting transfers between devices, swap(): return lax.ppermute(array, 'mode', [(i, i ^ 1) for i in range(modes)])  17.8 us
    pallas_call x1, Pallas kernels, local(): pl.pallas_call(functools.partial(main_kernel, tiles), out_shape=(jax.Shap...  14.4 us
    ppermute x3, starting transfers between devices, along_x(): lax.ppermute(array, 'mode', [(i, (i + 2 * steps) % modes) for i in range(...  11.2 us
    ppermute x2, starting transfers between devices, between_tiles(): return lax.ppermute(array, ('tile', 'mode'), pairs)  9.14 us
    ppermute x2, starting transfers between devices, from_tile(): return lax.ppermute(array, ('tile', 'mode'), pairs)  8.6 us
    pallas_call x1, Pallas kernels, local(): pl.pallas_call(functools.partial(denom_kernel, tiles), out_shape=jax.Shap...  3.99 us
    ppermute x2, waiting for transfers between devices, from_tile(): return lax.ppermute(array, ('tile', 'mode'), pairs)  3.61 us
    ppermute x2, waiting for transfers between devices, between_tiles(): return lax.ppermute(array, ('tile', 'mode'), pairs)  2.3 us
  transfers between devices with their start and end apart: 12, of which 3 were waited for; matrix products, arithmetic and copies ran while one was open for 0% of the time, Pallas kernels for 5%

profile of v2, /device:TPU:513, one launch (start us, length us, event | category | flops | bytes accessed | tf_op | source)
XLA Modules:
  0.0 78.3 jit_solution(8678254335456324497)
XLA Ops:
  0.0 2.3 %pack.1 = (f32[1152,128]{1,0:T(8,128)}, f32[256,256]{1,0:T(8,128)}) custom-call(f32[2,320,256]{2,1,0:T(8,128)} %obj.3, f32[2,256,256]{2,1,0:T(8,128)} %int_own.1), custom_call_target="tpu_custom_call" | custom-call | tf_op jit(solution)/shard_map/pack/pallas_call | solution.py:239
  2.3 0.0 copy-start.5
  2.3 0.0 copy-start.4
  2.3 3.2 %collective-permute-start.2 = (f32[1152,128]{1,0:T(8,128)}, f32[1152,128]{1,0:T(8,128)S(1)}, u32[]{:S(2)}, u32[]{:S(2)}) collective-permute-start(f32[1152,128]{1,0:T(8,128)} %get-tuple-element.14), channel_id=1, source_target_pairs={{8,0},{10,2},{12,4},{14,6},{16,8},{1,9},{18,10},{3,11},{20,12},{5,... | collective-permute-start | bytes 1769480 | tf_op jit(solution)/shard_map/ppermute | solution.py:236
  5.5 4.7 %collective-permute-start.4 = (f32[1,2,256,256]{3,2,1,0:T(8,128)}, f32[1,2,256,256]{3,2,1,0:T(8,128)S(1)}, u32[]{:S(2)}, u32[]{:S(2)}) collective-permute-start(f32[1,2,256,256]{3,2,1,0:T(8,128)} %rest_0_.1), channel_id=1, source_target_pairs={{0,4},{1,5},{2,6},{3,7},{4,0},{5,1},{6,2},{7,3},{8,12},{9,13},{10,... | collective-permute-start | bytes 1572872 | tf_op jit(solution)/shard_map/ppermute | solution.py:215
  10.2 2.2 %collective-permute-start = (f32[1,2,256,256]{3,2,1,0:T(8,128)}, f32[1,2,256,256]{3,2,1,0:T(8,128)S(1)}, u32[]{:S(2)}, u32[]{:S(2)}) collective-permute-start(f32[1,2,256,256]{3,2,1,0:T(8,128)} %rest_0_.1), channel_id=1, source_target_pairs={{0,2},{1,3},{2,4},{3,5},{4,6},{5,7},{6,0},{7,1},{8,10},{9,11},{10,... | collective-permute-start | bytes 1572872 | tf_op jit(solution)/shard_map/ppermute | solution.py:215
  12.4 4.3 %collective-permute-start.1 = (f32[1,2,256,256]{3,2,1,0:T(8,128)}, f32[1,2,256,256]{3,2,1,0:T(8,128)S(1)}, u32[]{:S(2)}, u32[]{:S(2)}) collective-permute-start(f32[1,2,256,256]{3,2,1,0:T(8,128)} %rest_0_.1), channel_id=1, source_target_pairs={{0,6},{1,7},{2,0},{3,1},{4,2},{5,3},{6,4},{7,5},{8,14},{9,15},{10,... | collective-permute-start | bytes 1572872 | tf_op jit(solution)/shard_map/ppermute | solution.py:215
  16.7 5.4 %collective-permute-start.3 = (f32[256,256]{1,0:T(8,128)}, f32[256,256]{1,0:T(8,128)S(1)}, u32[]{:S(2)}, u32[]{:S(2)}) collective-permute-start(f32[256,256]{1,0:T(8,128)} %get-tuple-element.15), channel_id=1, source_target_pairs={{9,1},{11,3},{13,5},{15,7},{0,8},{17,9},{2,10},{19,11},{4,12},{21,... | collective-permute-start | bytes 786440 | tf_op jit(solution)/shard_map/ppermute | solution.py:236
  22.1 3.6 %collective-permute-done.3.outward = f32[256,256]{1,0:T(8,128)S(1)} collective-permute-done((f32[256,256]{1,0:T(8,128)}, f32[256,256]{1,0:T(8,128)S(1)}, u32[]{:S(2)}, u32[]{:S(2)}) %collective-permute-start.3) | collective-permute-done | bytes 262176 | tf_op jit(solution)/shard_map/ppermute | solution.py:236
  25.7 9.6 %collective-permute-start.5 = (f32[1,2,256,256]{3,2,1,0:T(8,128)}, f32[1,2,256,256]{3,2,1,0:T(8,128)S(1)}, u32[]{:S(2)}, u32[]{:S(2)}) collective-permute-start(f32[1,2,256,256]{3,2,1,0:T(8,128)} %rest_0_.1), channel_id=1, source_target_pairs={{0,1},{1,0},{2,3},{3,2},{4,5},{5,4},{6,7},{7,6},{8,9},{9,8},{10,11... | collective-permute-start | bytes 1572872 | tf_op jit(solution)/shard_map/ppermute | solution.py:218
  35.3 0.0 collective-permute-done.4.rest_3_
  35.3 1.9 %collective-permute-start.8 = (f32[1,2,256,256]{3,2,1,0:T(8,128)S(1)}, f32[1,2,256,256]{3,2,1,0:T(8,128)S(1)}, u32[]{:S(2)}, u32[]{:S(2)}) collective-permute-start(f32[1,2,256,256]{3,2,1,0:T(8,128)S(1)} %collective-permute-done.4.rest_3_), channel_id=1, source_target_pairs={{0,1},{1,0},{2,3},{3,2},{4,5},{5,4},{6,7},{7,6},{8,9},{9,8},{10,11... | collective-permute-start | bytes 1572872 | tf_op jit(solution)/shard_map/ppermute | solution.py:218
  37.2 0.0 collective-permute-done.rest_1_
  37.2 0.0 collective-permute-done.1.rest_2_
  37.2 0.0 collective-permute-done.2.inward
  37.2 2.4 %collective-permute-start.6 = (f32[1,2,256,256]{3,2,1,0:T(8,128)S(1)}, f32[1,2,256,256]{3,2,1,0:T(8,128)S(1)}, u32[]{:S(2)}, u32[]{:S(2)}) collective-permute-start(f32[1,2,256,256]{3,2,1,0:T(8,128)S(1)} %collective-permute-done.rest_1_), channel_id=1, source_target_pairs={{0,1},{1,0},{2,3},{3,2},{4,5},{5,4},{6,7},{7,6},{8,9},{9,8},{10,11... | collective-permute-start | bytes 1572872 | tf_op jit(solution)/shard_map/ppermute | solution.py:218
  39.7 1.9 %collective-permute-start.7 = (f32[1,2,256,256]{3,2,1,0:T(8,128)S(1)}, f32[1,2,256,256]{3,2,1,0:T(8,128)S(1)}, u32[]{:S(2)}, u32[]{:S(2)}) collective-permute-start(f32[1,2,256,256]{3,2,1,0:T(8,128)S(1)} %collective-permute-done.1.rest_2_), channel_id=1, source_target_pairs={{0,1},{1,0},{2,3},{3,2},{4,5},{5,4},{6,7},{7,6},{8,9},{9,8},{10,11... | collective-permute-start | bytes 1572872 | tf_op jit(solution)/shard_map/ppermute | solution.py:218
  41.6 0.0 collective-permute-done.5.rest_4_
  41.6 0.0 collective-permute-done.6.rest_5_
  41.6 1.8 %collective-permute-done.7.rest_6_ = f32[1,2,256,256]{3,2,1,0:T(8,128)S(1)} collective-permute-done((f32[1,2,256,256]{3,2,1,0:T(8,128)S(1)}, f32[1,2,256,256]{3,2,1,0:T(8,128)S(1)}, u32[]{:S(2)}, u32[]{:S(2)}) %collective-permute-start.7) | collective-permute-done | bytes 524320 | tf_op jit(solution)/shard_map/ppermute | solution.py:218
  43.5 0.0 copy-start.2
  43.5 1.0 %copy-done.2 = f32[1,2,256,256]{3,2,1,0:T(8,128)S(1)} copy-done((f32[1,2,256,256]{3,2,1,0:T(8,128)S(1)}, f32[1,2,256,256]{3,2,1,0:T(8,128)}, u32[]{:S(2)}) %copy-start.2) | copy-done | bytes 524312
  44.5 14.4 %update_terms.1 = (f32[2,320,256]{2,1,0:T(8,128)S(1)}, f32[2,320,128]{2,1,0:T(8,128)S(1)}, f32[256,256]{1,0:T(8,128)S(1)}) custom-call(s32[2,192]{1,0:T(2,128)S(1)} %bitcast.2, f32[2,129]{1,0:T(2,128)S(1)} %copy-done.5, f32[2,256,256]{2,1,0:T(8,128)S(1)} %copy-done.1, f32[1152,128]{1,0:T(8,128)S(1)} %collective-permute-done.2.inward, ...), custom_call_target="tpu_custom_call" | custom-call | tf_op jit(solution)/shard_map/update_terms/pallas_call | solution.py:256
  58.9 0.7 copy-done.3
  59.6 2.0 %collective-permute-start.9 = (f32[2,320,256]{2,1,0:T(8,128)S(1)}, f32[2,320,256]{2,1,0:T(8,128)S(1)}, u32[]{:S(2)}, u32[]{:S(2)}) collective-permute-start(f32[2,320,256]{2,1,0:T(8,128)S(1)} %get-tuple-element.20), channel_id=1, source_target_pairs={{0,1},{1,0},{2,3},{3,2},{4,5},{5,4},{6,7},{7,6},{8,9},{9,8},{10,11... | collective-permute-start | bytes 1966088 | tf_op jit(solution)/shard_map/ppermute | solution.py:218
  61.7 1.9 %collective-permute-start.10 = (f32[2,320,128]{2,1,0:T(8,128)S(1)}, f32[2,320,128]{2,1,0:T(8,128)S(1)}, u32[]{:S(2)}, u32[]{:S(2)}) collective-permute-start(f32[2,320,128]{2,1,0:T(8,128)S(1)} %get-tuple-element.21), channel_id=1, source_target_pairs={{0,8},{2,10},{4,12},{6,14},{8,16},{9,1},{10,18},{11,3},{12,20},{13... | collective-permute-start | bytes 983048 | tf_op jit(solution)/shard_map/ppermute | solution.py:227
  63.6 7.2 %collective-permute-start.11 = (f32[2,320,128]{2,1,0:T(8,128)S(1)}, f32[2,320,128]{2,1,0:T(8,128)S(1)}, u32[]{:S(2)}, u32[]{:S(2)}) collective-permute-start(f32[2,320,128]{2,1,0:T(8,128)S(1)} %get-tuple-element.21), channel_id=1, source_target_pairs={{0,9},{2,11},{4,13},{6,15},{8,17},{9,0},{10,19},{11,2},{12,21},{13... | collective-permute-start | bytes 983048 | tf_op jit(solution)/shard_map/ppermute | solution.py:227
  70.8 4.0 %denominator.1 = f32[320,256]{1,0:T(8,128)} custom-call(s32[2,192]{1,0:T(2,128)} %bitcast.1, f32[256,256]{1,0:T(8,128)} %copy-done.3), custom_call_target="tpu_custom_call" | custom-call | tf_op jit(solution)/shard_map/denominator/pallas_call | solution.py:287
  74.8 0.0 copy-start.6
  74.8 0.0 collective-permute-done.10
  74.8 2.3 %collective-permute-done.11 = f32[2,320,128]{2,1,0:T(8,128)S(1)} collective-permute-done((f32[2,320,128]{2,1,0:T(8,128)S(1)}, f32[2,320,128]{2,1,0:T(8,128)S(1)}, u32[]{:S(2)}, u32[]{:S(2)}) %collective-permute-start.11) | collective-permute-done | bytes 327712 | tf_op jit(solution)/shard_map/ppermute | solution.py:227
  77.2 1.0 %fusion.1 = f32[2,320,256]{2,1,0:T(8,128)} fusion(f32[2,320,256]{2,1,0:T(8,128)S(1)} %copy-done, f32[2,320,128]{2,1,0:T(8,128)S(1)} %get-tuple-element.24, f32[2,320,128]{2,1,0:T(8,128)S(1)} %get-tuple-element.23, f32[2,320,256]{2,1,0:T(8,128)S(1)} %get-tuple-element.20, f32[2,320,256]{2,1,0:T(8,128)S(1)} %collective-permute-done.9, f32[320,256]{1,0:T(8,128)S(1)} %copy-done.6), kind=kLoop, calls=%fused_computation.2 | loop fusion | flops 819200 | bytes 3604480 | tf_op jit(solution)/shard_map/add | solution.py:302
  (11 shorter events, 0.1 us)
Async XLA Ops:
  0.0 43.5 %copy-start.1 = (f32[2,256,256]{2,1,0:T(8,128)S(1)}, f32[2,256,256]{2,1,0:T(8,128)}, u32[]{:S(2)}) copy-start(f32[2,256,256]{2,1,0:T(8,128)} %int_own.1) | copy-start | bytes 1572868
  0.0 43.5 %copy-start = (f32[2,320,256]{2,1,0:T(8,128)S(1)}, f32[2,320,256]{2,1,0:T(8,128)}, u32[]{:S(2)}) copy-start(f32[2,320,256]{2,1,0:T(8,128)} %obj.3) | copy-start | bytes 1966084
  2.3 41.2 %copy-start.5 = (f32[2,129]{1,0:T(2,128)S(1)}, f32[2,129]{1,0:T(2,128)}, u32[]{:S(2)}) copy-start(f32[2,129]{1,0:T(2,128)} %taps_ref.1) | copy-start | bytes 3100
  2.3 41.2 %copy-start.4 = (s32[192,2]{0,1:T(2,128)S(1)}, s32[192,2]{0,1:T(2,128)}, u32[]{:S(2)}) copy-start(s32[192,2]{0,1:T(2,128)} %param.6) | copy-start | bytes 4612
  2.3 34.9 %collective-permute-start.2 = (f32[1152,128]{1,0:T(8,128)}, f32[1152,128]{1,0:T(8,128)S(1)}, u32[]{:S(2)}, u32[]{:S(2)}) collective-permute-start(f32[1152,128]{1,0:T(8,128)} %get-tuple-element.14), channel_id=1, source_target_pairs={{8,0},{10,2},{12,4},{14,6},{16,8},{1,9},{18,10},{3,11},{20,12},{5,... | collective-permute-start | bytes 1769480 | tf_op jit(solution)/shard_map/ppermute | solution.py:236
  5.5 29.8 %collective-permute-start.4 = (f32[1,2,256,256]{3,2,1,0:T(8,128)}, f32[1,2,256,256]{3,2,1,0:T(8,128)S(1)}, u32[]{:S(2)}, u32[]{:S(2)}) collective-permute-start(f32[1,2,256,256]{3,2,1,0:T(8,128)} %rest_0_.1), channel_id=1, source_target_pairs={{0,4},{1,5},{2,6},{3,7},{4,0},{5,1},{6,2},{7,3},{8,12},{9,13},{10,... | collective-permute-start | bytes 1572872 | tf_op jit(solution)/shard_map/ppermute | solution.py:215
  10.2 27.0 %collective-permute-start = (f32[1,2,256,256]{3,2,1,0:T(8,128)}, f32[1,2,256,256]{3,2,1,0:T(8,128)S(1)}, u32[]{:S(2)}, u32[]{:S(2)}) collective-permute-start(f32[1,2,256,256]{3,2,1,0:T(8,128)} %rest_0_.1), channel_id=1, source_target_pairs={{0,2},{1,3},{2,4},{3,5},{4,6},{5,7},{6,0},{7,1},{8,10},{9,11},{10,... | collective-permute-start | bytes 1572872 | tf_op jit(solution)/shard_map/ppermute | solution.py:215
  12.4 24.8 %collective-permute-start.1 = (f32[1,2,256,256]{3,2,1,0:T(8,128)}, f32[1,2,256,256]{3,2,1,0:T(8,128)S(1)}, u32[]{:S(2)}, u32[]{:S(2)}) collective-permute-start(f32[1,2,256,256]{3,2,1,0:T(8,128)} %rest_0_.1), channel_id=1, source_target_pairs={{0,6},{1,7},{2,0},{3,1},{4,2},{5,3},{6,4},{7,5},{8,14},{9,15},{10,... | collective-permute-start | bytes 1572872 | tf_op jit(solution)/shard_map/ppermute | solution.py:215
  16.7 9.0 %collective-permute-start.3 = (f32[256,256]{1,0:T(8,128)}, f32[256,256]{1,0:T(8,128)S(1)}, u32[]{:S(2)}, u32[]{:S(2)}) collective-permute-start(f32[256,256]{1,0:T(8,128)} %get-tuple-element.15), channel_id=1, source_target_pairs={{9,1},{11,3},{13,5},{15,7},{0,8},{17,9},{2,10},{19,11},{4,12},{21,... | collective-permute-start | bytes 786440 | tf_op jit(solution)/shard_map/ppermute | solution.py:236
  25.7 15.9 %collective-permute-start.5 = (f32[1,2,256,256]{3,2,1,0:T(8,128)}, f32[1,2,256,256]{3,2,1,0:T(8,128)S(1)}, u32[]{:S(2)}, u32[]{:S(2)}) collective-permute-start(f32[1,2,256,256]{3,2,1,0:T(8,128)} %rest_0_.1), channel_id=1, source_target_pairs={{0,1},{1,0},{2,3},{3,2},{4,5},{5,4},{6,7},{7,6},{8,9},{9,8},{10,11... | collective-permute-start | bytes 1572872 | tf_op jit(solution)/shard_map/ppermute | solution.py:218
  35.3 6.3 %collective-permute-start.8 = (f32[1,2,256,256]{3,2,1,0:T(8,128)S(1)}, f32[1,2,256,256]{3,2,1,0:T(8,128)S(1)}, u32[]{:S(2)}, u32[]{:S(2)}) collective-permute-start(f32[1,2,256,256]{3,2,1,0:T(8,128)S(1)} %collective-permute-done.4.rest_3_), channel_id=1, source_target_pairs={{0,1},{1,0},{2,3},{3,2},{4,5},{5,4},{6,7},{7,6},{8,9},{9,8},{10,11... | collective-permute-start | bytes 1572872 | tf_op jit(solution)/shard_map/ppermute | solution.py:218
  37.2 4.4 %collective-permute-start.6 = (f32[1,2,256,256]{3,2,1,0:T(8,128)S(1)}, f32[1,2,256,256]{3,2,1,0:T(8,128)S(1)}, u32[]{:S(2)}, u32[]{:S(2)}) collective-permute-start(f32[1,2,256,256]{3,2,1,0:T(8,128)S(1)} %collective-permute-done.rest_1_), channel_id=1, source_target_pairs={{0,1},{1,0},{2,3},{3,2},{4,5},{5,4},{6,7},{7,6},{8,9},{9,8},{10,11... | collective-permute-start | bytes 1572872 | tf_op jit(solution)/shard_map/ppermute | solution.py:218
  39.7 3.8 %collective-permute-start.7 = (f32[1,2,256,256]{3,2,1,0:T(8,128)S(1)}, f32[1,2,256,256]{3,2,1,0:T(8,128)S(1)}, u32[]{:S(2)}, u32[]{:S(2)}) collective-permute-start(f32[1,2,256,256]{3,2,1,0:T(8,128)S(1)} %collective-permute-done.1.rest_2_), channel_id=1, source_target_pairs={{0,1},{1,0},{2,3},{3,2},{4,5},{5,4},{6,7},{7,6},{8,9},{9,8},{10,11... | collective-permute-start | bytes 1572872 | tf_op jit(solution)/shard_map/ppermute | solution.py:218
  43.5 1.0 %copy-start.2 = (f32[1,2,256,256]{3,2,1,0:T(8,128)S(1)}, f32[1,2,256,256]{3,2,1,0:T(8,128)}, u32[]{:S(2)}) copy-start(f32[1,2,256,256]{3,2,1,0:T(8,128)} %rest_0_.1) | copy-start | bytes 1572868
  58.9 0.7 copy-start.3
  59.6 17.6 %collective-permute-start.9 = (f32[2,320,256]{2,1,0:T(8,128)S(1)}, f32[2,320,256]{2,1,0:T(8,128)S(1)}, u32[]{:S(2)}, u32[]{:S(2)}) collective-permute-start(f32[2,320,256]{2,1,0:T(8,128)S(1)} %get-tuple-element.20), channel_id=1, source_target_pairs={{0,1},{1,0},{2,3},{3,2},{4,5},{5,4},{6,7},{7,6},{8,9},{9,8},{10,11... | collective-permute-start | bytes 1966088 | tf_op jit(solution)/shard_map/ppermute | solution.py:218
  61.7 13.2 %collective-permute-start.10 = (f32[2,320,128]{2,1,0:T(8,128)S(1)}, f32[2,320,128]{2,1,0:T(8,128)S(1)}, u32[]{:S(2)}, u32[]{:S(2)}) collective-permute-start(f32[2,320,128]{2,1,0:T(8,128)S(1)} %get-tuple-element.21), channel_id=1, source_target_pairs={{0,8},{2,10},{4,12},{6,14},{8,16},{9,1},{10,18},{11,3},{12,20},{13... | collective-permute-start | bytes 983048 | tf_op jit(solution)/shard_map/ppermute | solution.py:227
  63.6 13.6 %collective-permute-start.11 = (f32[2,320,128]{2,1,0:T(8,128)S(1)}, f32[2,320,128]{2,1,0:T(8,128)S(1)}, u32[]{:S(2)}, u32[]{:S(2)}) collective-permute-start(f32[2,320,128]{2,1,0:T(8,128)S(1)} %get-tuple-element.21), channel_id=1, source_target_pairs={{0,9},{2,11},{4,13},{6,15},{8,17},{9,0},{10,19},{11,2},{12,21},{13... | collective-permute-start | bytes 983048 | tf_op jit(solution)/shard_map/ppermute | solution.py:227
  74.8 2.4 %copy-start.6 = (f32[320,256]{1,0:T(8,128)S(1)}, f32[320,256]{1,0:T(8,128)}, u32[]{:S(2)}) copy-start(f32[320,256]{1,0:T(8,128)} %denominator.1) | copy-start | bytes 983044

commit v3 on v2

v3 whole, which is shorter than its diff:
```python
import functools

import jax
import jax.numpy as jnp
from jax import lax
from jax.experimental import pallas as pl
from jax.experimental.pallas import tpu as pltpu
from jax.sharding import PartitionSpec as P

P_SIZE = 256
BAND = 64
TW = 256
HALF = 128
OH = 320
MODES = 8
EXT = TW + HALF
TALL = P_SIZE + 8
GROUP = 2
HELD = MODES // 2
F32 = jnp.float32
BF16 = jnp.bfloat16


def place_of(tiles):
    return lax.axis_index("tile"), lax.rem(lax.axis_index("mode"), 2)


def slot_of(pos_ref, tile, core, tiles, shift):
    block = tile + shift
    inside = (block >= 0) & (block < tiles)
    pattern = 2 * jnp.clip(block, 0, tiles - 1) + core
    return inside, pos_ref[0, pattern], pos_ref[1, pattern]


def aligned(top_row):
    extra = lax.rem(top_row, 8)
    return pl.multiple_of(top_row - extra, 8), extra


def lowered(window, extra, width):
    tall = jnp.concatenate([window, jnp.zeros((TALL - P_SIZE, P_SIZE), F32)], axis=0)
    return jnp.concatenate([pltpu.roll(tall, extra, 0), jnp.zeros((TALL, width - P_SIZE), F32)], axis=1)


def pack_kernel(obj, inten, halo, chosen, sem):
    core = lax.rem(lax.axis_index("mode"), 2)
    edge = pl.ds(pl.multiple_of(core * HALF, HALF), HALF)
    run_copies([(obj.at[:, :, edge], halo), (inten.at[core], chosen)], sem)


def run_copies(moves, sem):
    copies = [pltpu.make_async_copy(src, dst, sem.at[i]) for i, (src, dst) in enumerate(moves)]
    for copy in copies:
        copy.start()
    for copy in copies:
        copy.wait()


def merge_kernel(own, first, second, third, merged, sem):
    arrays = (own, first, second, third)
    run_copies([(array.at[0], merged.at[2 * i : 2 * i + 2]) for i, array in enumerate(arrays)], sem)


def window_of(pos_ref, tiles, slot):
    tile, core = place_of(tiles)
    inside, top_row, column = slot_of(pos_ref, tile, core, tiles, (slot - 1) * (1 - 2 * core))
    offset = column - tile * TW - (1 - core) * HALF
    here = inside & (column >= tile * TW) & (column < (tile + 1) * TW)
    return here, top_row, offset


def mix(first, second, low, midb):
    mid = jnp.dot(first, low[...], preferred_element_type=F32)
    for unit in range(GROUP):
        own = slice(unit * P_SIZE, (unit + 1) * P_SIZE)
        midb[own, :P_SIZE] = mid[:P_SIZE, own].astype(BF16)
        midb[own, P_SIZE:] = mid[P_SIZE:, own].astype(BF16)
    return jnp.dot(midb[...], second, preferred_element_type=F32)


def forward(probe, patch_re, patch_im, stacks, low, midb, far, power):
    for start in range(0, HELD, GROUP):
        for unit in range(GROUP):
            own = slice(unit * P_SIZE, (unit + 1) * P_SIZE)
            pr = probe[2 * (start + unit)]
            pi = probe[2 * (start + unit) + 1]
            low[:P_SIZE, own] = (pr * patch_re[...] - pi * patch_im[...]).astype(BF16)
            low[P_SIZE:, own] = (pr * patch_im[...] + pi * patch_re[...]).astype(BF16)
        out = mix(stacks[0], stacks[1], low, midb)
        for unit in range(GROUP):
            block = out[unit * P_SIZE : (unit + 1) * P_SIZE]
            far[start + unit] = block
            term = block[:, :P_SIZE] * block[:, :P_SIZE] + block[:, P_SIZE:] * block[:, P_SIZE:]
            power[...] += term


def first_kernel(tiles, pos_ref, taps_ref, obj, halo, mine, far, patch, power, stacks, wave, low, midb, row_pad, sem):
    _, core = place_of(tiles)
    rim = pl.ds(pl.multiple_of((1 - core) * TW, HALF), HALF)
    moves = (
        (obj, wave.at[:, :OH, pl.ds(pl.multiple_of(core * HALF, HALF), TW)]),
        (halo, wave.at[:, :OH, rim]),
    )
    copies = [pltpu.make_async_copy(src, dst, sem.at[i]) for i, (src, dst) in enumerate(moves)]
    for copy in copies:
        copy.start()

    row_pad[...] = jnp.zeros_like(row_pad)
    row_pad[0:2, 0 : 2 * BAND + 1] = taps_ref[...]

    def band(part):
        line = jnp.broadcast_to(row_pad[part : part + 1, :], (P_SIZE, 2 * P_SIZE))
        turned = pltpu.roll(line, 2 * P_SIZE - BAND, 1, stride=1, stride_axis=0)
        return turned[:, :P_SIZE]

    band_re = band(0)
    band_im = band(1)
    turned_re = band_re.T
    turned_im = band_im.T
    for which, blocks in enumerate(((band_re, -band_im, band_im), (turned_re, turned_im, -turned_im))):
        stacks[which, :P_SIZE, :P_SIZE] = blocks[0].astype(BF16)
        stacks[which, :P_SIZE, P_SIZE:] = blocks[1].astype(BF16)
        stacks[which, P_SIZE:, :P_SIZE] = blocks[2].astype(BF16)
        stacks[which, P_SIZE:, P_SIZE:] = blocks[0].astype(BF16)

    for copy in copies:
        copy.wait()

    @pl.loop(0, 3)
    def _(slot):
        here, top_row, offset = window_of(pos_ref, tiles, slot)

        @pl.when(here)
        def _():
            base, extra = aligned(top_row)
            for part in range(2):
                rows = wave[part, pl.ds(base, TALL), :]
                turned = pltpu.roll(rows, lax.rem(EXT - offset, EXT), 1)[:, :P_SIZE]
                patch[slot, part] = pltpu.roll(turned, lax.rem(TALL - extra, TALL), 0)[:P_SIZE]
            power[slot] = jnp.zeros((P_SIZE, P_SIZE), F32)
            forward(mine, patch.at[slot, 0], patch.at[slot, 1], stacks, low, midb, far.at[slot], power.at[slot])


def second_kernel(
    tiles, pos_ref, inten, inward, outward, mine, theirs, far, patch, power, stacks, mid_out, rim_out, weight,
    total, meas, far_too, low, midb, ratio, acc,
):
    _, core = place_of(tiles)
    total[...] = jnp.zeros_like(total)
    meas[0] = outward[...]
    meas[1] = inten[core]
    meas[2] = inward[...]
    weight[...] = jnp.zeros_like(weight)

    @pl.loop(0, MODES)
    def _(plane):
        weight[...] += mine[plane] * mine[plane] + theirs[plane] * theirs[plane]

    @pl.loop(0, 3)
    def _(slot):
        here, top_row, offset = window_of(pos_ref, tiles, slot)

        @pl.when(here)
        def _():
            base, extra = aligned(top_row)
            ratio[...] = power[slot]
            forward(theirs, patch.at[slot, 0], patch.at[slot, 1], stacks, low, midb, far_too, ratio)
            ratio[...] = jnp.sqrt(meas[slot]) / jnp.sqrt(ratio[...] + 1.0)
            acc[0] = -weight[...] * patch[slot, 0]
            acc[1] = -weight[...] * patch[slot, 1]
            for source, probe in ((far.at[slot], mine), (far_too, theirs)):
                for start in range(0, HELD, GROUP):
                    for unit in range(GROUP):
                        own = slice(unit * P_SIZE, (unit + 1) * P_SIZE)
                        low[:P_SIZE, own] = (source[start + unit, :, :P_SIZE] * ratio[...]).astype(BF16)
                        low[P_SIZE:, own] = (source[start + unit, :, P_SIZE:] * ratio[...]).astype(BF16)
                    out = mix(stacks[1], stacks[0], low, midb)
                    term_re = 0.0
                    term_im = 0.0
                    for unit in range(GROUP):
                        back_re = out[unit * P_SIZE : (unit + 1) * P_SIZE, :P_SIZE]
                        back_im = out[unit * P_SIZE : (unit + 1) * P_SIZE, P_SIZE:]
                        pr = probe[2 * (start + unit)]
                        pi = probe[2 * (start + unit) + 1]
                        term_re += pr * back_re + pi * back_im
                        term_im += pr * back_im - pi * back_re
                    acc[0] += term_re
                    acc[1] += term_im

            for part in range(2):
                total[part, pl.ds(base, TALL), :] += pltpu.roll(lowered(acc[part], extra, EXT), offset, 1)

    mid_out[...] = total[:, :OH, pl.ds(pl.multiple_of(core * HALF, HALF), TW)]
    rim_out[...] = total[:, :OH, pl.ds(pl.multiple_of((1 - core) * TW, HALF), HALF)]


def denom_kernel(tiles, pos_ref, weight, scale, denom):
    tile, _ = place_of(tiles)
    denom[...] = jnp.zeros_like(denom)
    for parity, shifts in ((0, (-2, -1, 0, 1)), (1, (-1, 0, 1, 2))):
        for shift in shifts:
            inside, top_row, column = slot_of(pos_ref, tile, parity, tiles, shift)
            start = column - HALF - tile * TW

            @pl.when(inside & (start > -P_SIZE) & (start < TW))
            def _():
                base, extra = aligned(top_row)
                wide = lowered(weight[...], extra, 2 * P_SIZE)
                turned = pltpu.roll(wide, jnp.where(start < 0, start + 2 * P_SIZE, start), 1)
                denom[pl.ds(base, TALL), :] += turned[:, :TW]

    scale[...] = 1.0 / (denom[:OH] + 0.5)


ANY = pl.BlockSpec(memory_space=pl.ANY)
HBM = pl.BlockSpec(memory_space=pltpu.HBM)
VMEM = pl.BlockSpec(memory_space=pltpu.VMEM)
SMEM = pl.BlockSpec(memory_space=pltpu.SMEM)


def f32(*shape):
    return jax.ShapeDtypeStruct(shape, F32)


def limit(mib):
    return pltpu.CompilerParams(vmem_limit_bytes=mib * 2**20)


def cost(us):
    return pl.CostEstimate(flops=0, bytes_accessed=int(us * 3.5e6), transcendentals=0)


def local(intensity, positions, object_field, probe_modes, kernel_taps):
    tiles = lax.axis_size("tile")
    modes = lax.axis_size("mode")
    core = lax.rem(lax.axis_index("mode"), 2)
    spots = positions.T

    def along_x(array, steps):
        return lax.ppermute(array, "mode", [(i, (i + 2 * steps) % modes) for i in range(modes)])

    def swap(array):
        return lax.ppermute(array, "mode", [(i, i ^ 1) for i in range(modes)])

    def from_tile(array, step):
        pairs = []
        for tile in range(tiles):
            for mode in range(modes):
                source = tile + step if mode % 2 == 0 else tile - step
                if 0 <= source < tiles:
                    pairs.append((source * modes + mode, tile * modes + mode))
        return lax.ppermute(array, ("tile", "mode"), pairs)

    ring = [along_x(probe_modes, step) for step in (1, -1, 2)]
    halo, chosen = pl.pallas_call(
        pack_kernel,
        out_shape=(f32(2, OH, HALF), f32(P_SIZE, P_SIZE)),
        in_specs=[HBM, HBM],
        out_specs=(VMEM, VMEM),
        scratch_shapes=[pltpu.SemaphoreType.DMA((2,))],
        compiler_params=limit(4),
        cost_estimate=cost(2.2),
        name="pack",
    )(object_field, intensity)
    halo = from_tile(halo, 1)
    inward = from_tile(chosen, 1)
    outward = from_tile(chosen, -1)

    mine = pl.pallas_call(
        merge_kernel,
        out_shape=f32(MODES, P_SIZE, P_SIZE),
        in_specs=[ANY] * 4,
        out_specs=VMEM,
        scratch_shapes=[pltpu.SemaphoreType.DMA((4,))],
        compiler_params=limit(4),
        cost_estimate=cost(2.0),
        name="merge",
    )(probe_modes, *ring)
    mine, halo, inward, outward = lax.optimization_barrier((mine, halo, inward, outward))
    theirs = swap(mine)

    stages = [
        pltpu.VMEM((2 * P_SIZE, GROUP * P_SIZE), BF16),
        pltpu.VMEM((GROUP * P_SIZE, 2 * P_SIZE), BF16),
    ]
    far, patch, power, stacks = pl.pallas_call(
        functools.partial(first_kernel, tiles),
        out_shape=(
            f32(3, HELD, P_SIZE, 2 * P_SIZE),
            f32(3, 2, P_SIZE, P_SIZE),
            f32(3, P_SIZE, P_SIZE),
            jax.ShapeDtypeStruct((2, 2 * P_SIZE, 2 * P_SIZE), BF16),
        ),
        in_specs=[SMEM, VMEM, ANY, ANY, VMEM],
        out_specs=(VMEM,) * 4,
        scratch_shapes=[pltpu.VMEM((2, OH + 8, EXT), F32)]
        + stages
        + [pltpu.VMEM((8, 2 * P_SIZE), F32), pltpu.SemaphoreType.DMA((2,))],
        compiler_params=limit(20),
        cost_estimate=cost(6.0),
        name="far_of_own_modes",
    )(spots, kernel_taps, object_field, halo, mine)

    middle, rim, weight = pl.pallas_call(
        functools.partial(second_kernel, tiles),
        out_shape=(f32(2, OH, TW), f32(2, OH, HALF), f32(P_SIZE, P_SIZE)),
        in_specs=[SMEM] + [VMEM] * 9,
        out_specs=(VMEM,) * 3,
        scratch_shapes=[
            pltpu.VMEM((2, OH + 8, EXT), F32),
            pltpu.VMEM((3, P_SIZE, P_SIZE), F32),
            pltpu.VMEM((HELD, P_SIZE, 2 * P_SIZE), F32),
        ]
        + stages
        + [pltpu.VMEM((P_SIZE, P_SIZE), F32), pltpu.VMEM((2, P_SIZE, P_SIZE), F32)],
        compiler_params=limit(20),
        cost_estimate=cost(10.0),
        name="update_terms",
    )(spots, intensity, inward, outward, mine, theirs, far, patch, power, stacks)

    arrived = from_tile(rim, -1)
    scale = pl.pallas_call(
        functools.partial(denom_kernel, tiles),
        out_shape=f32(OH, TW),
        in_specs=[SMEM, VMEM],
        out_specs=VMEM,
        scratch_shapes=[pltpu.VMEM((OH + 8, TW), F32)],
        compiler_params=limit(4),
        cost_estimate=cost(3.5),
        name="denominator",
    )(spots, weight)
    blank = jnp.zeros_like(arrived)
    low = jnp.where(core == 0, arrived, blank)
    high = jnp.where(core == 0, blank, arrived)
    terms = (middle + jnp.concatenate([low, high], axis=2)) * scale
    return object_field + (terms + swap(terms))


def solution(mesh):
    return jax.shard_map(
        local,
        mesh=mesh,
        in_specs=(
            P("tile", None, None),
            P(),
            P(None, None, "tile"),
            P("mode", None, None, None),
            P(),
        ),
        out_specs=P(None, None, "tile"),
        check_vma=False,
    )
```

time: 78.8 us -> 70.8 us (0.90)
  the two profiles are of different devices: /device:TPU:513 before, /device:TPU:1 now
where the time goes in v3:
time: 70.8 us; the launch traced here: 70.2 us
  starting transfers between devices  36.4 us (51%)
  waiting for transfers between devices  25.4 us (36%)
  Pallas kernels  3.99 us (6%)
  local copies, waits for them, and re-layouts  3.19 us (5%)
  other arithmetic  1.1 us (2%)
    ppermute x4, waiting for transfers between devices, from_tile(): return lax.ppermute(array, ('tile', 'mode'), pairs)  16.8 us
    ppermute x2, starting transfers between devices, swap(): return lax.ppermute(array, 'mode', [(i, i ^ 1) for i in range(modes)])  16.5 us
    ppermute x3, starting transfers between devices, along_x(): lax.ppermute(array, 'mode', [(i, (i + 2 * steps) % modes) for i in range(...  10.8 us
    ppermute x4, starting transfers between devices, from_tile(): return lax.ppermute(array, ('tile', 'mode'), pairs)  9.14 us
    ppermute x2, waiting for transfers between devices, swap(): return lax.ppermute(array, 'mode', [(i, i ^ 1) for i in range(modes)])  4.39 us
    ppermute x3, waiting for transfers between devices, along_x(): lax.ppermute(array, 'mode', [(i, (i + 2 * steps) % modes) for i in range(...  4.13 us
    unnamed x14, local copies, waits for them, and re-layouts  3.19 us
    pallas_call x1, Pallas kernels, local(): pl.pallas_call(functools.partial(denom_kernel, tiles), out_shape=f32(OH,...  1.48 us
  transfers between devices with their start and end apart: 9, of which 5 were waited for; matrix products, arithmetic and copies ran while one was open for 0% of the time, Pallas kernels for 4%

profile of v3, /device:TPU:1, one launch (start us, length us, event | category | flops | bytes accessed | tf_op | source)
XLA Modules:
  0.0 70.2 jit_solution(4600158682414678021)
XLA Ops:
  0.0 3.9 %collective-permute-start = (f32[1,2,256,256]{3,2,1,0:T(8,128)}, f32[1,2,256,256]{3,2,1,0:T(8,128)S(1)}, u32[]{:S(2)}, u32[]{:S(2)}) collective-permute-start(f32[1,2,256,256]{3,2,1,0:T(8,128)} %own.1), channel_id=1, source_target_pairs={{0,2},{1,3},{2,4},{3,5},{4,6},{5,7},{6,0},{7,1},{8,10},{9,11},{10,... | collective-permute-start | bytes 1572872 | tf_op jit(solution)/shard_map/ppermute | solution.py:240
  3.9 3.2 %collective-permute-start.1 = (f32[1,2,256,256]{3,2,1,0:T(8,128)}, f32[1,2,256,256]{3,2,1,0:T(8,128)S(1)}, u32[]{:S(2)}, u32[]{:S(2)}) collective-permute-start(f32[1,2,256,256]{3,2,1,0:T(8,128)} %own.1), channel_id=1, source_target_pairs={{0,6},{1,7},{2,0},{3,1},{4,2},{5,3},{6,4},{7,5},{8,14},{9,15},{10,... | collective-permute-start | bytes 1572872 | tf_op jit(solution)/shard_map/ppermute | solution.py:240
  7.1 3.6 %collective-permute-start.2 = (f32[1,2,256,256]{3,2,1,0:T(8,128)}, f32[1,2,256,256]{3,2,1,0:T(8,128)S(1)}, u32[]{:S(2)}, u32[]{:S(2)}) collective-permute-start(f32[1,2,256,256]{3,2,1,0:T(8,128)} %own.1), channel_id=1, source_target_pairs={{0,4},{1,5},{2,6},{3,7},{4,0},{5,1},{6,2},{7,3},{8,12},{9,13},{10,... | collective-permute-start | bytes 1572872 | tf_op jit(solution)/shard_map/ppermute | solution.py:240
  10.8 0.0 copy-start
  10.8 1.1 %copy-done = f32[2,320,256]{2,1,0:T(8,128)S(1)} copy-done((f32[2,320,256]{2,1,0:T(8,128)S(1)}, f32[2,320,256]{2,1,0:T(8,128)}, u32[]{:S(2)}) %copy-start) | copy-done | bytes 655384
  11.9 1.0 %copy-done.2 = f32[2,256,256]{2,1,0:T(8,128)S(1)} copy-done((f32[2,256,256]{2,1,0:T(8,128)S(1)}, f32[2,256,256]{2,1,0:T(8,128)}, u32[]{:S(2)}) %copy-start.2) | copy-done | bytes 524312
  12.9 0.1 pack.1
  13.0 0.0 copy-start.5
  13.0 3.2 %collective-permute-start.3 = (f32[2,320,128]{2,1,0:T(8,128)S(1)}, f32[2,320,128]{2,1,0:T(8,128)S(1)}, u32[]{:S(2)}, u32[]{:S(2)}) collective-permute-start(f32[2,320,128]{2,1,0:T(8,128)S(1)} %get-tuple-element.18), channel_id=1, source_target_pairs={{8,0},{10,2},{12,4},{14,6},{16,8},{1,9},{18,10},{3,11},{20,12},{5,... | collective-permute-start | bytes 983048 | tf_op jit(solution)/shard_map/ppermute | solution.py:252
  16.2 0.0 copy-start.1
  16.2 3.3 %collective-permute-start.4 = (f32[256,256]{1,0:T(8,128)S(1)}, f32[256,256]{1,0:T(8,128)S(1)}, u32[]{:S(2)}, u32[]{:S(2)}) collective-permute-start(f32[256,256]{1,0:T(8,128)S(1)} %get-tuple-element.19), channel_id=1, source_target_pairs={{8,0},{10,2},{12,4},{14,6},{16,8},{1,9},{18,10},{3,11},{20,12},{5,... | collective-permute-start | bytes 786440 | tf_op jit(solution)/shard_map/ppermute | solution.py:252
  19.6 0.0 collective-permute-done.first
  19.6 1.3 %collective-permute-start.5 = (f32[256,256]{1,0:T(8,128)S(1)}, f32[256,256]{1,0:T(8,128)S(1)}, u32[]{:S(2)}, u32[]{:S(2)}) collective-permute-start(f32[256,256]{1,0:T(8,128)S(1)} %get-tuple-element.19), channel_id=1, source_target_pairs={{9,1},{11,3},{13,5},{15,7},{0,8},{17,9},{2,10},{19,11},{4,12},{21,... | collective-permute-start | bytes 786440 | tf_op jit(solution)/shard_map/ppermute | solution.py:252
  20.9 0.0 collective-permute-done.1.second
  20.9 4.1 %collective-permute-done.2.third = f32[1,2,256,256]{3,2,1,0:T(8,128)S(1)} collective-permute-done((f32[1,2,256,256]{3,2,1,0:T(8,128)}, f32[1,2,256,256]{3,2,1,0:T(8,128)S(1)}, u32[]{:S(2)}, u32[]{:S(2)}) %collective-permute-start.2) | collective-permute-done | bytes 524320 | tf_op jit(solution)/shard_map/ppermute | solution.py:240
  25.0 1.0 %copy-done.4 = f32[1,2,256,256]{3,2,1,0:T(8,128)S(1)} copy-done((f32[1,2,256,256]{3,2,1,0:T(8,128)S(1)}, f32[1,2,256,256]{3,2,1,0:T(8,128)}, u32[]{:S(2)}) %copy-start.4) | copy-done | bytes 524312
  26.1 0.2 merge.1.mine
  26.3 0.0 copy-start.3
  26.3 0.0 collective-permute-done.4.inward
  26.3 0.9 %collective-permute-done.5.outward = f32[256,256]{1,0:T(8,128)S(1)} collective-permute-done((f32[256,256]{1,0:T(8,128)S(1)}, f32[256,256]{1,0:T(8,128)S(1)}, u32[]{:S(2)}, u32[]{:S(2)}) %collective-permute-start.5) | collective-permute-done | bytes 262176 | tf_op jit(solution)/shard_map/ppermute | solution.py:252
  27.1 0.0 collective-permute-done.3.halo
  27.2 14.1 %collective-permute-start.6 = (f32[8,256,256]{2,1,0:T(8,128)S(1)}, f32[8,256,256]{2,1,0:T(8,128)S(1)}, u32[]{:S(2)}, u32[]{:S(2)}) collective-permute-start(f32[8,256,256]{2,1,0:T(8,128)S(1)} %merge.1.mine), channel_id=1, source_target_pairs={{0,1},{1,0},{2,3},{3,2},{4,5},{5,4},{6,7},{7,6},{8,9},{9,8},{10,11... | collective-permute-start | bytes 6291464 | tf_op jit(solution)/shard_map/ppermute | solution.py:243
  41.3 1.0 %far_of_own_modes.1 = (f32[3,4,256,512]{3,2,1,0:T(8,128)S(1)}, f32[3,2,256,256]{3,2,1,0:T(8,128)S(1)}, f32[3,256,256]{2,1,0:T(8,128)S(1)}, bf16[2,512,512]{2,1,0:T(8,128)(2,1)S(1)}) custom-call(s32[2,192]{1,0:T(2,128)S(1)} %bitcast.1, f32[2,129]{1,0:T(2,128)S(1)} %copy-done.6, f32[2,320,256]{2,1,0:T(8,128)S(1)} %copy-done.1, ...), custom_call_target="tpu_custom_call" | custom-call | bytes 21000000 | tf_op jit(solution)/shard_map/far_of_own_modes/pallas_call | solution.py:286
  42.4 2.7 %collective-permute-done.6.theirs = f32[8,256,256]{2,1,0:T(8,128)S(1)} collective-permute-done((f32[8,256,256]{2,1,0:T(8,128)S(1)}, f32[8,256,256]{2,1,0:T(8,128)S(1)}, u32[]{:S(2)}, u32[]{:S(2)}) %collective-permute-start.6) | collective-permute-done | bytes 2097184 | tf_op jit(solution)/shard_map/ppermute | solution.py:243
  45.1 1.2 %update_terms.1 = (f32[2,320,256]{2,1,0:T(8,128)S(1)}, f32[2,320,128]{2,1,0:T(8,128)S(1)}, f32[256,256]{1,0:T(8,128)S(1)}) custom-call(s32[2,192]{1,0:T(2,128)S(1)} %bitcast.2, f32[2,256,256]{2,1,0:T(8,128)S(1)} %copy-done.3, f32[256,256]{1,0:T(8,128)S(1)} %collective-permute-done.4.inward, f32[256,256]{1,0:T(8,128)S(1)} %collective-permute-done.5.outward, ...), custom_call_target="tpu_custom_call" | custom-call | bytes 35000000 | tf_op jit(solution)/shard_map/update_terms/pallas_call | solution.py:304
  46.3 1.3 %collective-permute-start.7 = (f32[2,320,128]{2,1,0:T(8,128)S(1)}, f32[2,320,128]{2,1,0:T(8,128)S(1)}, u32[]{:S(2)}, u32[]{:S(2)}) collective-permute-start(f32[2,320,128]{2,1,0:T(8,128)S(1)} %get-tuple-element.29), channel_id=1, source_target_pairs={{9,1},{11,3},{13,5},{15,7},{0,8},{17,9},{2,10},{19,11},{4,12},{21,... | collective-permute-start | bytes 983048 | tf_op jit(solution)/shard_map/ppermute | solution.py:252
  47.6 1.5 %denominator.1 = f32[320,256]{1,0:T(8,128)S(1)} custom-call(s32[2,192]{1,0:T(2,128)S(1)} %bitcast.3, f32[256,256]{1,0:T(8,128)S(1)} %get-tuple-element.30.weight), custom_call_target="tpu_custom_call" | custom-call | bytes 12250000 | tf_op jit(solution)/shard_map/denominator/pallas_call | solution.py:322
  49.1 16.0 %collective-permute-done.7 = f32[2,320,128]{2,1,0:T(8,128)S(1)} collective-permute-done((f32[2,320,128]{2,1,0:T(8,128)S(1)}, f32[2,320,128]{2,1,0:T(8,128)S(1)}, u32[]{:S(2)}, u32[]{:S(2)}) %collective-permute-start.7) | collective-permute-done | bytes 327712 | tf_op jit(solution)/shard_map/ppermute | solution.py:252
  65.1 0.1 fusion
  65.2 2.3 %collective-permute-start.8 = (f32[2,320,256]{2,1,0:T(8,128)S(1)}, f32[2,320,256]{2,1,0:T(8,128)S(1)}, u32[]{:S(2)}, u32[]{:S(2)}) collective-permute-start(f32[2,320,256]{2,1,0:T(8,128)S(1)} %fusion), channel_id=1, source_target_pairs={{0,1},{1,0},{2,3},{3,2},{4,5},{5,4},{6,7},{7,6},{8,9},{9,8},{10,11... | collective-permute-start | bytes 1966088 | tf_op jit(solution)/shard_map/ppermute | solution.py:243
  67.5 1.7 %collective-permute-done.8 = f32[2,320,256]{2,1,0:T(8,128)S(1)} collective-permute-done((f32[2,320,256]{2,1,0:T(8,128)S(1)}, f32[2,320,256]{2,1,0:T(8,128)S(1)}, u32[]{:S(2)}, u32[]{:S(2)}) %collective-permute-start.8) | collective-permute-done | bytes 655392 | tf_op jit(solution)/shard_map/ppermute | solution.py:243
  69.2 1.0 %add_add_fusion = f32[2,320,256]{2,1,0:T(8,128)} fusion(f32[2,320,256]{2,1,0:T(8,128)S(1)} %copy-done.1, f32[2,320,256]{2,1,0:T(8,128)S(1)} %fusion, f32[2,320,256]{2,1,0:T(8,128)S(1)} %collective-permute-done.8), kind=kLoop, calls=%fused_computation.2 | loop fusion | flops 327680 | bytes 2621440 | tf_op jit(solution)/shard_map/add | solution.py:336
  (8 shorter events, 0.1 us)
Async XLA Ops:
  0.0 19.6 %collective-permute-start = (f32[1,2,256,256]{3,2,1,0:T(8,128)}, f32[1,2,256,256]{3,2,1,0:T(8,128)S(1)}, u32[]{:S(2)}, u32[]{:S(2)}) collective-permute-start(f32[1,2,256,256]{3,2,1,0:T(8,128)} %own.1), channel_id=1, source_target_pairs={{0,2},{1,3},{2,4},{3,5},{4,6},{5,7},{6,0},{7,1},{8,10},{9,11},{10,... | collective-permute-start | bytes 1572872 | tf_op jit(solution)/shard_map/ppermute | solution.py:240
  3.9 16.9 %collective-permute-start.1 = (f32[1,2,256,256]{3,2,1,0:T(8,128)}, f32[1,2,256,256]{3,2,1,0:T(8,128)S(1)}, u32[]{:S(2)}, u32[]{:S(2)}) collective-permute-start(f32[1,2,256,256]{3,2,1,0:T(8,128)} %own.1), channel_id=1, source_target_pairs={{0,6},{1,7},{2,0},{3,1},{4,2},{5,3},{6,4},{7,5},{8,14},{9,15},{10,... | collective-permute-start | bytes 1572872 | tf_op jit(solution)/shard_map/ppermute | solution.py:240
  7.1 17.9 %collective-permute-start.2 = (f32[1,2,256,256]{3,2,1,0:T(8,128)}, f32[1,2,256,256]{3,2,1,0:T(8,128)S(1)}, u32[]{:S(2)}, u32[]{:S(2)}) collective-permute-start(f32[1,2,256,256]{3,2,1,0:T(8,128)} %own.1), channel_id=1, source_target_pairs={{0,4},{1,5},{2,6},{3,7},{4,0},{5,1},{6,2},{7,3},{8,12},{9,13},{10,... | collective-permute-start | bytes 1572872 | tf_op jit(solution)/shard_map/ppermute | solution.py:240
  10.8 1.1 %copy-start = (f32[2,320,256]{2,1,0:T(8,128)S(1)}, f32[2,320,256]{2,1,0:T(8,128)}, u32[]{:S(2)}) copy-start(f32[2,320,256]{2,1,0:T(8,128)} %obj.3) | copy-start | bytes 1966084
  11.9 1.0 %copy-start.2 = (f32[2,256,256]{2,1,0:T(8,128)S(1)}, f32[2,256,256]{2,1,0:T(8,128)}, u32[]{:S(2)}) copy-start(f32[2,256,256]{2,1,0:T(8,128)} %inten.3) | copy-start | bytes 1572868
  12.9 28.4 %copy-start.6 = (f32[2,129]{1,0:T(2,128)S(1)}, f32[2,129]{1,0:T(2,128)}, u32[]{:S(2)}) copy-start(f32[2,129]{1,0:T(2,128)} %taps_ref.1) | copy-start | bytes 3100
  13.0 28.3 %copy-start.5 = (s32[192,2]{0,1:T(2,128)S(1)}, s32[192,2]{0,1:T(2,128)}, u32[]{:S(2)}) copy-start(s32[192,2]{0,1:T(2,128)} %param.6) | copy-start | bytes 4612
  13.0 14.2 %collective-permute-start.3 = (f32[2,320,128]{2,1,0:T(8,128)S(1)}, f32[2,320,128]{2,1,0:T(8,128)S(1)}, u32[]{:S(2)}, u32[]{:S(2)}) collective-permute-start(f32[2,320,128]{2,1,0:T(8,128)S(1)} %get-tuple-element.18), channel_id=1, source_target_pairs={{8,0},{10,2},{12,4},{14,6},{16,8},{1,9},{18,10},{3,11},{20,12},{5,... | collective-permute-start | bytes 983048 | tf_op jit(solution)/shard_map/ppermute | solution.py:252
  16.2 25.1 %copy-start.1 = (f32[2,320,256]{2,1,0:T(8,128)S(1)}, f32[2,320,256]{2,1,0:T(8,128)}, u32[]{:S(2)}) copy-start(f32[2,320,256]{2,1,0:T(8,128)} %obj.3) | copy-start | bytes 1966084
  16.2 10.0 %collective-permute-start.4 = (f32[256,256]{1,0:T(8,128)S(1)}, f32[256,256]{1,0:T(8,128)S(1)}, u32[]{:S(2)}, u32[]{:S(2)}) collective-permute-start(f32[256,256]{1,0:T(8,128)S(1)} %get-tuple-element.19), channel_id=1, source_target_pairs={{8,0},{10,2},{12,4},{14,6},{16,8},{1,9},{18,10},{3,11},{20,12},{5,... | collective-permute-start | bytes 786440 | tf_op jit(solution)/shard_map/ppermute | solution.py:252
  19.6 7.6 %collective-permute-start.5 = (f32[256,256]{1,0:T(8,128)S(1)}, f32[256,256]{1,0:T(8,128)S(1)}, u32[]{:S(2)}, u32[]{:S(2)}) collective-permute-start(f32[256,256]{1,0:T(8,128)S(1)} %get-tuple-element.19), channel_id=1, source_target_pairs={{9,1},{11,3},{13,5},{15,7},{0,8},{17,9},{2,10},{19,11},{4,12},{21,... | collective-permute-start | bytes 786440 | tf_op jit(solution)/shard_map/ppermute | solution.py:252
  25.0 1.0 %copy-start.4 = (f32[1,2,256,256]{3,2,1,0:T(8,128)S(1)}, f32[1,2,256,256]{3,2,1,0:T(8,128)}, u32[]{:S(2)}) copy-start(f32[1,2,256,256]{3,2,1,0:T(8,128)} %own.1) | copy-start | bytes 1572868
  26.3 18.8 %copy-start.3 = (f32[2,256,256]{2,1,0:T(8,128)S(1)}, f32[2,256,256]{2,1,0:T(8,128)}, u32[]{:S(2)}) copy-start(f32[2,256,256]{2,1,0:T(8,128)} %inten.3) | copy-start | bytes 1572868
  27.2 17.9 %collective-permute-start.6 = (f32[8,256,256]{2,1,0:T(8,128)S(1)}, f32[8,256,256]{2,1,0:T(8,128)S(1)}, u32[]{:S(2)}, u32[]{:S(2)}) collective-permute-start(f32[8,256,256]{2,1,0:T(8,128)S(1)} %merge.1.mine), channel_id=1, source_target_pairs={{0,1},{1,0},{2,3},{3,2},{4,5},{5,4},{6,7},{7,6},{8,9},{9,8},{10,11... | collective-permute-start | bytes 6291464 | tf_op jit(solution)/shard_map/ppermute | solution.py:243
  46.3 18.8 %collective-permute-start.7 = (f32[2,320,128]{2,1,0:T(8,128)S(1)}, f32[2,320,128]{2,1,0:T(8,128)S(1)}, u32[]{:S(2)}, u32[]{:S(2)}) collective-permute-start(f32[2,320,128]{2,1,0:T(8,128)S(1)} %get-tuple-element.29), channel_id=1, source_target_pairs={{9,1},{11,3},{13,5},{15,7},{0,8},{17,9},{2,10},{19,11},{4,12},{21,... | collective-permute-start | bytes 983048 | tf_op jit(solution)/shard_map/ppermute | solution.py:252
  65.2 4.0 %collective-permute-start.8 = (f32[2,320,256]{2,1,0:T(8,128)S(1)}, f32[2,320,256]{2,1,0:T(8,128)S(1)}, u32[]{:S(2)}, u32[]{:S(2)}) collective-permute-start(f32[2,320,256]{2,1,0:T(8,128)S(1)} %fusion), channel_id=1, source_target_pairs={{0,1},{1,0},{2,3},{3,2},{4,5},{5,4},{6,7},{7,6},{8,9},{9,8},{10,11... | collective-permute-start | bytes 1966088 | tf_op jit(solution)/shard_map/ppermute | solution.py:243

commit v4 on v3

--- a/solution.py
+++ b/solution.py
@@ -42,12 +42,6 @@
     return jnp.concatenate([pltpu.roll(tall, extra, 0), jnp.zeros((TALL, width - P_SIZE), F32)], axis=1)
 
 
-def pack_kernel(obj, inten, halo, chosen, sem):
-    core = lax.rem(lax.axis_index("mode"), 2)
-    edge = pl.ds(pl.multiple_of(core * HALF, HALF), HALF)
-    run_copies([(obj.at[:, :, edge], halo), (inten.at[core], chosen)], sem)
-
-
 def run_copies(moves, sem):
     copies = [pltpu.make_async_copy(src, dst, sem.at[i]) for i, (src, dst) in enumerate(moves)]
     for copy in copies:
@@ -56,9 +50,18 @@
         copy.wait()
 
 
-def merge_kernel(own, first, second, third, merged, sem):
-    arrays = (own, first, second, third)
-    run_copies([(array.at[0], merged.at[2 * i : 2 * i + 2]) for i, array in enumerate(arrays)], sem)
+def pack_kernel(obj, own, halo, merged, sem):
+    core = lax.rem(lax.axis_index("mode"), 2)
+    edge = pl.ds(pl.multiple_of(core * HALF, HALF), HALF)
+    run_copies([(obj.at[:, :, edge], halo), (own.at[0], merged.at[0:2])], sem)
+
+
+def merge_kernel(before, first, second, third, inward, merged, sem):
+    del before
+    core = lax.rem(lax.axis_index("mode"), 2)
+    moves = [(array.at[0], merged.at[2 * i + 2 : 2 * i + 4]) for i, array in enumerate((first, second, third))]
+    moves.append((inward.at[1 - core], merged.at[MODES]))
+    run_copies(moves, sem)
 
 
 def window_of(pos_ref, tiles, slot):
@@ -69,32 +72,35 @@
     return here, top_row, offset
 
 
-def mix(first, second, low, midb):
-    mid = jnp.dot(first, low[...], preferred_element_type=F32)
-    for unit in range(GROUP):
-        own = slice(unit * P_SIZE, (unit + 1) * P_SIZE)
+def columns_of(unit):
+    return slice(unit * P_SIZE, (unit + 1) * P_SIZE)
+
+
+def mix(first, second, low, midb, units):
+    width = units * P_SIZE
+    mid = jnp.dot(first, low[:, :width], preferred_element_type=F32)
+    for unit in range(units):
+        own = columns_of(unit)
         midb[own, :P_SIZE] = mid[:P_SIZE, own].astype(BF16)
         midb[own, P_SIZE:] = mid[P_SIZE:, own].astype(BF16)
-    return jnp.dot(midb[...], second, preferred_element_type=F32)
-
-
-def forward(probe, patch_re, patch_im, stacks, low, midb, far, power):
-    for start in range(0, HELD, GROUP):
-        for unit in range(GROUP):
-            own = slice(unit * P_SIZE, (unit + 1) * P_SIZE)
-            pr = probe[2 * (start + unit)]
-            pi = probe[2 * (start + unit) + 1]
-            low[:P_SIZE, own] = (pr * patch_re[...] - pi * patch_im[...]).astype(BF16)
-            low[P_SIZE:, own] = (pr * patch_im[...] + pi * patch_re[...]).astype(BF16)
-        out = mix(stacks[0], stacks[1], low, midb)
-        for unit in range(GROUP):
-            block = out[unit * P_SIZE : (unit + 1) * P_SIZE]
-            far[start + unit] = block
-            term = block[:, :P_SIZE] * block[:, :P_SIZE] + block[:, P_SIZE:] * block[:, P_SIZE:]
-            power[...] += term
-
-
-def first_kernel(tiles, pos_ref, taps_ref, obj, halo, mine, far, patch, power, stacks, wave, low, midb, row_pad, sem):
+    return jnp.dot(midb[:width], second, preferred_element_type=F32)
+
+
+def forward(probe, modes, patch_re, patch_im, stacks, low, midb, far, power):
+    for unit, mode in enumerate(modes):
+        own = columns_of(unit)
+        pr = probe[2 * mode]
+        pi = probe[2 * mode + 1]
+        low[:P_SIZE, own] = (pr * patch_re[...] - pi * patch_im[...]).astype(BF16)
+        low[P_SIZE:, own] = (pr * patch_im[...] + pi * patch_re[...]).astype(BF16)
+    out = mix(stacks[0], stacks[1], low, midb, len(modes))
+    for unit in range(len(modes)):
+        block = out[columns_of(unit)]
+        far[unit] = block
+        power[...] += block[:, :P_SIZE] * block[:, :P_SIZE] + block[:, P_SIZE:] * block[:, P_SIZE:]
+
+
+def window_kernel(tiles, pos_ref, taps_ref, obj, halo, own, patch, stacks, far, power, wave, low, midb, row_pad, sem):
     _, core = place_of(tiles)
     rim = pl.ds(pl.multiple_of((1 - core) * TW, HALF), HALF)
     moves = (
@@ -138,18 +144,30 @@
                 turned = pltpu.roll(rows, lax.rem(EXT - offset, EXT), 1)[:, :P_SIZE]
                 patch[slot, part] = pltpu.roll(turned, lax.rem(TALL - extra, TALL), 0)[:P_SIZE]
             power[slot] = jnp.zeros((P_SIZE, P_SIZE), F32)
-            forward(mine, patch.at[slot, 0], patch.at[slot, 1], stacks, low, midb, far.at[slot], power.at[slot])
+            forward(own.at[0], (0,), patch.at[slot, 0], patch.at[slot, 1], stacks, low, midb, far.at[slot], power.at[slot])
+
+
+def first_kernel(tiles, pos_ref, mine, patch, stacks, before, far, power, low, midb):
+    @pl.loop(0, 3)
+    def _(slot):
+        here, _, _ = window_of(pos_ref, tiles, slot)
+
+        @pl.when(here)
+        def _():
+            power[slot] = before[slot]
+            sides = (patch.at[slot, 0], patch.at[slot, 1])
+            forward(mine, (1, 2, 3), *sides, stacks, low, midb, far.at[slot], power.at[slot])
 
 
 def second_kernel(
-    tiles, pos_ref, inten, inward, outward, mine, theirs, far, patch, power, stacks, mid_out, rim_out, weight,
+    tiles, pos_ref, inten, inward, mine, theirs, far_own, far_ring, patch, power, stacks, mid_out, rim_out, weight,
     total, meas, far_too, low, midb, ratio, acc,
 ):
     _, core = place_of(tiles)
     total[...] = jnp.zeros_like(total)
-    meas[0] = outward[...]
+    meas[0] = theirs[MODES]
     meas[1] = inten[core]
-    meas[2] = inward[...]
+    meas[2] = inward[core]
     weight[...] = jnp.zeros_like(weight)
 
     @pl.loop(0, MODES)
@@ -164,28 +182,33 @@
         def _():
             base, extra = aligned(top_row)
             ratio[...] = power[slot]
-            forward(theirs, patch.at[slot, 0], patch.at[slot, 1], stacks, low, midb, far_too, ratio)
+            sides = (patch.at[slot, 0], patch.at[slot, 1])
+            forward(theirs, (0, 1), *sides, stacks, low, midb, far_too.at[0:2], ratio)
+            forward(theirs, (2, 3), *sides, stacks, low, midb, far_too.at[2:4], ratio)
             ratio[...] = jnp.sqrt(meas[slot]) / jnp.sqrt(ratio[...] + 1.0)
             acc[0] = -weight[...] * patch[slot, 0]
             acc[1] = -weight[...] * patch[slot, 1]
-            for source, probe in ((far.at[slot], mine), (far_too, theirs)):
-                for start in range(0, HELD, GROUP):
-                    for unit in range(GROUP):
-                        own = slice(unit * P_SIZE, (unit + 1) * P_SIZE)
-                        low[:P_SIZE, own] = (source[start + unit, :, :P_SIZE] * ratio[...]).astype(BF16)
-                        low[P_SIZE:, own] = (source[start + unit, :, P_SIZE:] * ratio[...]).astype(BF16)
-                    out = mix(stacks[1], stacks[0], low, midb)
-                    term_re = 0.0
-                    term_im = 0.0
-                    for unit in range(GROUP):
-                        back_re = out[unit * P_SIZE : (unit + 1) * P_SIZE, :P_SIZE]
-                        back_im = out[unit * P_SIZE : (unit + 1) * P_SIZE, P_SIZE:]
-                        pr = probe[2 * (start + unit)]
-                        pi = probe[2 * (start + unit) + 1]
-                        term_re += pr * back_re + pi * back_im
-                        term_im += pr * back_im - pi * back_re
-                    acc[0] += term_re
-                    acc[1] += term_im
+            fields = [(far_own.at[slot, 0], mine, 0)]
+            fields += [(far_ring.at[slot, i], mine, i + 1) for i in range(3)]
+            fields += [(far_too.at[i], theirs, i) for i in range(HELD)]
+            for start in range(0, MODES, GROUP):
+                group = fields[start : start + GROUP]
+                for unit, (source, _, _) in enumerate(group):
+                    own = columns_of(unit)
+                    low[:P_SIZE, own] = (source[:, :P_SIZE] * ratio[...]).astype(BF16)
+                    low[P_SIZE:, own] = (source[:, P_SIZE:] * ratio[...]).astype(BF16)
+                out = mix(stacks[1], stacks[0], low, midb, GROUP)
+                term_re = 0.0
+                term_im = 0.0
+                for unit, (_, probe, mode) in enumerate(group):
+                    back_re = out[columns_of(unit), :P_SIZE]
+                    back_im = out[columns_of(unit), P_SIZE:]
+                    pr = probe[2 * mode]
+                    pi = probe[2 * mode + 1]
+                    term_re += pr * back_re + pi * back_im
+                    term_im += pr * back_im - pi * back_re
+                acc[0] += term_re
+                acc[1] += term_im
 
             for part in range(2):
                 total[part, pl.ds(base, TALL), :] += pltpu.roll(lowered(acc[part], extra, EXT), offset, 1)
@@ -252,54 +275,67 @@
         return lax.ppermute(array, ("tile", "mode"), pairs)
 
     ring = [along_x(probe_modes, step) for step in (1, -1, 2)]
-    halo, chosen = pl.pallas_call(
+    halo, held = pl.pallas_call(
         pack_kernel,
-        out_shape=(f32(2, OH, HALF), f32(P_SIZE, P_SIZE)),
-        in_specs=[HBM, HBM],
+        out_shape=(f32(2, OH, HALF), f32(MODES + 1, P_SIZE, P_SIZE)),
+        in_specs=[ANY, ANY],
         out_specs=(VMEM, VMEM),
         scratch_shapes=[pltpu.SemaphoreType.DMA((2,))],
         compiler_params=limit(4),
         cost_estimate=cost(2.2),
         name="pack",
-    )(object_field, intensity)
+    )(object_field, probe_modes)
     halo = from_tile(halo, 1)
-    inward = from_tile(chosen, 1)
-    outward = from_tile(chosen, -1)
-
-    mine = pl.pallas_call(
-        merge_kernel,
-        out_shape=f32(MODES, P_SIZE, P_SIZE),
-        in_specs=[ANY] * 4,
-        out_specs=VMEM,
-        scratch_shapes=[pltpu.SemaphoreType.DMA((4,))],
-        compiler_params=limit(4),
-        cost_estimate=cost(2.0),
-        name="merge",
-    )(probe_modes, *ring)
-    mine, halo, inward, outward = lax.optimization_barrier((mine, halo, inward, outward))
-    theirs = swap(mine)
-
-    stages = [
-        pltpu.VMEM((2 * P_SIZE, GROUP * P_SIZE), BF16),
-        pltpu.VMEM((GROUP * P_SIZE, 2 * P_SIZE), BF16),
-    ]
-    far, patch, power, stacks = pl.pallas_call(
-        functools.partial(first_kernel, tiles),
+    inward = from_tile(intensity, 1)
+
+    def stages(units):
+        return [
+            pltpu.VMEM((2 * P_SIZE, units * P_SIZE), BF16),
+            pltpu.VMEM((units * P_SIZE, 2 * P_SIZE), BF16),
+        ]
+
+    patch, stacks, far_own, power = pl.pallas_call(
+        functools.partial(window_kernel, tiles),
         out_shape=(
-            f32(3, HELD, P_SIZE, 2 * P_SIZE),
             f32(3, 2, P_SIZE, P_SIZE),
+            jax.ShapeDtypeStruct((2, 2 * P_SIZE, 2 * P_SIZE), BF16),
+            f32(3, 1, P_SIZE, 2 * P_SIZE),
             f32(3, P_SIZE, P_SIZE),
-            jax.ShapeDtypeStruct((2, 2 * P_SIZE, 2 * P_SIZE), BF16),
         ),
         in_specs=[SMEM, VMEM, ANY, ANY, VMEM],
         out_specs=(VMEM,) * 4,
         scratch_shapes=[pltpu.VMEM((2, OH + 8, EXT), F32)]
-        + stages
+        + stages(1)
         + [pltpu.VMEM((8, 2 * P_SIZE), F32), pltpu.SemaphoreType.DMA((2,))],
-        compiler_params=limit(20),
-        cost_estimate=cost(6.0),
+        compiler_params=limit(16),
+        cost_estimate=cost(4.0),
+        name="windows",
+    )(spots, kernel_taps, object_field, halo, probe_modes)
+
+    mine = pl.pallas_call(
+        merge_kernel,
+        out_shape=f32(MODES + 1, P_SIZE, P_SIZE),
+        in_specs=[ANY] * 5,
+        out_specs=ANY,
+        scratch_shapes=[pltpu.SemaphoreType.DMA((4,))],
+        input_output_aliases={0: 0},
+        compiler_params=limit(4),
+        cost_estimate=cost(1.0),
+        name="merge",
+    )(held, *ring, inward)
+    mine, patch, stacks, far_own, power = lax.optimization_barrier((mine, patch, stacks, far_own, power))
+    theirs = swap(mine)
+
+    far_ring, power = pl.pallas_call(
+        functools.partial(first_kernel, tiles),
+        out_shape=(f32(3, 3, P_SIZE, 2 * P_SIZE), f32(3, P_SIZE, P_SIZE)),
+        in_specs=[SMEM] + [VMEM] * 4,
+        out_specs=(VMEM,) * 2,
+        scratch_shapes=stages(3),
+        compiler_params=limit(16),
+        cost_estimate=cost(4.0),
         name="far_of_own_modes",
-    )(spots, kernel_taps, object_field, halo, mine)
+    )(spots, mine, patch, stacks, power)
 
     middle, rim, weight = pl.pallas_call(
         functools.partial(second_kernel, tiles),
@@ -311,12 +347,12 @@
             pltpu.VMEM((3, P_SIZE, P_SIZE), F32),
             pltpu.VMEM((HELD, P_SIZE, 2 * P_SIZE), F32),
         ]
-        + stages
+        + stages(GROUP)
         + [pltpu.VMEM((P_SIZE, P_SIZE), F32), pltpu.VMEM((2, P_SIZE, P_SIZE), F32)],
         compiler_params=limit(20),
         cost_estimate=cost(10.0),
         name="update_terms",
-    )(spots, intensity, inward, outward, mine, theirs, far, patch, power, stacks)
+    )(spots, intensity, inward, mine, theirs, far_own, far_ring, patch, power, stacks)
 
     arrived = from_tile(rim, -1)
     scale = pl.pallas_call(

time: 70.8 us -> 71.1 us (level)
  starting transfers between devices: 36.4 us -> 33.1 us
  local copies, waits for them, and re-layouts: 3.19 us -> 5.63 us
  Pallas kernels: 3.99 us -> 4.73 us
    ppermute x3, waiting for transfers between devices: 4.13 us -> 0.58 us  [along_x(): lax.ppermute(array, 'mode', [(i, (i + 2 * steps) % modes) for i in range(...]
    ppermute x4 -> x3, waiting for transfers between devices: 16.8 us -> 19.5 us  [from_tile(): return lax.ppermute(array, ('tile', 'mode'), pairs)]
    unnamed x14 -> x18, local copies, waits for them, and re-layouts: 3.19 us -> 5.63 us
    ppermute x2, starting transfers between devices: 16.5 us -> 14.5 us  [swap(): return lax.ppermute(array, 'mode', [(i, i ^ 1) for i in range(modes)])]
    pallas_call x2 -> x3, Pallas kernels: 0.24 us -> 1.28 us  [the longest x1 1.04 us: local(): pl.pallas_call(functools.partial(window_kernel, tiles), out_shape=(f32(3,...]
    ppermute x3, starting transfers between devices: 10.8 us -> 9.94 us  [along_x(): lax.ppermute(array, 'mode', [(i, (i + 2 * steps) % modes) for i in range(...]
    ppermute x2, waiting for transfers between devices: 4.39 us -> 5.16 us  [swap(): return lax.ppermute(array, 'mode', [(i, i ^ 1) for i in range(modes)])]
    ppermute x4 -> x3, starting transfers between devices: 9.14 us -> 8.7 us  [from_tile(): return lax.ppermute(array, ('tile', 'mode'), pairs)]
  transfers between devices with their start and end apart: 9 -> 8, of which waited for: 5 -> 5; matrix products, arithmetic and copies ran while one was open for 0% -> 0% of each run, Pallas kernels for 4% -> 5%
where the time goes in v4:
time: 71.1 us; the launch traced here: 70 us
  starting transfers between devices  33.1 us (47%)
  waiting for transfers between devices  25.2 us (35%)
  local copies, waits for them, and re-layouts  5.63 us (8%)
  Pallas kernels  4.73 us (7%)
  other arithmetic  1.1 us (2%)
    ppermute x3, waiting for transfers between devices, from_tile(): return lax.ppermute(array, ('tile', 'mode'), pairs)  19.5 us
    ppermute x2, starting transfers between devices, swap(): return lax.ppermute(array, 'mode', [(i, i ^ 1) for i in range(modes)])  14.5 us
    ppermute x3, starting transfers between devices, along_x(): lax.ppermute(array, 'mode', [(i, (i + 2 * steps) % modes) for i in range(...  9.94 us
    ppermute x3, starting transfers between devices, from_tile(): return lax.ppermute(array, ('tile', 'mode'), pairs)  8.7 us
    unnamed x18, local copies, waits for them, and re-layouts  5.63 us
    ppermute x2, waiting for transfers between devices, swap(): return lax.ppermute(array, 'mode', [(i, i ^ 1) for i in range(modes)])  5.16 us
    pallas_call x1, Pallas kernels, local(): pl.pallas_call(functools.partial(denom_kernel, tiles), out_shape=f32(OH,...  1.48 us
  transfers between devices with their start and end apart: 8, of which 5 were waited for; matrix products, arithmetic and copies ran while one was open for 0% of the time, Pallas kernels for 5%

profile of v4, /device:TPU:1, one launch (start us, length us, event | category | flops | bytes accessed | tf_op | source)
XLA Modules:
  0.0 70.0 jit_solution(13159511748346687051)
XLA Ops:
  0.0 4.1 %collective-permute-start = (f32[2,256,256]{2,1,0:T(8,128)}, f32[2,256,256]{2,1,0:T(8,128)S(1)}, u32[]{:S(2)}, u32[]{:S(2)}) collective-permute-start(f32[2,256,256]{2,1,0:T(8,128)} %inten.1), channel_id=1, source_target_pairs={{8,0},{10,2},{12,4},{14,6},{16,8},{1,9},{18,10},{3,11},{20,12},{5,... | collective-permute-start | bytes 1572872 | tf_op jit(solution)/shard_map/ppermute | solution.py:275
  4.1 3.1 %collective-permute-start.1 = (f32[1,2,256,256]{3,2,1,0:T(8,128)}, f32[1,2,256,256]{3,2,1,0:T(8,128)S(1)}, u32[]{:S(2)}, u32[]{:S(2)}) collective-permute-start(f32[1,2,256,256]{3,2,1,0:T(8,128)} %own.3), channel_id=1, source_target_pairs={{0,2},{1,3},{2,4},{3,5},{4,6},{5,7},{6,0},{7,1},{8,10},{9,11},{10,... | collective-permute-start | bytes 1572872 | tf_op jit(solution)/shard_map/ppermute | solution.py:263
  7.2 3.4 %collective-permute-start.2 = (f32[1,2,256,256]{3,2,1,0:T(8,128)}, f32[1,2,256,256]{3,2,1,0:T(8,128)S(1)}, u32[]{:S(2)}, u32[]{:S(2)}) collective-permute-start(f32[1,2,256,256]{3,2,1,0:T(8,128)} %own.3), channel_id=1, source_target_pairs={{0,6},{1,7},{2,0},{3,1},{4,2},{5,3},{6,4},{7,5},{8,14},{9,15},{10,... | collective-permute-start | bytes 1572872 | tf_op jit(solution)/shard_map/ppermute | solution.py:263
  10.6 3.4 %collective-permute-start.3 = (f32[1,2,256,256]{3,2,1,0:T(8,128)}, f32[1,2,256,256]{3,2,1,0:T(8,128)S(1)}, u32[]{:S(2)}, u32[]{:S(2)}) collective-permute-start(f32[1,2,256,256]{3,2,1,0:T(8,128)} %own.3), channel_id=1, source_target_pairs={{0,4},{1,5},{2,6},{3,7},{4,0},{5,1},{6,2},{7,3},{8,12},{9,13},{10,... | collective-permute-start | bytes 1572872 | tf_op jit(solution)/shard_map/ppermute | solution.py:263
  14.0 0.0 copy-start
  14.0 1.1 %copy-done = f32[2,320,256]{2,1,0:T(8,128)S(1)} copy-done((f32[2,320,256]{2,1,0:T(8,128)S(1)}, f32[2,320,256]{2,1,0:T(8,128)}, u32[]{:S(2)}) %copy-start) | copy-done | bytes 655384
  15.1 1.0 %copy-done.3 = f32[1,2,256,256]{3,2,1,0:T(8,128)S(1)} copy-done((f32[1,2,256,256]{3,2,1,0:T(8,128)S(1)}, f32[1,2,256,256]{3,2,1,0:T(8,128)}, u32[]{:S(2)}) %copy-start.3) | copy-done | bytes 524312
  16.2 0.1 pack.1
  16.2 3.2 %collective-permute-start.4 = (f32[2,320,128]{2,1,0:T(8,128)S(1)}, f32[2,320,128]{2,1,0:T(8,128)S(1)}, u32[]{:S(2)}, u32[]{:S(2)}) collective-permute-start(f32[2,320,128]{2,1,0:T(8,128)S(1)} %get-tuple-element.22), channel_id=1, source_target_pairs={{8,0},{10,2},{12,4},{14,6},{16,8},{1,9},{18,10},{3,11},{20,12},{5,... | collective-permute-start | bytes 983048 | tf_op jit(solution)/shard_map/ppermute | solution.py:275
  19.5 4.0 %collective-permute-done.4.halo = f32[2,320,128]{2,1,0:T(8,128)S(1)} collective-permute-done((f32[2,320,128]{2,1,0:T(8,128)S(1)}, f32[2,320,128]{2,1,0:T(8,128)S(1)}, u32[]{:S(2)}, u32[]{:S(2)}) %collective-permute-start.4) | collective-permute-done | bytes 327712 | tf_op jit(solution)/shard_map/ppermute | solution.py:275
  23.5 1.1 %copy-done.1 = f32[2,320,256]{2,1,0:T(8,128)S(1)} copy-done((f32[2,320,256]{2,1,0:T(8,128)S(1)}, f32[2,320,256]{2,1,0:T(8,128)}, u32[]{:S(2)}) %copy-start.1) | copy-done | bytes 655384
  24.5 1.0 %copy-done.4 = f32[1,2,256,256]{3,2,1,0:T(8,128)S(1)} copy-done((f32[1,2,256,256]{3,2,1,0:T(8,128)S(1)}, f32[1,2,256,256]{3,2,1,0:T(8,128)}, u32[]{:S(2)}) %copy-start.4) | copy-done | bytes 524312
  25.6 0.7 copy-done.6
  26.3 0.7 copy-done.8
  26.9 1.0 %windows.1 = (f32[3,2,256,256]{3,2,1,0:T(8,128)S(1)}, bf16[2,512,512]{2,1,0:T(8,128)(2,1)S(1)}, f32[3,1,256,512]{3,2,1,0:T(8,128)S(1)}, f32[3,256,256]{2,1,0:T(8,128)S(1)}) custom-call(s32[2,192]{1,0:T(2,128)S(1)} %bitcast.1, f32[2,129]{1,0:T(2,128)S(1)} %copy-done.8, f32[2,320,256]{2,1,0:T(8,128)S(1)} %copy-done.1, ...), custom_call_target="tpu_custom_call" | custom-call | bytes 14000000 | tf_op jit(solution)/shard_map/windows/pallas_call | solution.py:297
  28.0 0.0 collective-permute-done.2.second
  28.0 0.6 collective-permute-done.3.third
  28.6 0.2 merge.1.mine
  28.8 0.0 copy-start.5
  28.8 0.0 copy-start.7
  28.8 11.8 %collective-permute-start.5 = (f32[9,256,256]{2,1,0:T(8,128)S(1)}, f32[9,256,256]{2,1,0:T(8,128)S(1)}, u32[]{:S(2)}, u32[]{:S(2)}) collective-permute-start(f32[9,256,256]{2,1,0:T(8,128)S(1)} %merge.1.mine), channel_id=1, source_target_pairs={{0,1},{1,0},{2,3},{3,2},{4,5},{5,4},{6,7},{7,6},{8,9},{9,8},{10,11... | collective-permute-start | bytes 7077896 | tf_op jit(solution)/shard_map/ppermute | solution.py:266
  40.6 0.7 far_of_own_modes.1
  41.3 3.5 %collective-permute-done.5.theirs = f32[9,256,256]{2,1,0:T(8,128)S(1)} collective-permute-done((f32[9,256,256]{2,1,0:T(8,128)S(1)}, f32[9,256,256]{2,1,0:T(8,128)S(1)}, u32[]{:S(2)}, u32[]{:S(2)}) %collective-permute-start.5) | collective-permute-done | bytes 2359328 | tf_op jit(solution)/shard_map/ppermute | solution.py:266
  44.7 1.3 %update_terms.1 = (f32[2,320,256]{2,1,0:T(8,128)S(1)}, f32[2,320,128]{2,1,0:T(8,128)S(1)}, f32[256,256]{1,0:T(8,128)S(1)}) custom-call(s32[2,192]{1,0:T(2,128)S(1)} %bitcast.3, f32[2,256,256]{2,1,0:T(8,128)S(1)} %copy-done.5, f32[2,256,256]{2,1,0:T(8,128)S(1)} %collective-permute-done.inward, f32[9,256,256]{2,1,0:T(8,128)S(1)} %merge.1.mine, ...), custom_call_target="tpu_custom_call" | custom-call | bytes 35000000 | tf_op jit(solution)/shard_map/update_terms/pallas_call | solution.py:340
  46.0 0.0 copy-start.2
  46.1 1.4 %collective-permute-start.6 = (f32[2,320,128]{2,1,0:T(8,128)S(1)}, f32[2,320,128]{2,1,0:T(8,128)S(1)}, u32[]{:S(2)}, u32[]{:S(2)}) collective-permute-start(f32[2,320,128]{2,1,0:T(8,128)S(1)} %get-tuple-element.35), channel_id=1, source_target_pairs={{9,1},{11,3},{13,5},{15,7},{0,8},{17,9},{2,10},{19,11},{4,12},{21,... | collective-permute-start | bytes 983048 | tf_op jit(solution)/shard_map/ppermute | solution.py:275
  47.5 1.5 %denominator.1 = f32[320,256]{1,0:T(8,128)S(1)} custom-call(s32[2,192]{1,0:T(2,128)S(1)} %bitcast.4, f32[256,256]{1,0:T(8,128)S(1)} %get-tuple-element.36.weight), custom_call_target="tpu_custom_call" | custom-call | bytes 12250000 | tf_op jit(solution)/shard_map/denominator/pallas_call | solution.py:358
  49.0 15.5 %collective-permute-done.6 = f32[2,320,128]{2,1,0:T(8,128)S(1)} collective-permute-done((f32[2,320,128]{2,1,0:T(8,128)S(1)}, f32[2,320,128]{2,1,0:T(8,128)S(1)}, u32[]{:S(2)}, u32[]{:S(2)}) %collective-permute-start.6) | collective-permute-done | bytes 327712 | tf_op jit(solution)/shard_map/ppermute | solution.py:275
  64.5 0.1 fusion
  64.6 2.7 %collective-permute-start.7 = (f32[2,320,256]{2,1,0:T(8,128)S(1)}, f32[2,320,256]{2,1,0:T(8,128)S(1)}, u32[]{:S(2)}, u32[]{:S(2)}) collective-permute-start(f32[2,320,256]{2,1,0:T(8,128)S(1)} %fusion), channel_id=1, source_target_pairs={{0,1},{1,0},{2,3},{3,2},{4,5},{5,4},{6,7},{7,6},{8,9},{9,8},{10,11... | collective-permute-start | bytes 1966088 | tf_op jit(solution)/shard_map/ppermute | solution.py:266
  67.3 1.7 %collective-permute-done.7 = f32[2,320,256]{2,1,0:T(8,128)S(1)} collective-permute-done((f32[2,320,256]{2,1,0:T(8,128)S(1)}, f32[2,320,256]{2,1,0:T(8,128)S(1)}, u32[]{:S(2)}, u32[]{:S(2)}) %collective-permute-start.7) | collective-permute-done | bytes 655392 | tf_op jit(solution)/shard_map/ppermute | solution.py:266
  69.0 1.0 %add_add_fusion = f32[2,320,256]{2,1,0:T(8,128)} fusion(f32[2,320,256]{2,1,0:T(8,128)S(1)} %copy-done.2, f32[2,320,256]{2,1,0:T(8,128)S(1)} %fusion, f32[2,320,256]{2,1,0:T(8,128)S(1)} %collective-permute-done.7), kind=kLoop, calls=%fused_computation.2 | loop fusion | flops 327680 | bytes 2621440 | tf_op jit(solution)/shard_map/add | solution.py:372
  (11 shorter events, 0.1 us)
Async XLA Ops:
  0.0 28.0 %collective-permute-start = (f32[2,256,256]{2,1,0:T(8,128)}, f32[2,256,256]{2,1,0:T(8,128)S(1)}, u32[]{:S(2)}, u32[]{:S(2)}) collective-permute-start(f32[2,256,256]{2,1,0:T(8,128)} %inten.1), channel_id=1, source_target_pairs={{8,0},{10,2},{12,4},{14,6},{16,8},{1,9},{18,10},{3,11},{20,12},{5,... | collective-permute-start | bytes 1572872 | tf_op jit(solution)/shard_map/ppermute | solution.py:275
  4.1 23.9 %collective-permute-start.1 = (f32[1,2,256,256]{3,2,1,0:T(8,128)}, f32[1,2,256,256]{3,2,1,0:T(8,128)S(1)}, u32[]{:S(2)}, u32[]{:S(2)}) collective-permute-start(f32[1,2,256,256]{3,2,1,0:T(8,128)} %own.3), channel_id=1, source_target_pairs={{0,2},{1,3},{2,4},{3,5},{4,6},{5,7},{6,0},{7,1},{8,10},{9,11},{10,... | collective-permute-start | bytes 1572872 | tf_op jit(solution)/shard_map/ppermute | solution.py:263
  7.2 20.8 %collective-permute-start.2 = (f32[1,2,256,256]{3,2,1,0:T(8,128)}, f32[1,2,256,256]{3,2,1,0:T(8,128)S(1)}, u32[]{:S(2)}, u32[]{:S(2)}) collective-permute-start(f32[1,2,256,256]{3,2,1,0:T(8,128)} %own.3), channel_id=1, source_target_pairs={{0,6},{1,7},{2,0},{3,1},{4,2},{5,3},{6,4},{7,5},{8,14},{9,15},{10,... | collective-permute-start | bytes 1572872 | tf_op jit(solution)/shard_map/ppermute | solution.py:263
  10.6 18.0 %collective-permute-start.3 = (f32[1,2,256,256]{3,2,1,0:T(8,128)}, f32[1,2,256,256]{3,2,1,0:T(8,128)S(1)}, u32[]{:S(2)}, u32[]{:S(2)}) collective-permute-start(f32[1,2,256,256]{3,2,1,0:T(8,128)} %own.3), channel_id=1, source_target_pairs={{0,4},{1,5},{2,6},{3,7},{4,0},{5,1},{6,2},{7,3},{8,12},{9,13},{10,... | collective-permute-start | bytes 1572872 | tf_op jit(solution)/shard_map/ppermute | solution.py:263
  14.0 1.1 %copy-start = (f32[2,320,256]{2,1,0:T(8,128)S(1)}, f32[2,320,256]{2,1,0:T(8,128)}, u32[]{:S(2)}) copy-start(f32[2,320,256]{2,1,0:T(8,128)} %obj.3) | copy-start | bytes 1966084
  15.1 1.0 %copy-start.3 = (f32[1,2,256,256]{3,2,1,0:T(8,128)S(1)}, f32[1,2,256,256]{3,2,1,0:T(8,128)}, u32[]{:S(2)}) copy-start(f32[1,2,256,256]{3,2,1,0:T(8,128)} %own.3) | copy-start | bytes 1572868
  16.2 7.2 %collective-permute-start.4 = (f32[2,320,128]{2,1,0:T(8,128)S(1)}, f32[2,320,128]{2,1,0:T(8,128)S(1)}, u32[]{:S(2)}, u32[]{:S(2)}) collective-permute-start(f32[2,320,128]{2,1,0:T(8,128)S(1)} %get-tuple-element.22), channel_id=1, source_target_pairs={{8,0},{10,2},{12,4},{14,6},{16,8},{1,9},{18,10},{3,11},{20,12},{5,... | collective-permute-start | bytes 983048 | tf_op jit(solution)/shard_map/ppermute | solution.py:275
  23.5 1.1 %copy-start.1 = (f32[2,320,256]{2,1,0:T(8,128)S(1)}, f32[2,320,256]{2,1,0:T(8,128)}, u32[]{:S(2)}) copy-start(f32[2,320,256]{2,1,0:T(8,128)} %obj.3) | copy-start | bytes 1966084
  24.5 1.0 %copy-start.4 = (f32[1,2,256,256]{3,2,1,0:T(8,128)S(1)}, f32[1,2,256,256]{3,2,1,0:T(8,128)}, u32[]{:S(2)}) copy-start(f32[1,2,256,256]{3,2,1,0:T(8,128)} %own.3) | copy-start | bytes 1572868
  25.6 0.7 copy-start.6
  26.3 0.7 copy-start.8
  28.8 16.0 %copy-start.5 = (f32[2,256,256]{2,1,0:T(8,128)S(1)}, f32[2,256,256]{2,1,0:T(8,128)}, u32[]{:S(2)}) copy-start(f32[2,256,256]{2,1,0:T(8,128)} %inten.1) | copy-start | bytes 1572868
  28.8 16.0 %copy-start.7 = (s32[192,2]{0,1:T(2,128)S(1)}, s32[192,2]{0,1:T(2,128)}, u32[]{:S(2)}) copy-start(s32[192,2]{0,1:T(2,128)} %param.6) | copy-start | bytes 4612
  28.8 15.9 %collective-permute-start.5 = (f32[9,256,256]{2,1,0:T(8,128)S(1)}, f32[9,256,256]{2,1,0:T(8,128)S(1)}, u32[]{:S(2)}, u32[]{:S(2)}) collective-permute-start(f32[9,256,256]{2,1,0:T(8,128)S(1)} %merge.1.mine), channel_id=1, source_target_pairs={{0,1},{1,0},{2,3},{3,2},{4,5},{5,4},{6,7},{7,6},{8,9},{9,8},{10,11... | collective-permute-start | bytes 7077896 | tf_op jit(solution)/shard_map/ppermute | solution.py:266
  46.0 23.0 %copy-start.2 = (f32[2,320,256]{2,1,0:T(8,128)S(1)}, f32[2,320,256]{2,1,0:T(8,128)}, u32[]{:S(2)}) copy-start(f32[2,320,256]{2,1,0:T(8,128)} %obj.3) | copy-start | bytes 1966084
  46.1 18.4 %collective-permute-start.6 = (f32[2,320,128]{2,1,0:T(8,128)S(1)}, f32[2,320,128]{2,1,0:T(8,128)S(1)}, u32[]{:S(2)}, u32[]{:S(2)}) collective-permute-start(f32[2,320,128]{2,1,0:T(8,128)S(1)} %get-tuple-element.35), channel_id=1, source_target_pairs={{9,1},{11,3},{13,5},{15,7},{0,8},{17,9},{2,10},{19,11},{4,12},{21,... | collective-permute-start | bytes 983048 | tf_op jit(solution)/shard_map/ppermute | solution.py:275
  64.6 4.4 %collective-permute-start.7 = (f32[2,320,256]{2,1,0:T(8,128)S(1)}, f32[2,320,256]{2,1,0:T(8,128)S(1)}, u32[]{:S(2)}, u32[]{:S(2)}) collective-permute-start(f32[2,320,256]{2,1,0:T(8,128)S(1)} %fusion), channel_id=1, source_target_pairs={{0,1},{1,0},{2,3},{3,2},{4,5},{5,4},{6,7},{7,6},{8,9},{9,8},{10,11... | collective-permute-start | bytes 1966088 | tf_op jit(solution)/shard_map/ppermute | solution.py:266

commit v5 on v4

--- a/solution.py
+++ b/solution.py
@@ -50,16 +50,9 @@
         copy.wait()
 
 
-def pack_kernel(obj, own, halo, merged, sem):
+def merge_kernel(own, first, second, third, inward, merged, sem):
     core = lax.rem(lax.axis_index("mode"), 2)
-    edge = pl.ds(pl.multiple_of(core * HALF, HALF), HALF)
-    run_copies([(obj.at[:, :, edge], halo), (own.at[0], merged.at[0:2])], sem)
-
-
-def merge_kernel(before, first, second, third, inward, merged, sem):
-    del before
-    core = lax.rem(lax.axis_index("mode"), 2)
-    moves = [(array.at[0], merged.at[2 * i + 2 : 2 * i + 4]) for i, array in enumerate((first, second, third))]
+    moves = [(array.at[0], merged.at[2 * i : 2 * i + 2]) for i, array in enumerate((own, first, second, third))]
     moves.append((inward.at[1 - core], merged.at[MODES]))
     run_copies(moves, sem)
 
@@ -100,12 +93,12 @@
         power[...] += block[:, :P_SIZE] * block[:, :P_SIZE] + block[:, P_SIZE:] * block[:, P_SIZE:]
 
 
-def window_kernel(tiles, pos_ref, taps_ref, obj, halo, own, patch, stacks, far, power, wave, low, midb, row_pad, sem):
+def window_kernel(tiles, pos_ref, taps_ref, obj, beside, own, patch, stacks, far, power, wave, low, midb, row_pad, sem):
     _, core = place_of(tiles)
     rim = pl.ds(pl.multiple_of((1 - core) * TW, HALF), HALF)
     moves = (
         (obj, wave.at[:, :OH, pl.ds(pl.multiple_of(core * HALF, HALF), TW)]),
-        (halo, wave.at[:, :OH, rim]),
+        (beside.at[:, :, pl.ds(pl.multiple_of(core * HALF, HALF), HALF)], wave.at[:, :OH, rim]),
     )
     copies = [pltpu.make_async_copy(src, dst, sem.at[i]) for i, (src, dst) in enumerate(moves)]
     for copy in copies:
@@ -275,17 +268,7 @@
         return lax.ppermute(array, ("tile", "mode"), pairs)
 
     ring = [along_x(probe_modes, step) for step in (1, -1, 2)]
-    halo, held = pl.pallas_call(
-        pack_kernel,
-        out_shape=(f32(2, OH, HALF), f32(MODES + 1, P_SIZE, P_SIZE)),
-        in_specs=[ANY, ANY],
-        out_specs=(VMEM, VMEM),
-        scratch_shapes=[pltpu.SemaphoreType.DMA((2,))],
-        compiler_params=limit(4),
-        cost_estimate=cost(2.2),
-        name="pack",
-    )(object_field, probe_modes)
-    halo = from_tile(halo, 1)
+    beside = from_tile(object_field, 1)
     inward = from_tile(intensity, 1)
 
     def stages(units):
@@ -310,20 +293,21 @@
         compiler_params=limit(16),
         cost_estimate=cost(4.0),
         name="windows",
-    )(spots, kernel_taps, object_field, halo, probe_modes)
-
+    )(spots, kernel_taps, object_field, beside, probe_modes)
+
+    held, inward, patch, stacks, far_own, power = lax.optimization_barrier(
+        (probe_modes, inward, patch, stacks, far_own, power)
+    )
     mine = pl.pallas_call(
         merge_kernel,
         out_shape=f32(MODES + 1, P_SIZE, P_SIZE),
         in_specs=[ANY] * 5,
-        out_specs=ANY,
-        scratch_shapes=[pltpu.SemaphoreType.DMA((4,))],
-        input_output_aliases={0: 0},
+        out_specs=VMEM,
+        scratch_shapes=[pltpu.SemaphoreType.DMA((5,))],
         compiler_params=limit(4),
         cost_estimate=cost(1.0),
         name="merge",
     )(held, *ring, inward)
-    mine, patch, stacks, far_own, power = lax.optimization_barrier((mine, patch, stacks, far_own, power))
     theirs = swap(mine)
 
     far_ring, power = pl.pallas_call(

time: 71.1 us -> 71.4 us (level)
  the two profiles are of different devices: /device:TPU:1 before, /device:TPU:67 now
where the time goes in v5:
time: 71.4 us; the launch traced here: 71 us
  starting transfers between devices  28 us (39%)
  waiting for transfers between devices  19.5 us (27%)
  Pallas kernels  18.8 us (26%)
  local copies, waits for them, and re-layouts  3.5 us (5%)
  other arithmetic  1.1 us (2%)
    ppermute x3, waiting for transfers between devices, along_x(): lax.ppermute(array, 'mode', [(i, (i + 2 * steps) % modes) for i in range(...  12.4 us
    ppermute x2, starting transfers between devices, swap(): return lax.ppermute(array, 'mode', [(i, i ^ 1) for i in range(modes)])  10.5 us
    pallas_call x1, Pallas kernels, local(): pl.pallas_call(functools.partial(second_kernel, tiles), out_shape=(f32(2,...  10.4 us
    ppermute x3, starting transfers between devices, along_x(): lax.ppermute(array, 'mode', [(i, (i + 2 * steps) % modes) for i in range(...  9.03 us
    ppermute x3, starting transfers between devices, from_tile(): return lax.ppermute(array, ('tile', 'mode'), pairs)  8.45 us
    ppermute x3, waiting for transfers between devices, from_tile(): return lax.ppermute(array, ('tile', 'mode'), pairs)  3.98 us
    unnamed x14, local copies, waits for them, and re-layouts  3.5 us
    pallas_call x1, Pallas kernels, local(): pl.pallas_call(functools.partial(window_kernel, tiles), out_shape=(f32(3,...  3.29 us
  transfers between devices with their start and end apart: 8, of which 5 were waited for; matrix products, arithmetic and copies ran while one was open for 0% of the time, Pallas kernels for 12%

profile of v5, /device:TPU:67, one launch (start us, length us, event | category | flops | bytes accessed | tf_op | source)
XLA Modules:
  0.0 71.0 jit_solution(18311840708215713144)
XLA Ops:
  0.0 3.2 %collective-permute-start.1 = (f32[2,320,256]{2,1,0:T(8,128)}, f32[2,320,256]{2,1,0:T(8,128)S(1)}, u32[]{:S(2)}, u32[]{:S(2)}) collective-permute-start(f32[2,320,256]{2,1,0:T(8,128)} %obj.1), channel_id=1, source_target_pairs={{8,0},{10,2},{12,4},{14,6},{16,8},{1,9},{18,10},{3,11},{20,12},{5,... | collective-permute-start | bytes 1966088 | tf_op jit(solution)/shard_map/ppermute | solution.py:268
  3.2 3.2 %collective-permute-start = (f32[2,256,256]{2,1,0:T(8,128)}, f32[2,256,256]{2,1,0:T(8,128)S(1)}, u32[]{:S(2)}, u32[]{:S(2)}) collective-permute-start(f32[2,256,256]{2,1,0:T(8,128)} %inten.1), channel_id=1, source_target_pairs={{8,0},{10,2},{12,4},{14,6},{16,8},{1,9},{18,10},{3,11},{20,12},{5,... | collective-permute-start | bytes 1572872 | tf_op jit(solution)/shard_map/ppermute | solution.py:268
  6.4 3.1 %collective-permute-start.2 = (f32[1,2,256,256]{3,2,1,0:T(8,128)}, f32[1,2,256,256]{3,2,1,0:T(8,128)S(1)}, u32[]{:S(2)}, u32[]{:S(2)}) collective-permute-start(f32[1,2,256,256]{3,2,1,0:T(8,128)} %own.2), channel_id=1, source_target_pairs={{0,2},{1,3},{2,4},{3,5},{4,6},{5,7},{6,0},{7,1},{8,10},{9,11},{10,... | collective-permute-start | bytes 1572872 | tf_op jit(solution)/shard_map/ppermute | solution.py:256
  9.5 2.2 %collective-permute-start.3 = (f32[1,2,256,256]{3,2,1,0:T(8,128)}, f32[1,2,256,256]{3,2,1,0:T(8,128)S(1)}, u32[]{:S(2)}, u32[]{:S(2)}) collective-permute-start(f32[1,2,256,256]{3,2,1,0:T(8,128)} %own.2), channel_id=1, source_target_pairs={{0,6},{1,7},{2,0},{3,1},{4,2},{5,3},{6,4},{7,5},{8,14},{9,15},{10,... | collective-permute-start | bytes 1572872 | tf_op jit(solution)/shard_map/ppermute | solution.py:256
  11.7 3.8 %collective-permute-start.4 = (f32[1,2,256,256]{3,2,1,0:T(8,128)}, f32[1,2,256,256]{3,2,1,0:T(8,128)S(1)}, u32[]{:S(2)}, u32[]{:S(2)}) collective-permute-start(f32[1,2,256,256]{3,2,1,0:T(8,128)} %own.2), channel_id=1, source_target_pairs={{0,4},{1,5},{2,6},{3,7},{4,0},{5,1},{6,2},{7,3},{8,12},{9,13},{10,... | collective-permute-start | bytes 1572872 | tf_op jit(solution)/shard_map/ppermute | solution.py:256
  15.5 0.0 collective-permute-done.1.beside
  15.5 0.0 copy-start
  15.5 1.1 %copy-done = f32[2,320,256]{2,1,0:T(8,128)S(1)} copy-done((f32[2,320,256]{2,1,0:T(8,128)S(1)}, f32[2,320,256]{2,1,0:T(8,128)}, u32[]{:S(2)}) %copy-start) | copy-done | bytes 655384
  16.6 1.0 %copy-done.2 = f32[1,2,256,256]{3,2,1,0:T(8,128)S(1)} copy-done((f32[1,2,256,256]{3,2,1,0:T(8,128)S(1)}, f32[1,2,256,256]{3,2,1,0:T(8,128)}, u32[]{:S(2)}) %copy-start.2) | copy-done | bytes 524312
  17.6 0.7 copy-done.4
  18.3 0.7 copy-done.6
  19.0 3.3 %windows.1 = (f32[3,2,256,256]{3,2,1,0:T(8,128)S(1)}, bf16[2,512,512]{2,1,0:T(8,128)(2,1)S(1)}, f32[3,1,256,512]{3,2,1,0:T(8,128)S(1)}, f32[3,256,256]{2,1,0:T(8,128)S(1)}) custom-call(s32[2,192]{1,0:T(2,128)S(1)} %bitcast.1, f32[2,129]{1,0:T(2,128)S(1)} %copy-done.6, f32[2,320,256]{2,1,0:T(8,128)S(1)} %copy-done, ...), custom_call_target="tpu_custom_call" | custom-call | bytes 14000000 | tf_op jit(solution)/shard_map/windows/pallas_call | solution.py:280
  22.3 0.0 collective-permute-done.inward
  22.3 0.0 collective-permute-done.2.first
  22.3 0.5 collective-permute-done.3.second
  22.8 11.9 %collective-permute-done.4.third = f32[1,2,256,256]{3,2,1,0:T(8,128)S(1)} collective-permute-done((f32[1,2,256,256]{3,2,1,0:T(8,128)}, f32[1,2,256,256]{3,2,1,0:T(8,128)S(1)}, u32[]{:S(2)}, u32[]{:S(2)}) %collective-permute-start.4) | collective-permute-done | bytes 524320 | tf_op jit(solution)/shard_map/ppermute | solution.py:256
  34.7 0.2 merge.1.mine
  34.9 0.0 copy-start.3
  34.9 0.0 copy-start.5
  34.9 5.2 %collective-permute-start.5 = (f32[9,256,256]{2,1,0:T(8,128)S(1)}, f32[9,256,256]{2,1,0:T(8,128)S(1)}, u32[]{:S(2)}, u32[]{:S(2)}) collective-permute-start(f32[9,256,256]{2,1,0:T(8,128)S(1)} %merge.1.mine), channel_id=1, source_target_pairs={{0,1},{1,0},{2,3},{3,2},{4,5},{5,4},{6,7},{7,6},{8,9},{9,8},{10,11... | collective-permute-start | bytes 7077896 | tf_op jit(solution)/shard_map/ppermute | solution.py:259
  40.1 2.7 %far_of_own_modes.1 = (f32[3,3,256,512]{3,2,1,0:T(8,128)S(1)}, f32[3,256,256]{2,1,0:T(8,128)S(1)}) custom-call(s32[2,192]{1,0:T(2,128)S(1)} %bitcast.2, f32[9,256,256]{2,1,0:T(8,128)S(1)} %merge.1.mine, f32[3,2,256,256]{3,2,1,0:T(8,128)S(1)} %get-tuple-element.27.patch, bf16[2,512,512]{2,1,0:T(8,128)(2,1)S(1)} %get-tuple-element.28.stacks, ...), custom_call_target="tpu_custom_call" | custom-call | bytes 14000000 | tf_op jit(solution)/shard_map/far_of_own_modes/pallas_call | solution.py:313
  42.9 1.4 %collective-permute-done.5.theirs = f32[9,256,256]{2,1,0:T(8,128)S(1)} collective-permute-done((f32[9,256,256]{2,1,0:T(8,128)S(1)}, f32[9,256,256]{2,1,0:T(8,128)S(1)}, u32[]{:S(2)}, u32[]{:S(2)}) %collective-permute-start.5) | collective-permute-done | bytes 2359328 | tf_op jit(solution)/shard_map/ppermute | solution.py:259
  44.3 0.0 copy-done.3
  44.3 10.4 %update_terms.1 = (f32[2,320,256]{2,1,0:T(8,128)S(1)}, f32[2,320,128]{2,1,0:T(8,128)S(1)}, f32[256,256]{1,0:T(8,128)S(1)}) custom-call(s32[2,192]{1,0:T(2,128)S(1)} %bitcast.3, f32[2,256,256]{2,1,0:T(8,128)S(1)} %copy-done.3, f32[2,256,256]{2,1,0:T(8,128)S(1)} %collective-permute-done.inward, f32[9,256,256]{2,1,0:T(8,128)S(1)} %merge.1.mine, ...), custom_call_target="tpu_custom_call" | custom-call | bytes 35000000 | tf_op jit(solution)/shard_map/update_terms/pallas_call | solution.py:324
  54.7 0.0 copy-start.1
  54.7 2.1 %collective-permute-start.6 = (f32[2,320,128]{2,1,0:T(8,128)S(1)}, f32[2,320,128]{2,1,0:T(8,128)S(1)}, u32[]{:S(2)}, u32[]{:S(2)}) collective-permute-start(f32[2,320,128]{2,1,0:T(8,128)S(1)} %get-tuple-element.33), channel_id=1, source_target_pairs={{9,1},{11,3},{13,5},{15,7},{0,8},{17,9},{2,10},{19,11},{4,12},{21,... | collective-permute-start | bytes 983048 | tf_op jit(solution)/shard_map/ppermute | solution.py:268
  56.8 2.2 %denominator.1 = f32[320,256]{1,0:T(8,128)S(1)} custom-call(s32[2,192]{1,0:T(2,128)S(1)} %bitcast.4, f32[256,256]{1,0:T(8,128)S(1)} %get-tuple-element.34.weight), custom_call_target="tpu_custom_call" | custom-call | bytes 12250000 | tf_op jit(solution)/shard_map/denominator/pallas_call | solution.py:342
  59.0 4.0 %collective-permute-done.6 = f32[2,320,128]{2,1,0:T(8,128)S(1)} collective-permute-done((f32[2,320,128]{2,1,0:T(8,128)S(1)}, f32[2,320,128]{2,1,0:T(8,128)S(1)}, u32[]{:S(2)}, u32[]{:S(2)}) %collective-permute-start.6) | collective-permute-done | bytes 327712 | tf_op jit(solution)/shard_map/ppermute | solution.py:268
  63.0 0.1 fusion
  63.1 5.3 %collective-permute-start.7 = (f32[2,320,256]{2,1,0:T(8,128)S(1)}, f32[2,320,256]{2,1,0:T(8,128)S(1)}, u32[]{:S(2)}, u32[]{:S(2)}) collective-permute-start(f32[2,320,256]{2,1,0:T(8,128)S(1)} %fusion), channel_id=1, source_target_pairs={{0,1},{1,0},{2,3},{3,2},{4,5},{5,4},{6,7},{7,6},{8,9},{9,8},{10,11... | collective-permute-start | bytes 1966088 | tf_op jit(solution)/shard_map/ppermute | solution.py:259
  68.3 1.7 %collective-permute-done.7 = f32[2,320,256]{2,1,0:T(8,128)S(1)} collective-permute-done((f32[2,320,256]{2,1,0:T(8,128)S(1)}, f32[2,320,256]{2,1,0:T(8,128)S(1)}, u32[]{:S(2)}, u32[]{:S(2)}) %collective-permute-start.7) | collective-permute-done | bytes 655392 | tf_op jit(solution)/shard_map/ppermute | solution.py:259
  70.0 1.0 %add_add_fusion = f32[2,320,256]{2,1,0:T(8,128)} fusion(f32[2,320,256]{2,1,0:T(8,128)S(1)} %copy-done.1, f32[2,320,256]{2,1,0:T(8,128)S(1)} %fusion, f32[2,320,256]{2,1,0:T(8,128)S(1)} %collective-permute-done.7), kind=kLoop, calls=%fused_computation.2 | loop fusion | flops 327680 | bytes 2621440 | tf_op jit(solution)/shard_map/add | solution.py:356
  (6 shorter events, 0.1 us)
Async XLA Ops:
  0.0 15.5 %collective-permute-start.1 = (f32[2,320,256]{2,1,0:T(8,128)}, f32[2,320,256]{2,1,0:T(8,128)S(1)}, u32[]{:S(2)}, u32[]{:S(2)}) collective-permute-start(f32[2,320,256]{2,1,0:T(8,128)} %obj.1), channel_id=1, source_target_pairs={{8,0},{10,2},{12,4},{14,6},{16,8},{1,9},{18,10},{3,11},{20,12},{5,... | collective-permute-start | bytes 1966088 | tf_op jit(solution)/shard_map/ppermute | solution.py:268
  3.2 19.1 %collective-permute-start = (f32[2,256,256]{2,1,0:T(8,128)}, f32[2,256,256]{2,1,0:T(8,128)S(1)}, u32[]{:S(2)}, u32[]{:S(2)}) collective-permute-start(f32[2,256,256]{2,1,0:T(8,128)} %inten.1), channel_id=1, source_target_pairs={{8,0},{10,2},{12,4},{14,6},{16,8},{1,9},{18,10},{3,11},{20,12},{5,... | collective-permute-start | bytes 1572872 | tf_op jit(solution)/shard_map/ppermute | solution.py:268
  6.4 15.9 %collective-permute-start.2 = (f32[1,2,256,256]{3,2,1,0:T(8,128)}, f32[1,2,256,256]{3,2,1,0:T(8,128)S(1)}, u32[]{:S(2)}, u32[]{:S(2)}) collective-permute-start(f32[1,2,256,256]{3,2,1,0:T(8,128)} %own.2), channel_id=1, source_target_pairs={{0,2},{1,3},{2,4},{3,5},{4,6},{5,7},{6,0},{7,1},{8,10},{9,11},{10,... | collective-permute-start | bytes 1572872 | tf_op jit(solution)/shard_map/ppermute | solution.py:256
  9.5 13.2 %collective-permute-start.3 = (f32[1,2,256,256]{3,2,1,0:T(8,128)}, f32[1,2,256,256]{3,2,1,0:T(8,128)S(1)}, u32[]{:S(2)}, u32[]{:S(2)}) collective-permute-start(f32[1,2,256,256]{3,2,1,0:T(8,128)} %own.2), channel_id=1, source_target_pairs={{0,6},{1,7},{2,0},{3,1},{4,2},{5,3},{6,4},{7,5},{8,14},{9,15},{10,... | collective-permute-start | bytes 1572872 | tf_op jit(solution)/shard_map/ppermute | solution.py:256
  11.7 22.9 %collective-permute-start.4 = (f32[1,2,256,256]{3,2,1,0:T(8,128)}, f32[1,2,256,256]{3,2,1,0:T(8,128)S(1)}, u32[]{:S(2)}, u32[]{:S(2)}) collective-permute-start(f32[1,2,256,256]{3,2,1,0:T(8,128)} %own.2), channel_id=1, source_target_pairs={{0,4},{1,5},{2,6},{3,7},{4,0},{5,1},{6,2},{7,3},{8,12},{9,13},{10,... | collective-permute-start | bytes 1572872 | tf_op jit(solution)/shard_map/ppermute | solution.py:256
  15.5 1.1 %copy-start = (f32[2,320,256]{2,1,0:T(8,128)S(1)}, f32[2,320,256]{2,1,0:T(8,128)}, u32[]{:S(2)}) copy-start(f32[2,320,256]{2,1,0:T(8,128)} %obj.1) | copy-start | bytes 1966084
  16.6 1.0 %copy-start.2 = (f32[1,2,256,256]{3,2,1,0:T(8,128)S(1)}, f32[1,2,256,256]{3,2,1,0:T(8,128)}, u32[]{:S(2)}) copy-start(f32[1,2,256,256]{3,2,1,0:T(8,128)} %own.2) | copy-start | bytes 1572868
  17.6 0.7 copy-start.4
  18.3 0.7 copy-start.6
  34.9 9.4 %copy-start.3 = (f32[2,256,256]{2,1,0:T(8,128)S(1)}, f32[2,256,256]{2,1,0:T(8,128)}, u32[]{:S(2)}) copy-start(f32[2,256,256]{2,1,0:T(8,128)} %inten.1) | copy-start | bytes 1572868
  34.9 9.4 %copy-start.5 = (s32[192,2]{0,1:T(2,128)S(1)}, s32[192,2]{0,1:T(2,128)}, u32[]{:S(2)}) copy-start(s32[192,2]{0,1:T(2,128)} %param.6) | copy-start | bytes 4612
  34.9 9.4 %collective-permute-start.5 = (f32[9,256,256]{2,1,0:T(8,128)S(1)}, f32[9,256,256]{2,1,0:T(8,128)S(1)}, u32[]{:S(2)}, u32[]{:S(2)}) collective-permute-start(f32[9,256,256]{2,1,0:T(8,128)S(1)} %merge.1.mine), channel_id=1, source_target_pairs={{0,1},{1,0},{2,3},{3,2},{4,5},{5,4},{6,7},{7,6},{8,9},{9,8},{10,11... | collective-permute-start | bytes 7077896 | tf_op jit(solution)/shard_map/ppermute | solution.py:259
  54.7 15.4 %copy-start.1 = (f32[2,320,256]{2,1,0:T(8,128)S(1)}, f32[2,320,256]{2,1,0:T(8,128)}, u32[]{:S(2)}) copy-start(f32[2,320,256]{2,1,0:T(8,128)} %obj.1) | copy-start | bytes 1966084
  54.7 8.2 %collective-permute-start.6 = (f32[2,320,128]{2,1,0:T(8,128)S(1)}, f32[2,320,128]{2,1,0:T(8,128)S(1)}, u32[]{:S(2)}, u32[]{:S(2)}) collective-permute-start(f32[2,320,128]{2,1,0:T(8,128)S(1)} %get-tuple-element.33), channel_id=1, source_target_pairs={{9,1},{11,3},{13,5},{15,7},{0,8},{17,9},{2,10},{19,11},{4,12},{21,... | collective-permute-start | bytes 983048 | tf_op jit(solution)/shard_map/ppermute | solution.py:268
  63.1 7.0 %collective-permute-start.7 = (f32[2,320,256]{2,1,0:T(8,128)S(1)}, f32[2,320,256]{2,1,0:T(8,128)S(1)}, u32[]{:S(2)}, u32[]{:S(2)}) collective-permute-start(f32[2,320,256]{2,1,0:T(8,128)S(1)} %fusion), channel_id=1, source_target_pairs={{0,1},{1,0},{2,3},{3,2},{4,5},{5,4},{6,7},{7,6},{8,9},{9,8},{10,11... | collective-permute-start | bytes 1966088 | tf_op jit(solution)/shard_map/ppermute | solution.py:259

commit v6 on v4

--- a/solution.py
+++ b/solution.py
@@ -56,12 +56,16 @@
     run_copies([(obj.at[:, :, edge], halo), (own.at[0], merged.at[0:2])], sem)
 
 
-def merge_kernel(before, first, second, third, inward, merged, sem):
+def merge_kernel(before, first, second, third, merged, sem):
+    del before
+    arrays = (first, second, third)
+    run_copies([(array.at[0], merged.at[2 * i + 2 : 2 * i + 4]) for i, array in enumerate(arrays)], sem)
+
+
+def append_kernel(inward, before, merged, sem):
     del before
     core = lax.rem(lax.axis_index("mode"), 2)
-    moves = [(array.at[0], merged.at[2 * i + 2 : 2 * i + 4]) for i, array in enumerate((first, second, third))]
-    moves.append((inward.at[1 - core], merged.at[MODES]))
-    run_copies(moves, sem)
+    run_copies([(inward.at[1 - core], merged.at[MODES])], sem)
 
 
 def window_of(pos_ref, tiles, slot):
@@ -100,12 +104,12 @@
         power[...] += block[:, :P_SIZE] * block[:, :P_SIZE] + block[:, P_SIZE:] * block[:, P_SIZE:]
 
 
-def window_kernel(tiles, pos_ref, taps_ref, obj, halo, own, patch, stacks, far, power, wave, low, midb, row_pad, sem):
+def first_kernel(tiles, pos_ref, taps_ref, obj, beside, mine, patch, stacks, far, power, wave, low, midb, row_pad, sem):
     _, core = place_of(tiles)
     rim = pl.ds(pl.multiple_of((1 - core) * TW, HALF), HALF)
     moves = (
         (obj, wave.at[:, :OH, pl.ds(pl.multiple_of(core * HALF, HALF), TW)]),
-        (halo, wave.at[:, :OH, rim]),
+        (beside, wave.at[:, :OH, rim]),
     )
     copies = [pltpu.make_async_copy(src, dst, sem.at[i]) for i, (src, dst) in enumerate(moves)]
     for copy in copies:
@@ -144,23 +148,13 @@
                 turned = pltpu.roll(rows, lax.rem(EXT - offset, EXT), 1)[:, :P_SIZE]
                 patch[slot, part] = pltpu.roll(turned, lax.rem(TALL - extra, TALL), 0)[:P_SIZE]
             power[slot] = jnp.zeros((P_SIZE, P_SIZE), F32)
-            forward(own.at[0], (0,), patch.at[slot, 0], patch.at[slot, 1], stacks, low, midb, far.at[slot], power.at[slot])
-
-
-def first_kernel(tiles, pos_ref, mine, patch, stacks, before, far, power, low, midb):
-    @pl.loop(0, 3)
-    def _(slot):
-        here, _, _ = window_of(pos_ref, tiles, slot)
-
-        @pl.when(here)
-        def _():
-            power[slot] = before[slot]
             sides = (patch.at[slot, 0], patch.at[slot, 1])
-            forward(mine, (1, 2, 3), *sides, stacks, low, midb, far.at[slot], power.at[slot])
+            forward(mine, (0, 1), *sides, stacks, low, midb, far.at[slot, 0:2], power.at[slot])
+            forward(mine, (2, 3), *sides, stacks, low, midb, far.at[slot, 2:4], power.at[slot])
 
 
 def second_kernel(
-    tiles, pos_ref, inten, inward, mine, theirs, far_own, far_ring, patch, power, stacks, mid_out, rim_out, weight,
+    tiles, pos_ref, inten, inward, mine, theirs, far, patch, power, stacks, mid_out, rim_out, weight,
     total, meas, far_too, low, midb, ratio, acc,
 ):
     _, core = place_of(tiles)
@@ -188,8 +182,7 @@
             ratio[...] = jnp.sqrt(meas[slot]) / jnp.sqrt(ratio[...] + 1.0)
             acc[0] = -weight[...] * patch[slot, 0]
             acc[1] = -weight[...] * patch[slot, 1]
-            fields = [(far_own.at[slot, 0], mine, 0)]
-            fields += [(far_ring.at[slot, i], mine, i + 1) for i in range(3)]
+            fields = [(far.at[slot, i], mine, i) for i in range(HELD)]
             fields += [(far_too.at[i], theirs, i) for i in range(HELD)]
             for start in range(0, MODES, GROUP):
                 group = fields[start : start + GROUP]
@@ -275,7 +268,7 @@
         return lax.ppermute(array, ("tile", "mode"), pairs)
 
     ring = [along_x(probe_modes, step) for step in (1, -1, 2)]
-    halo, held = pl.pallas_call(
+    edge, held = pl.pallas_call(
         pack_kernel,
         out_shape=(f32(2, OH, HALF), f32(MODES + 1, P_SIZE, P_SIZE)),
         in_specs=[ANY, ANY],
@@ -285,7 +278,7 @@
         cost_estimate=cost(2.2),
         name="pack",
     )(object_field, probe_modes)
-    halo = from_tile(halo, 1)
+    beside = from_tile(edge, 1)
     inward = from_tile(intensity, 1)
 
     def stages(units):
@@ -294,53 +287,52 @@
             pltpu.VMEM((units * P_SIZE, 2 * P_SIZE), BF16),
         ]
 
-    patch, stacks, far_own, power = pl.pallas_call(
-        functools.partial(window_kernel, tiles),
+    mine = pl.pallas_call(
+        merge_kernel,
+        out_shape=f32(MODES + 1, P_SIZE, P_SIZE),
+        in_specs=[ANY] * 4,
+        out_specs=ANY,
+        scratch_shapes=[pltpu.SemaphoreType.DMA((3,))],
+        input_output_aliases={0: 0},
+        compiler_params=limit(4),
+        cost_estimate=cost(1.0),
+        name="merge",
+    )(held, *ring)
+    mine = pl.pallas_call(
+        append_kernel,
+        out_shape=f32(MODES + 1, P_SIZE, P_SIZE),
+        in_specs=[ANY, ANY],
+        out_specs=ANY,
+        scratch_shapes=[pltpu.SemaphoreType.DMA((1,))],
+        input_output_aliases={1: 0},
+        compiler_params=limit(4),
+        name="append",
+    )(inward, mine)
+    mine, beside = lax.optimization_barrier((mine, beside))
+    theirs = swap(mine)
+
+    patch, stacks, far, power = pl.pallas_call(
+        functools.partial(first_kernel, tiles),
         out_shape=(
             f32(3, 2, P_SIZE, P_SIZE),
             jax.ShapeDtypeStruct((2, 2 * P_SIZE, 2 * P_SIZE), BF16),
-            f32(3, 1, P_SIZE, 2 * P_SIZE),
+            f32(3, HELD, P_SIZE, 2 * P_SIZE),
             f32(3, P_SIZE, P_SIZE),
         ),
         in_specs=[SMEM, VMEM, ANY, ANY, VMEM],
         out_specs=(VMEM,) * 4,
         scratch_shapes=[pltpu.VMEM((2, OH + 8, EXT), F32)]
-        + stages(1)
+        + stages(GROUP)
         + [pltpu.VMEM((8, 2 * P_SIZE), F32), pltpu.SemaphoreType.DMA((2,))],
         compiler_params=limit(16),
-        cost_estimate=cost(4.0),
-        name="windows",
-    )(spots, kernel_taps, object_field, halo, probe_modes)
-
-    mine = pl.pallas_call(
-        merge_kernel,
-        out_shape=f32(MODES + 1, P_SIZE, P_SIZE),
-        in_specs=[ANY] * 5,
-        out_specs=ANY,
-        scratch_shapes=[pltpu.SemaphoreType.DMA((4,))],
-        input_output_aliases={0: 0},
-        compiler_params=limit(4),
-        cost_estimate=cost(1.0),
-        name="merge",
-    )(held, *ring, inward)
-    mine, patch, stacks, far_own, power = lax.optimization_barrier((mine, patch, stacks, far_own, power))
-    theirs = swap(mine)
-
-    far_ring, power = pl.pallas_call(
-        functools.partial(first_kernel, tiles),
-        out_shape=(f32(3, 3, P_SIZE, 2 * P_SIZE), f32(3, P_SIZE, P_SIZE)),
-        in_specs=[SMEM] + [VMEM] * 4,
-        out_specs=(VMEM,) * 2,
-        scratch_shapes=stages(3),
-        compiler_params=limit(16),
-        cost_estimate=cost(4.0),
+        cost_estimate=cost(6.0),
         name="far_of_own_modes",
-    )(spots, mine, patch, stacks, power)
+    )(spots, kernel_taps, object_field, beside, mine)
 
     middle, rim, weight = pl.pallas_call(
         functools.partial(second_kernel, tiles),
         out_shape=(f32(2, OH, TW), f32(2, OH, HALF), f32(P_SIZE, P_SIZE)),
-        in_specs=[SMEM] + [VMEM] * 9,
+        in_specs=[SMEM] + [VMEM] * 8,
         out_specs=(VMEM,) * 3,
         scratch_shapes=[
             pltpu.VMEM((2, OH + 8, EXT), F32),
@@ -352,7 +344,7 @@
         compiler_params=limit(20),
         cost_estimate=cost(10.0),
         name="update_terms",
-    )(spots, intensity, inward, mine, theirs, far_own, far_ring, patch, power, stacks)
+    )(spots, intensity, inward, mine, theirs, far, patch, power, stacks)
 
     arrived = from_tile(rim, -1)
     scale = pl.pallas_call(

time: 71.1 us -> 66.4 us (0.934)
  the two profiles are of different devices: /device:TPU:1 before, /device:TPU:259 now
where the time goes in v6:
time: 66.4 us; the launch traced here: 66 us
  starting transfers between devices  30.1 us (45%)
  waiting for transfers between devices  21.5 us (32%)
  Pallas kernels  11 us (17%)
  local copies, waits for them, and re-layouts  2.15 us (3%)
  other arithmetic  1.1 us (2%)
    ppermute x3, waiting for transfers between devices, along_x(): lax.ppermute(array, 'mode', [(i, (i + 2 * steps) % modes) for i in range(...  11.9 us
    ppermute x3, starting transfers between devices, from_tile(): return lax.ppermute(array, ('tile', 'mode'), pairs)  10.6 us
    ppermute x2, starting transfers between devices, swap(): return lax.ppermute(array, 'mode', [(i, i ^ 1) for i in range(modes)])  10.4 us
    ppermute x3, starting transfers between devices, along_x(): lax.ppermute(array, 'mode', [(i, (i + 2 * steps) % modes) for i in range(...  9.02 us
    ppermute x3, waiting for transfers between devices, from_tile(): return lax.ppermute(array, ('tile', 'mode'), pairs)  6.79 us
    pallas_call x1, Pallas kernels, local(): pl.pallas_call(functools.partial(second_kernel, tiles), out_shape=(f32(2,...  5.84 us
    pallas_call x1, Pallas kernels, local(): pl.pallas_call(functools.partial(first_kernel, tiles), out_shape=(f32(3,...  2.92 us
    ppermute x2, waiting for transfers between devices, swap(): return lax.ppermute(array, 'mode', [(i, i ^ 1) for i in range(modes)])  2.88 us
  transfers between devices with their start and end apart: 8, of which 4 were waited for; matrix products, arithmetic and copies ran while one was open for 0% of the time, Pallas kernels for 8%

profile of v6, /device:TPU:259, one launch (start us, length us, event | category | flops | bytes accessed | tf_op | source)
XLA Modules:
  0.0 66.0 jit_solution(6818707676841259011)
XLA Ops:
  0.0 3.1 %collective-permute-start.1 = (f32[1,2,256,256]{3,2,1,0:T(8,128)}, f32[1,2,256,256]{3,2,1,0:T(8,128)S(1)}, u32[]{:S(2)}, u32[]{:S(2)}) collective-permute-start(f32[1,2,256,256]{3,2,1,0:T(8,128)} %own.1), channel_id=1, source_target_pairs={{0,2},{1,3},{2,4},{3,5},{4,6},{5,7},{6,0},{7,1},{8,10},{9,11},{10,... | collective-permute-start | bytes 1572872 | tf_op jit(solution)/shard_map/ppermute | solution.py:256
  3.1 2.2 %collective-permute-start.2 = (f32[1,2,256,256]{3,2,1,0:T(8,128)}, f32[1,2,256,256]{3,2,1,0:T(8,128)S(1)}, u32[]{:S(2)}, u32[]{:S(2)}) collective-permute-start(f32[1,2,256,256]{3,2,1,0:T(8,128)} %own.1), channel_id=1, source_target_pairs={{0,6},{1,7},{2,0},{3,1},{4,2},{5,3},{6,4},{7,5},{8,14},{9,15},{10,... | collective-permute-start | bytes 1572872 | tf_op jit(solution)/shard_map/ppermute | solution.py:256
  5.3 3.8 %collective-permute-start.3 = (f32[1,2,256,256]{3,2,1,0:T(8,128)}, f32[1,2,256,256]{3,2,1,0:T(8,128)S(1)}, u32[]{:S(2)}, u32[]{:S(2)}) collective-permute-start(f32[1,2,256,256]{3,2,1,0:T(8,128)} %own.1), channel_id=1, source_target_pairs={{0,4},{1,5},{2,6},{3,7},{4,0},{5,1},{6,2},{7,3},{8,12},{9,13},{10,... | collective-permute-start | bytes 1572872 | tf_op jit(solution)/shard_map/ppermute | solution.py:256
  9.0 3.2 %collective-permute-start = (f32[2,256,256]{2,1,0:T(8,128)}, f32[2,256,256]{2,1,0:T(8,128)S(1)}, u32[]{:S(2)}, u32[]{:S(2)}) collective-permute-start(f32[2,256,256]{2,1,0:T(8,128)} %inten.1), channel_id=1, source_target_pairs={{8,0},{10,2},{12,4},{14,6},{16,8},{1,9},{18,10},{3,11},{20,12},{5,... | collective-permute-start | bytes 1572872 | tf_op jit(solution)/shard_map/ppermute | solution.py:268
  12.3 0.0 copy-start
  12.3 1.1 %copy-done = f32[2,320,256]{2,1,0:T(8,128)S(1)} copy-done((f32[2,320,256]{2,1,0:T(8,128)S(1)}, f32[2,320,256]{2,1,0:T(8,128)}, u32[]{:S(2)}) %copy-start) | copy-done | bytes 655384
  13.4 1.0 %copy-done.3 = f32[1,2,256,256]{3,2,1,0:T(8,128)S(1)} copy-done((f32[1,2,256,256]{3,2,1,0:T(8,128)S(1)}, f32[1,2,256,256]{3,2,1,0:T(8,128)}, u32[]{:S(2)}) %copy-start.3) | copy-done | bytes 524312
  14.4 0.1 pack.1
  14.5 3.2 %collective-permute-start.4 = (f32[2,320,128]{2,1,0:T(8,128)S(1)}, f32[2,320,128]{2,1,0:T(8,128)S(1)}, u32[]{:S(2)}, u32[]{:S(2)}) collective-permute-start(f32[2,320,128]{2,1,0:T(8,128)S(1)} %get-tuple-element.17), channel_id=1, source_target_pairs={{8,0},{10,2},{12,4},{14,6},{16,8},{1,9},{18,10},{3,11},{20,12},{5,... | collective-permute-start | bytes 983048 | tf_op jit(solution)/shard_map/ppermute | solution.py:268
  17.7 0.0 collective-permute-done.1.first
  17.7 0.0 collective-permute-done.2.second
  17.7 11.8 %collective-permute-done.3.third = f32[1,2,256,256]{3,2,1,0:T(8,128)S(1)} collective-permute-done((f32[1,2,256,256]{3,2,1,0:T(8,128)}, f32[1,2,256,256]{3,2,1,0:T(8,128)S(1)}, u32[]{:S(2)}, u32[]{:S(2)}) %collective-permute-start.3) | collective-permute-done | bytes 524320 | tf_op jit(solution)/shard_map/ppermute | solution.py:256
  29.6 0.1 merge.1.before
  29.7 0.0 copy-start.1
  29.7 0.0 copy-start.4
  29.7 0.0 copy-start.5
  29.7 0.0 collective-permute-done.inward
  29.8 0.0 copy-start.2
  29.8 0.0 collective-permute-done.4.beside
  29.8 3.9 %collective-permute-start.5 = (f32[9,256,256]{2,1,0:T(8,128)S(1)}, f32[9,256,256]{2,1,0:T(8,128)S(1)}, u32[]{:S(2)}, u32[]{:S(2)}) collective-permute-start(f32[9,256,256]{2,1,0:T(8,128)S(1)} %append.1.mine), channel_id=1, source_target_pairs={{0,1},{1,0},{2,3},{3,2},{4,5},{5,4},{6,7},{7,6},{8,9},{9,8},{10,11... | collective-permute-start | bytes 7077896 | tf_op jit(solution)/shard_map/ppermute | solution.py:259
  33.7 0.0 copy-done.1
  33.8 0.0 copy-done.4
  33.8 2.9 %far_of_own_modes.1 = (f32[3,2,256,256]{3,2,1,0:T(8,128)S(1)}, bf16[2,512,512]{2,1,0:T(8,128)(2,1)S(1)}, f32[3,4,256,512]{3,2,1,0:T(8,128)S(1)}, f32[3,256,256]{2,1,0:T(8,128)S(1)}) custom-call(s32[2,192]{1,0:T(2,128)S(1)} %bitcast.1, f32[2,129]{1,0:T(2,128)S(1)} %copy-done.5, f32[2,320,256]{2,1,0:T(8,128)S(1)} %copy-done.1, ...), custom_call_target="tpu_custom_call" | custom-call | bytes 21000000 | tf_op jit(solution)/shard_map/far_of_own_modes/pallas_call | solution.py:314
  36.7 1.2 %collective-permute-done.5.theirs = f32[9,256,256]{2,1,0:T(8,128)S(1)} collective-permute-done((f32[9,256,256]{2,1,0:T(8,128)S(1)}, f32[9,256,256]{2,1,0:T(8,128)S(1)}, u32[]{:S(2)}, u32[]{:S(2)}) %collective-permute-start.5) | collective-permute-done | bytes 2359328 | tf_op jit(solution)/shard_map/ppermute | solution.py:259
  37.9 5.8 %update_terms.1 = (f32[2,320,256]{2,1,0:T(8,128)S(1)}, f32[2,320,128]{2,1,0:T(8,128)S(1)}, f32[256,256]{1,0:T(8,128)S(1)}) custom-call(s32[2,192]{1,0:T(2,128)S(1)} %bitcast.2, f32[2,256,256]{2,1,0:T(8,128)S(1)} %copy-done.2, f32[2,256,256]{2,1,0:T(8,128)S(1)} %collective-permute-done.inward, f32[9,256,256]{2,1,0:T(8,128)S(1)} %append.1.mine, ...), custom_call_target="tpu_custom_call" | custom-call | bytes 35000000 | tf_op jit(solution)/shard_map/update_terms/pallas_call | solution.py:332
  43.7 4.2 %collective-permute-start.6 = (f32[2,320,128]{2,1,0:T(8,128)S(1)}, f32[2,320,128]{2,1,0:T(8,128)S(1)}, u32[]{:S(2)}, u32[]{:S(2)}) collective-permute-start(f32[2,320,128]{2,1,0:T(8,128)S(1)} %get-tuple-element.25), channel_id=1, source_target_pairs={{9,1},{11,3},{13,5},{15,7},{0,8},{17,9},{2,10},{19,11},{4,12},{21,... | collective-permute-start | bytes 983048 | tf_op jit(solution)/shard_map/ppermute | solution.py:268
  47.9 2.0 %denominator.1 = f32[320,256]{1,0:T(8,128)S(1)} custom-call(s32[2,192]{1,0:T(2,128)S(1)} %bitcast.3, f32[256,256]{1,0:T(8,128)S(1)} %get-tuple-element.26.weight), custom_call_target="tpu_custom_call" | custom-call | bytes 12250000 | tf_op jit(solution)/shard_map/denominator/pallas_call | solution.py:350
  49.9 6.8 %collective-permute-done.6 = f32[2,320,128]{2,1,0:T(8,128)S(1)} collective-permute-done((f32[2,320,128]{2,1,0:T(8,128)S(1)}, f32[2,320,128]{2,1,0:T(8,128)S(1)}, u32[]{:S(2)}, u32[]{:S(2)}) %collective-permute-start.6) | collective-permute-done | bytes 327712 | tf_op jit(solution)/shard_map/ppermute | solution.py:268
  56.7 0.1 fusion
  56.8 6.5 %collective-permute-start.7 = (f32[2,320,256]{2,1,0:T(8,128)S(1)}, f32[2,320,256]{2,1,0:T(8,128)S(1)}, u32[]{:S(2)}, u32[]{:S(2)}) collective-permute-start(f32[2,320,256]{2,1,0:T(8,128)S(1)} %fusion), channel_id=1, source_target_pairs={{0,1},{1,0},{2,3},{3,2},{4,5},{5,4},{6,7},{7,6},{8,9},{9,8},{10,11... | collective-permute-start | bytes 1966088 | tf_op jit(solution)/shard_map/ppermute | solution.py:259
  63.4 1.7 %collective-permute-done.7 = f32[2,320,256]{2,1,0:T(8,128)S(1)} collective-permute-done((f32[2,320,256]{2,1,0:T(8,128)S(1)}, f32[2,320,256]{2,1,0:T(8,128)S(1)}, u32[]{:S(2)}, u32[]{:S(2)}) %collective-permute-start.7) | collective-permute-done | bytes 655392 | tf_op jit(solution)/shard_map/ppermute | solution.py:259
  65.1 1.0 %add_add_fusion = f32[2,320,256]{2,1,0:T(8,128)} fusion(f32[2,320,256]{2,1,0:T(8,128)S(1)} %copy-done.1, f32[2,320,256]{2,1,0:T(8,128)S(1)} %fusion, f32[2,320,256]{2,1,0:T(8,128)S(1)} %collective-permute-done.7), kind=kLoop, calls=%fused_computation.2 | loop fusion | flops 327680 | bytes 2621440 | tf_op jit(solution)/shard_map/add | solution.py:364
  (5 shorter events, 0.1 us)
Async XLA Ops:
  0.0 17.7 %collective-permute-start.1 = (f32[1,2,256,256]{3,2,1,0:T(8,128)}, f32[1,2,256,256]{3,2,1,0:T(8,128)S(1)}, u32[]{:S(2)}, u32[]{:S(2)}) collective-permute-start(f32[1,2,256,256]{3,2,1,0:T(8,128)} %own.1), channel_id=1, source_target_pairs={{0,2},{1,3},{2,4},{3,5},{4,6},{5,7},{6,0},{7,1},{8,10},{9,11},{10,... | collective-permute-start | bytes 1572872 | tf_op jit(solution)/shard_map/ppermute | solution.py:256
  3.1 14.6 %collective-permute-start.2 = (f32[1,2,256,256]{3,2,1,0:T(8,128)}, f32[1,2,256,256]{3,2,1,0:T(8,128)S(1)}, u32[]{:S(2)}, u32[]{:S(2)}) collective-permute-start(f32[1,2,256,256]{3,2,1,0:T(8,128)} %own.1), channel_id=1, source_target_pairs={{0,6},{1,7},{2,0},{3,1},{4,2},{5,3},{6,4},{7,5},{8,14},{9,15},{10,... | collective-permute-start | bytes 1572872 | tf_op jit(solution)/shard_map/ppermute | solution.py:256
  5.3 24.3 %collective-permute-start.3 = (f32[1,2,256,256]{3,2,1,0:T(8,128)}, f32[1,2,256,256]{3,2,1,0:T(8,128)S(1)}, u32[]{:S(2)}, u32[]{:S(2)}) collective-permute-start(f32[1,2,256,256]{3,2,1,0:T(8,128)} %own.1), channel_id=1, source_target_pairs={{0,4},{1,5},{2,6},{3,7},{4,0},{5,1},{6,2},{7,3},{8,12},{9,13},{10,... | collective-permute-start | bytes 1572872 | tf_op jit(solution)/shard_map/ppermute | solution.py:256
  9.0 20.7 %collective-permute-start = (f32[2,256,256]{2,1,0:T(8,128)}, f32[2,256,256]{2,1,0:T(8,128)S(1)}, u32[]{:S(2)}, u32[]{:S(2)}) collective-permute-start(f32[2,256,256]{2,1,0:T(8,128)} %inten.1), channel_id=1, source_target_pairs={{8,0},{10,2},{12,4},{14,6},{16,8},{1,9},{18,10},{3,11},{20,12},{5,... | collective-permute-start | bytes 1572872 | tf_op jit(solution)/shard_map/ppermute | solution.py:268
  12.3 1.1 %copy-start = (f32[2,320,256]{2,1,0:T(8,128)S(1)}, f32[2,320,256]{2,1,0:T(8,128)}, u32[]{:S(2)}) copy-start(f32[2,320,256]{2,1,0:T(8,128)} %obj.3) | copy-start | bytes 1966084
  13.4 1.0 %copy-start.3 = (f32[1,2,256,256]{3,2,1,0:T(8,128)S(1)}, f32[1,2,256,256]{3,2,1,0:T(8,128)}, u32[]{:S(2)}) copy-start(f32[1,2,256,256]{3,2,1,0:T(8,128)} %own.1) | copy-start | bytes 1572868
  14.5 15.3 %collective-permute-start.4 = (f32[2,320,128]{2,1,0:T(8,128)S(1)}, f32[2,320,128]{2,1,0:T(8,128)S(1)}, u32[]{:S(2)}, u32[]{:S(2)}) collective-permute-start(f32[2,320,128]{2,1,0:T(8,128)S(1)} %get-tuple-element.17), channel_id=1, source_target_pairs={{8,0},{10,2},{12,4},{14,6},{16,8},{1,9},{18,10},{3,11},{20,12},{5,... | collective-permute-start | bytes 983048 | tf_op jit(solution)/shard_map/ppermute | solution.py:268
  29.7 4.0 %copy-start.1 = (f32[2,320,256]{2,1,0:T(8,128)S(1)}, f32[2,320,256]{2,1,0:T(8,128)}, u32[]{:S(2)}) copy-start(f32[2,320,256]{2,1,0:T(8,128)} %obj.3) | copy-start | bytes 1966084
  29.7 4.0 %copy-start.4 = (s32[192,2]{0,1:T(2,128)S(1)}, s32[192,2]{0,1:T(2,128)}, u32[]{:S(2)}) copy-start(s32[192,2]{0,1:T(2,128)} %param.6) | copy-start | bytes 4612
  29.7 4.0 %copy-start.5 = (f32[2,129]{1,0:T(2,128)S(1)}, f32[2,129]{1,0:T(2,128)}, u32[]{:S(2)}) copy-start(f32[2,129]{1,0:T(2,128)} %taps_ref.1) | copy-start | bytes 3100
  29.8 8.1 %copy-start.2 = (f32[2,256,256]{2,1,0:T(8,128)S(1)}, f32[2,256,256]{2,1,0:T(8,128)}, u32[]{:S(2)}) copy-start(f32[2,256,256]{2,1,0:T(8,128)} %inten.1) | copy-start | bytes 1572868
  29.8 8.1 %collective-permute-start.5 = (f32[9,256,256]{2,1,0:T(8,128)S(1)}, f32[9,256,256]{2,1,0:T(8,128)S(1)}, u32[]{:S(2)}, u32[]{:S(2)}) collective-permute-start(f32[9,256,256]{2,1,0:T(8,128)S(1)} %append.1.mine), channel_id=1, source_target_pairs={{0,1},{1,0},{2,3},{3,2},{4,5},{5,4},{6,7},{7,6},{8,9},{9,8},{10,11... | collective-permute-start | bytes 7077896 | tf_op jit(solution)/shard_map/ppermute | solution.py:259
  43.7 13.0 %collective-permute-start.6 = (f32[2,320,128]{2,1,0:T(8,128)S(1)}, f32[2,320,128]{2,1,0:T(8,128)S(1)}, u32[]{:S(2)}, u32[]{:S(2)}) collective-permute-start(f32[2,320,128]{2,1,0:T(8,128)S(1)} %get-tuple-element.25), channel_id=1, source_target_pairs={{9,1},{11,3},{13,5},{15,7},{0,8},{17,9},{2,10},{19,11},{4,12},{21,... | collective-permute-start | bytes 983048 | tf_op jit(solution)/shard_map/ppermute | solution.py:268
  56.8 8.3 %collective-permute-start.7 = (f32[2,320,256]{2,1,0:T(8,128)S(1)}, f32[2,320,256]{2,1,0:T(8,128)S(1)}, u32[]{:S(2)}, u32[]{:S(2)}) collective-permute-start(f32[2,320,256]{2,1,0:T(8,128)S(1)} %fusion), channel_id=1, source_target_pairs={{0,1},{1,0},{2,3},{3,2},{4,5},{5,4},{6,7},{7,6},{8,9},{9,8},{10,11... | collective-permute-start | bytes 1966088 | tf_op jit(solution)/shard_map/ppermute | solution.py:259

commit v7 on v6

--- a/solution.py
+++ b/solution.py
@@ -267,7 +267,7 @@
                     pairs.append((source * modes + mode, tile * modes + mode))
         return lax.ppermute(array, ("tile", "mode"), pairs)
 
-    ring = [along_x(probe_modes, step) for step in (1, -1, 2)]
+    ring = [along_x(probe_modes, step) for step in (2, 1, -1)]
     edge, held = pl.pallas_call(
         pack_kernel,
         out_shape=(f32(2, OH, HALF), f32(MODES + 1, P_SIZE, P_SIZE)),

time: 66.4 us -> 63.5 us (0.956)
  the two profiles are of different devices: /device:TPU:259 before, /device:TPU:1 now
where the time goes in v7:
time: 63.5 us; the launch traced here: 63.1 us
  starting transfers between devices  30.9 us (49%)
  waiting for transfers between devices  24.6 us (39%)
  Pallas kernels  4.07 us (6%)
  local copies, waits for them, and re-layouts  2.15 us (3%)
  other arithmetic  1.1 us (2%)
    ppermute x3, waiting for transfers between devices, from_tile(): return lax.ppermute(array, ('tile', 'mode'), pairs)  13.5 us
    ppermute x3, starting transfers between devices, along_x(): lax.ppermute(array, 'mode', [(i, (i + 2 * steps) % modes) for i in range(...  12 us
    ppermute x2, starting transfers between devices, swap(): return lax.ppermute(array, 'mode', [(i, i ^ 1) for i in range(modes)])  11.2 us
    ppermute x3, starting transfers between devices, from_tile(): return lax.ppermute(array, ('tile', 'mode'), pairs)  7.72 us
    ppermute x3, waiting for transfers between devices, along_x(): lax.ppermute(array, 'mode', [(i, (i + 2 * steps) % modes) for i in range(...  6.42 us
    ppermute x2, waiting for transfers between devices, swap(): return lax.ppermute(array, 'mode', [(i, i ^ 1) for i in range(modes)])  4.76 us
    unnamed x12, local copies, waits for them, and re-layouts  2.15 us
    pallas_call x1, Pallas kernels, local(): pl.pallas_call(functools.partial(denom_kernel, tiles), out_shape=f32(OH,...  1.47 us
  transfers between devices with their start and end apart: 8, of which 5 were waited for; matrix products, arithmetic and copies ran while one was open for 0% of the time, Pallas kernels for 4%

profile of v7, /device:TPU:1, one launch (start us, length us, event | category | flops | bytes accessed | tf_op | source)
XLA Modules:
  0.0 63.1 jit_solution(3786457679536236626)
XLA Ops:
  0.0 5.5 %collective-permute-start.1 = (f32[1,2,256,256]{3,2,1,0:T(8,128)}, f32[1,2,256,256]{3,2,1,0:T(8,128)S(1)}, u32[]{:S(2)}, u32[]{:S(2)}) collective-permute-start(f32[1,2,256,256]{3,2,1,0:T(8,128)} %own.1), channel_id=1, source_target_pairs={{0,4},{1,5},{2,6},{3,7},{4,0},{5,1},{6,2},{7,3},{8,12},{9,13},{10,... | collective-permute-start | bytes 1572872 | tf_op jit(solution)/shard_map/ppermute | solution.py:256
  5.5 2.2 %collective-permute-start.2 = (f32[1,2,256,256]{3,2,1,0:T(8,128)}, f32[1,2,256,256]{3,2,1,0:T(8,128)S(1)}, u32[]{:S(2)}, u32[]{:S(2)}) collective-permute-start(f32[1,2,256,256]{3,2,1,0:T(8,128)} %own.1), channel_id=1, source_target_pairs={{0,2},{1,3},{2,4},{3,5},{4,6},{5,7},{6,0},{7,1},{8,10},{9,11},{10,... | collective-permute-start | bytes 1572872 | tf_op jit(solution)/shard_map/ppermute | solution.py:256
  7.7 4.3 %collective-permute-start.3 = (f32[1,2,256,256]{3,2,1,0:T(8,128)}, f32[1,2,256,256]{3,2,1,0:T(8,128)S(1)}, u32[]{:S(2)}, u32[]{:S(2)}) collective-permute-start(f32[1,2,256,256]{3,2,1,0:T(8,128)} %own.1), channel_id=1, source_target_pairs={{0,6},{1,7},{2,0},{3,1},{4,2},{5,3},{6,4},{7,5},{8,14},{9,15},{10,... | collective-permute-start | bytes 1572872 | tf_op jit(solution)/shard_map/ppermute | solution.py:256
  12.0 3.2 %collective-permute-start = (f32[2,256,256]{2,1,0:T(8,128)}, f32[2,256,256]{2,1,0:T(8,128)S(1)}, u32[]{:S(2)}, u32[]{:S(2)}) collective-permute-start(f32[2,256,256]{2,1,0:T(8,128)} %inten.1), channel_id=1, source_target_pairs={{8,0},{10,2},{12,4},{14,6},{16,8},{1,9},{18,10},{3,11},{20,12},{5,... | collective-permute-start | bytes 1572872 | tf_op jit(solution)/shard_map/ppermute | solution.py:268
  15.2 0.0 copy-start
  15.2 1.1 %copy-done = f32[2,320,256]{2,1,0:T(8,128)S(1)} copy-done((f32[2,320,256]{2,1,0:T(8,128)S(1)}, f32[2,320,256]{2,1,0:T(8,128)}, u32[]{:S(2)}) %copy-start) | copy-done | bytes 655384
  16.3 1.0 %copy-done.3 = f32[1,2,256,256]{3,2,1,0:T(8,128)S(1)} copy-done((f32[1,2,256,256]{3,2,1,0:T(8,128)S(1)}, f32[1,2,256,256]{3,2,1,0:T(8,128)}, u32[]{:S(2)}) %copy-start.3) | copy-done | bytes 524312
  17.4 0.1 pack.1
  17.4 3.2 %collective-permute-start.4 = (f32[2,320,128]{2,1,0:T(8,128)S(1)}, f32[2,320,128]{2,1,0:T(8,128)S(1)}, u32[]{:S(2)}, u32[]{:S(2)}) collective-permute-start(f32[2,320,128]{2,1,0:T(8,128)S(1)} %get-tuple-element.17), channel_id=1, source_target_pairs={{8,0},{10,2},{12,4},{14,6},{16,8},{1,9},{18,10},{3,11},{20,12},{5,... | collective-permute-start | bytes 983048 | tf_op jit(solution)/shard_map/ppermute | solution.py:268
  20.6 0.0 collective-permute-done.1.first
  20.7 1.0 %collective-permute-done.2.second = f32[1,2,256,256]{3,2,1,0:T(8,128)S(1)} collective-permute-done((f32[1,2,256,256]{3,2,1,0:T(8,128)}, f32[1,2,256,256]{3,2,1,0:T(8,128)S(1)}, u32[]{:S(2)}, u32[]{:S(2)}) %collective-permute-start.2) | collective-permute-done | bytes 524320 | tf_op jit(solution)/shard_map/ppermute | solution.py:256
  21.6 5.4 %collective-permute-done.3.third = f32[1,2,256,256]{3,2,1,0:T(8,128)S(1)} collective-permute-done((f32[1,2,256,256]{3,2,1,0:T(8,128)}, f32[1,2,256,256]{3,2,1,0:T(8,128)S(1)}, u32[]{:S(2)}, u32[]{:S(2)}) %collective-permute-start.3) | collective-permute-done | bytes 524320 | tf_op jit(solution)/shard_map/ppermute | solution.py:256
  27.1 0.1 merge.1.before
  27.2 0.0 copy-start.1
  27.2 0.0 copy-start.4
  27.2 0.0 copy-start.5
  27.3 0.0 collective-permute-done.inward
  27.3 0.0 copy-start.2
  27.3 0.0 collective-permute-done.4.beside
  27.3 8.9 %collective-permute-start.5 = (f32[9,256,256]{2,1,0:T(8,128)S(1)}, f32[9,256,256]{2,1,0:T(8,128)S(1)}, u32[]{:S(2)}, u32[]{:S(2)}) collective-permute-start(f32[9,256,256]{2,1,0:T(8,128)S(1)} %append.1.mine), channel_id=1, source_target_pairs={{0,1},{1,0},{2,3},{3,2},{4,5},{5,4},{6,7},{7,6},{8,9},{9,8},{10,11... | collective-permute-start | bytes 7077896 | tf_op jit(solution)/shard_map/ppermute | solution.py:259
  36.2 0.0 copy-done.1
  36.2 0.0 copy-done.4
  36.2 1.0 %far_of_own_modes.1 = (f32[3,2,256,256]{3,2,1,0:T(8,128)S(1)}, bf16[2,512,512]{2,1,0:T(8,128)(2,1)S(1)}, f32[3,4,256,512]{3,2,1,0:T(8,128)S(1)}, f32[3,256,256]{2,1,0:T(8,128)S(1)}) custom-call(s32[2,192]{1,0:T(2,128)S(1)} %bitcast.1, f32[2,129]{1,0:T(2,128)S(1)} %copy-done.5, f32[2,320,256]{2,1,0:T(8,128)S(1)} %copy-done.1, ...), custom_call_target="tpu_custom_call" | custom-call | bytes 21000000 | tf_op jit(solution)/shard_map/far_of_own_modes/pallas_call | solution.py:314
  37.3 3.1 %collective-permute-done.5.theirs = f32[9,256,256]{2,1,0:T(8,128)S(1)} collective-permute-done((f32[9,256,256]{2,1,0:T(8,128)S(1)}, f32[9,256,256]{2,1,0:T(8,128)S(1)}, u32[]{:S(2)}, u32[]{:S(2)}) %collective-permute-start.5) | collective-permute-done | bytes 2359328 | tf_op jit(solution)/shard_map/ppermute | solution.py:259
  40.3 1.3 %update_terms.1 = (f32[2,320,256]{2,1,0:T(8,128)S(1)}, f32[2,320,128]{2,1,0:T(8,128)S(1)}, f32[256,256]{1,0:T(8,128)S(1)}) custom-call(s32[2,192]{1,0:T(2,128)S(1)} %bitcast.2, f32[2,256,256]{2,1,0:T(8,128)S(1)} %copy-done.2, f32[2,256,256]{2,1,0:T(8,128)S(1)} %collective-permute-done.inward, f32[9,256,256]{2,1,0:T(8,128)S(1)} %append.1.mine, ...), custom_call_target="tpu_custom_call" | custom-call | bytes 35000000 | tf_op jit(solution)/shard_map/update_terms/pallas_call | solution.py:332
  41.7 1.3 %collective-permute-start.6 = (f32[2,320,128]{2,1,0:T(8,128)S(1)}, f32[2,320,128]{2,1,0:T(8,128)S(1)}, u32[]{:S(2)}, u32[]{:S(2)}) collective-permute-start(f32[2,320,128]{2,1,0:T(8,128)S(1)} %get-tuple-element.25), channel_id=1, source_target_pairs={{9,1},{11,3},{13,5},{15,7},{0,8},{17,9},{2,10},{19,11},{4,12},{21,... | collective-permute-start | bytes 983048 | tf_op jit(solution)/shard_map/ppermute | solution.py:268
  43.0 1.5 %denominator.1 = f32[320,256]{1,0:T(8,128)S(1)} custom-call(s32[2,192]{1,0:T(2,128)S(1)} %bitcast.3, f32[256,256]{1,0:T(8,128)S(1)} %get-tuple-element.26.weight), custom_call_target="tpu_custom_call" | custom-call | bytes 12250000 | tf_op jit(solution)/shard_map/denominator/pallas_call | solution.py:350
  44.4 13.4 %collective-permute-done.6 = f32[2,320,128]{2,1,0:T(8,128)S(1)} collective-permute-done((f32[2,320,128]{2,1,0:T(8,128)S(1)}, f32[2,320,128]{2,1,0:T(8,128)S(1)}, u32[]{:S(2)}, u32[]{:S(2)}) %collective-permute-start.6) | collective-permute-done | bytes 327712 | tf_op jit(solution)/shard_map/ppermute | solution.py:268
  57.9 0.1 fusion
  58.0 2.4 %collective-permute-start.7 = (f32[2,320,256]{2,1,0:T(8,128)S(1)}, f32[2,320,256]{2,1,0:T(8,128)S(1)}, u32[]{:S(2)}, u32[]{:S(2)}) collective-permute-start(f32[2,320,256]{2,1,0:T(8,128)S(1)} %fusion), channel_id=1, source_target_pairs={{0,1},{1,0},{2,3},{3,2},{4,5},{5,4},{6,7},{7,6},{8,9},{9,8},{10,11... | collective-permute-start | bytes 1966088 | tf_op jit(solution)/shard_map/ppermute | solution.py:259
  60.4 1.7 %collective-permute-done.7 = f32[2,320,256]{2,1,0:T(8,128)S(1)} collective-permute-done((f32[2,320,256]{2,1,0:T(8,128)S(1)}, f32[2,320,256]{2,1,0:T(8,128)S(1)}, u32[]{:S(2)}, u32[]{:S(2)}) %collective-permute-start.7) | collective-permute-done | bytes 655392 | tf_op jit(solution)/shard_map/ppermute | solution.py:259
  62.1 1.0 %add_add_fusion = f32[2,320,256]{2,1,0:T(8,128)} fusion(f32[2,320,256]{2,1,0:T(8,128)S(1)} %copy-done.1, f32[2,320,256]{2,1,0:T(8,128)S(1)} %fusion, f32[2,320,256]{2,1,0:T(8,128)S(1)} %collective-permute-done.7), kind=kLoop, calls=%fused_computation.2 | loop fusion | flops 327680 | bytes 2621440 | tf_op jit(solution)/shard_map/add | solution.py:364
  (5 shorter events, 0.1 us)
Async XLA Ops:
  0.0 20.6 %collective-permute-start.1 = (f32[1,2,256,256]{3,2,1,0:T(8,128)}, f32[1,2,256,256]{3,2,1,0:T(8,128)S(1)}, u32[]{:S(2)}, u32[]{:S(2)}) collective-permute-start(f32[1,2,256,256]{3,2,1,0:T(8,128)} %own.1), channel_id=1, source_target_pairs={{0,4},{1,5},{2,6},{3,7},{4,0},{5,1},{6,2},{7,3},{8,12},{9,13},{10,... | collective-permute-start | bytes 1572872 | tf_op jit(solution)/shard_map/ppermute | solution.py:256
  5.5 16.2 %collective-permute-start.2 = (f32[1,2,256,256]{3,2,1,0:T(8,128)}, f32[1,2,256,256]{3,2,1,0:T(8,128)S(1)}, u32[]{:S(2)}, u32[]{:S(2)}) collective-permute-start(f32[1,2,256,256]{3,2,1,0:T(8,128)} %own.1), channel_id=1, source_target_pairs={{0,2},{1,3},{2,4},{3,5},{4,6},{5,7},{6,0},{7,1},{8,10},{9,11},{10,... | collective-permute-start | bytes 1572872 | tf_op jit(solution)/shard_map/ppermute | solution.py:256
  7.7 19.4 %collective-permute-start.3 = (f32[1,2,256,256]{3,2,1,0:T(8,128)}, f32[1,2,256,256]{3,2,1,0:T(8,128)S(1)}, u32[]{:S(2)}, u32[]{:S(2)}) collective-permute-start(f32[1,2,256,256]{3,2,1,0:T(8,128)} %own.1), channel_id=1, source_target_pairs={{0,6},{1,7},{2,0},{3,1},{4,2},{5,3},{6,4},{7,5},{8,14},{9,15},{10,... | collective-permute-start | bytes 1572872 | tf_op jit(solution)/shard_map/ppermute | solution.py:256
  12.0 15.3 %collective-permute-start = (f32[2,256,256]{2,1,0:T(8,128)}, f32[2,256,256]{2,1,0:T(8,128)S(1)}, u32[]{:S(2)}, u32[]{:S(2)}) collective-permute-start(f32[2,256,256]{2,1,0:T(8,128)} %inten.1), channel_id=1, source_target_pairs={{8,0},{10,2},{12,4},{14,6},{16,8},{1,9},{18,10},{3,11},{20,12},{5,... | collective-permute-start | bytes 1572872 | tf_op jit(solution)/shard_map/ppermute | solution.py:268
  15.2 1.1 %copy-start = (f32[2,320,256]{2,1,0:T(8,128)S(1)}, f32[2,320,256]{2,1,0:T(8,128)}, u32[]{:S(2)}) copy-start(f32[2,320,256]{2,1,0:T(8,128)} %obj.3) | copy-start | bytes 1966084
  16.3 1.0 %copy-start.3 = (f32[1,2,256,256]{3,2,1,0:T(8,128)S(1)}, f32[1,2,256,256]{3,2,1,0:T(8,128)}, u32[]{:S(2)}) copy-start(f32[1,2,256,256]{3,2,1,0:T(8,128)} %own.1) | copy-start | bytes 1572868
  17.4 9.9 %collective-permute-start.4 = (f32[2,320,128]{2,1,0:T(8,128)S(1)}, f32[2,320,128]{2,1,0:T(8,128)S(1)}, u32[]{:S(2)}, u32[]{:S(2)}) collective-permute-start(f32[2,320,128]{2,1,0:T(8,128)S(1)} %get-tuple-element.17), channel_id=1, source_target_pairs={{8,0},{10,2},{12,4},{14,6},{16,8},{1,9},{18,10},{3,11},{20,12},{5,... | collective-permute-start | bytes 983048 | tf_op jit(solution)/shard_map/ppermute | solution.py:268
  27.2 9.0 %copy-start.1 = (f32[2,320,256]{2,1,0:T(8,128)S(1)}, f32[2,320,256]{2,1,0:T(8,128)}, u32[]{:S(2)}) copy-start(f32[2,320,256]{2,1,0:T(8,128)} %obj.3) | copy-start | bytes 1966084
  27.2 9.0 %copy-start.4 = (s32[192,2]{0,1:T(2,128)S(1)}, s32[192,2]{0,1:T(2,128)}, u32[]{:S(2)}) copy-start(s32[192,2]{0,1:T(2,128)} %param.6) | copy-start | bytes 4612
  27.2 9.0 %copy-start.5 = (f32[2,129]{1,0:T(2,128)S(1)}, f32[2,129]{1,0:T(2,128)}, u32[]{:S(2)}) copy-start(f32[2,129]{1,0:T(2,128)} %taps_ref.1) | copy-start | bytes 3100
  27.3 13.0 %copy-start.2 = (f32[2,256,256]{2,1,0:T(8,128)S(1)}, f32[2,256,256]{2,1,0:T(8,128)}, u32[]{:S(2)}) copy-start(f32[2,256,256]{2,1,0:T(8,128)} %inten.1) | copy-start | bytes 1572868
  27.3 13.0 %collective-permute-start.5 = (f32[9,256,256]{2,1,0:T(8,128)S(1)}, f32[9,256,256]{2,1,0:T(8,128)S(1)}, u32[]{:S(2)}, u32[]{:S(2)}) collective-permute-start(f32[9,256,256]{2,1,0:T(8,128)S(1)} %append.1.mine), channel_id=1, source_target_pairs={{0,1},{1,0},{2,3},{3,2},{4,5},{5,4},{6,7},{7,6},{8,9},{9,8},{10,11... | collective-permute-start | bytes 7077896 | tf_op jit(solution)/shard_map/ppermute | solution.py:259
  41.7 16.2 %collective-permute-start.6 = (f32[2,320,128]{2,1,0:T(8,128)S(1)}, f32[2,320,128]{2,1,0:T(8,128)S(1)}, u32[]{:S(2)}, u32[]{:S(2)}) collective-permute-start(f32[2,320,128]{2,1,0:T(8,128)S(1)} %get-tuple-element.25), channel_id=1, source_target_pairs={{9,1},{11,3},{13,5},{15,7},{0,8},{17,9},{2,10},{19,11},{4,12},{21,... | collective-permute-start | bytes 983048 | tf_op jit(solution)/shard_map/ppermute | solution.py:268
  58.0 4.1 %collective-permute-start.7 = (f32[2,320,256]{2,1,0:T(8,128)S(1)}, f32[2,320,256]{2,1,0:T(8,128)S(1)}, u32[]{:S(2)}, u32[]{:S(2)}) collective-permute-start(f32[2,320,256]{2,1,0:T(8,128)S(1)} %fusion), channel_id=1, source_target_pairs={{0,1},{1,0},{2,3},{3,2},{4,5},{5,4},{6,7},{7,6},{8,9},{9,8},{10,11... | collective-permute-start | bytes 1966088 | tf_op jit(solution)/shard_map/ppermute | solution.py:259
